TPU v7x, 512 devices: a whole 4x8x8 slice. The times are simulated.
512 devices in a mesh: rows: 16 (over x, y_lo, core), pairs: 32 (over y_hi, z).
Axes of the slice: x: 4, y: 8 (y_hi: 4, y_lo: 2; y = y_hi * 2 + y_lo), z: 8, core: 2. Of those that a mesh axis runs over, the one named last changes fastest.
Arguments:
- snapshots: float32 [32768, 8192], P('rows', 'pairs'), may hold values from -1600 to 1600, as said below
Outputs:
- rotated: float32 [32768, 8192], P('rows', 'pairs')
Inputs may be any that keep to these rules, and one draw needn't show every extreme that they name: `snapshots`: finite real values.
All inputs are finite; a program needn't handle non-finite values.
Results may differ from a plain program's by a relative error of at most 0.00011.
Values sent between devices are 32-bit elements; how exact they have to be, the bound alone decides.
A program may use at most 64 MiB of HBM per device.

v0:
```python
import functools

import jax
import jax.numpy as jnp
from jax import lax
from jax.experimental import pallas as pl
from jax.experimental.pallas import tpu as pltpu
from jax.sharding import PartitionSpec as P

MESH = pl.DeviceIdType.MESH


def from_behind(value, axis, steps):
    count = lax.axis_size(axis)
    leading, last = (max(0, -steps), min(count, count - steps))
    return lax.ppermute(value, axis, [(source, source + steps) for source in range(leading, last)])


def gram_of(left, right):
    return lax.dot_general(left, right, (((0,), (0,)), ((), ())), precision=lax.Precision.HIGHEST)


def allreduce_kernel(n, chunk, g_ref, o_ref, recv, send_sem, recv_sem, send2_sem, recv2_sem):
    me = lax.axis_index("rows")
    col = lax.axis_index("pairs")

    barrier = pltpu.get_barrier_semaphore()
    for d in range(1, n):
        peer = lax.rem(me + d, n)
        pl.semaphore_signal(barrier, inc=1, device_id=(peer, col), device_id_type=MESH)
    pl.semaphore_wait(barrier, n - 1)

    scatter = []
    for d in range(1, n):
        peer = lax.rem(me + d, n)
        start = pl.multiple_of(peer * chunk, chunk)
        copy = pltpu.make_async_remote_copy(
            src_ref=g_ref.at[pl.ds(start, chunk), :],
            dst_ref=recv.at[d],
            send_sem=send_sem.at[d],
            recv_sem=recv_sem.at[d],
            device_id=(peer, col),
            device_id_type=MESH,
        )
        copy.start()
        scatter.append(copy)

    mine = pl.multiple_of(me * chunk, chunk)
    total = g_ref[pl.ds(mine, chunk), :]
    for d in range(1, n):
        scatter[d - 1].wait_recv()
        total = total + recv[d]
    o_ref[pl.ds(mine, chunk), :] = total
    for copy in scatter:
        copy.wait_send()

    gather = []
    for d in range(1, n):
        peer = lax.rem(me + d, n)
        copy = pltpu.make_async_remote_copy(
            src_ref=o_ref.at[pl.ds(mine, chunk), :],
            dst_ref=o_ref.at[pl.ds(mine, chunk), :],
            send_sem=send2_sem.at[d],
            recv_sem=recv2_sem.at[d],
            device_id=(peer, col),
            device_id_type=MESH,
        )
        copy.start()
        gather.append(copy)
    for d in range(1, n):
        source = lax.rem(me + n - d, n)
        start = pl.multiple_of(source * chunk, chunk)
        pltpu.make_async_remote_copy(
            src_ref=o_ref.at[pl.ds(start, chunk), :],
            dst_ref=o_ref.at[pl.ds(start, chunk), :],
            send_sem=send2_sem.at[d],
            recv_sem=recv2_sem.at[d],
            device_id=(source, col),
            device_id_type=MESH,
        ).wait_recv()
    for copy in gather:
        copy.wait_send()


def allreduce_rows(g):
    n = lax.axis_size("rows")
    rows, cols = g.shape
    chunk = rows // n
    return pl.pallas_call(
        functools.partial(allreduce_kernel, n, chunk),
        out_shape=jax.ShapeDtypeStruct((rows, cols), g.dtype),
        in_specs=[pl.BlockSpec(memory_space=pltpu.VMEM)],
        out_specs=pl.BlockSpec(memory_space=pltpu.VMEM),
        scratch_shapes=[
            pltpu.VMEM((n, chunk, cols), g.dtype),
            pltpu.SemaphoreType.DMA((n,)),
            pltpu.SemaphoreType.DMA((n,)),
            pltpu.SemaphoreType.DMA((n,)),
            pltpu.SemaphoreType.DMA((n,)),
        ],
        compiler_params=pltpu.CompilerParams(collective_id=0, has_side_effects=True),
    )(g)


def whitener(scaled):
    identity = jnp.eye(scaled.shape[0], dtype=scaled.dtype)
    level = jnp.trace(scaled) / scaled.shape[0]
    lower = jnp.linalg.cholesky(scaled + 0.1 * level * identity)
    inverse = lax.linalg.triangular_solve(lower, identity, left_side=True, lower=True)
    return inverse.T


def mm(left, right):
    return jnp.dot(left, right, precision=lax.Precision.HIGHEST)


def tmm(left, right):
    return gram_of(left, right)


def per_device(snapshots):
    local_rows = snapshots.shape[0]
    total = local_rows * lax.axis_size("rows")
    width = snapshots.shape[1] // 2
    count = lax.axis_size("pairs")
    index = lax.axis_index("pairs")
    first = index == 0
    last = index == count - 1
    pair = snapshots

    gram = allreduce_rows(gram_of(pair, pair)) / total
    sent, gram = lax.optimization_barrier((pair, gram))
    raw_a = jnp.where(first, pair, from_behind(sent, "pairs", 1))
    raw_b = jnp.where(last, pair, from_behind(sent, "pairs", -1))

    cross = allreduce_rows(gram_of(raw_a, raw_b)) / total

    whiten = whitener(gram)
    moment = tmm(whiten, mm(gram, whiten))
    top = jnp.concatenate([whiten[:, :width], moment[:width, :width]], axis=0)
    bottom = jnp.concatenate([whiten[:, width:], moment[width:, width:]], axis=0)
    outgoing = jnp.where(first, bottom, top)
    arrived_a = from_behind(outgoing, "pairs", 1)
    arrived_b = from_behind(bottom, "pairs", -1)
    side_a = jnp.where(first, top, arrived_a)
    side_b = jnp.where(last, top, arrived_b)
    rows = whiten.shape[0]
    x_a, m_a = side_a[:rows], side_a[rows:]
    x_b, m_b = side_b[:rows], side_b[rows:]

    off = tmm(x_a, mm(cross, x_b))
    gram2 = jnp.concatenate(
        [jnp.concatenate([m_a, off], axis=1), jnp.concatenate([off.T, m_b], axis=1)], axis=0
    )
    whiten2 = whitener(gram2)
    combined = jnp.concatenate([mm(x_a, whiten2[:width]), mm(x_b, whiten2[width:])], axis=0)
    return mm(jnp.concatenate([raw_a, raw_b], axis=1), combined)


def solution(mesh):
    return jax.shard_map(
        per_device,
        mesh=mesh,
        in_specs=(P("rows", "pairs"),),
        out_specs=P("rows", "pairs"),
        check_vma=False,
    )
```

profile of v0, /device:TPU:57, one launch (start us, length us, event | category | flops | bytes accessed | tf_op | source)
XLA Modules:
  0.0 235.3 jit_solution(15123474582026980712)
XLA Ops:
  0.0 6.5 %fusion.50.g_ref = f32[256,256]{1,0:T(8,128)} fusion(f32[2048,256]{1,0:T(8,128)} %param.4), kind=kOutput, calls=%fused_computation.97 | convolution fusion | flops 1610612736 | bytes 2359296 | tf_op jit(solution)/shard_map/dot_general | solution.py:20
  6.5 17.8 %shard_map.17 = f32[256,256]{1,0:T(8,128)} custom-call(f32[256,256]{1,0:T(8,128)} %fusion.50.g_ref), custom_call_target="tpu_custom_call" | custom-call | tf_op jit(solution)/shard_map/pallas_call | solution.py:89
  25.5 4.0 %collective-permute-start = (f32[2048,256]{1,0:T(8,128)S(1)}, f32[2048,256]{1,0:T(8,128)}, u32[]{:S(2)}, u32[]{:S(2)}) collective-permute-start(f32[2048,256]{1,0:T(8,128)S(1)} %copy-done), channel_id=1, source_target_pairs={{0,1},{1,2},{2,3},{3,4},{4,5},{5,6},{6,7},{7,8},{8,9},{9,10},{10,1... | collective-permute-start | bytes 6291464 | tf_op jit(solution)/shard_map/ppermute | solution.py:16
  29.5 10.5 %collective-permute-start.1 = (f32[2048,256]{1,0:T(8,128)S(1)}, f32[2048,256]{1,0:T(8,128)}, u32[]{:S(2)}, u32[]{:S(2)}) collective-permute-start(f32[2048,256]{1,0:T(8,128)S(1)} %copy-done), channel_id=1, source_target_pairs={{1,0},{2,1},{3,2},{4,3},{5,4},{6,5},{7,6},{8,7},{9,8},{10,9},{11,1... | collective-permute-start | bytes 6291464 | tf_op jit(solution)/shard_map/ppermute | solution.py:16
  41.6 11.7 %cholesky.130 = f32[128,128]{1,0:T(8,128)S(1)} custom-call(f32[128,128]{1,0:T(8,128)S(1)} %cholesky.194), custom_call_target="Cholesky" | custom-call | tf_op jit(solution)/shard_map/jit(cholesky)/cholesky | solution.py:108
  53.4 9.8 %custom-call.13 = f32[1,128,128]{1,2,0:T(8,128)S(1)} custom-call(f32[1,128,128]{2,1,0:T(8,128)S(1)} %get-tuple-element.64), custom_call_target="InvertDiagBlocksLowerTriangular" | custom-call | tf_op jit(solution)/shard_map/jit(cholesky)/cholesky | solution.py:108
  63.7 11.7 %cholesky.147 = f32[128,128]{1,0:T(8,128)S(1)} custom-call(f32[128,128]{1,0:T(8,128)S(1)} %convolution_subtract_fusion.3), custom_call_target="Cholesky" | custom-call | tf_op jit(solution)/shard_map/jit(cholesky)/cholesky | solution.py:108
  77.6 15.6 %while.4 = (s32[]{:T(128)}, f32[256,256]{1,0:T(8,128)S(1)}, s32[2,2]{1,0:T(2,128)S(1)}, f32[2,128,128]{2,1,0:T(8,128)S(1)}, s32[]{:T(128)}) while((s32[]{:T(128)}, f32[256,256]{1,0:T(8,128)S(1)}, s32[2,2]{1,0:T(2,128)S(1)}, f32[2,128,128]{2,1,0:T(8,128)S(1)}, s32[]{:T(128)}) %tuple.50), condition=%wide.while_cond, body=%wide.while_body.sunk | while | flops 2 | bytes 131189 | solution.py:109
  89.7 1.4 bitcast_dynamic-update-slice_fusion.4
  91.8 1.4 bitcast_dynamic-update-slice_fusion.4
  93.2 19.7 %custom-call.14 = f32[2,128,128]{1,2,0:T(8,128)S(1)} custom-call(f32[2,128,128]{2,1,0:T(8,128)S(1)} %get-tuple-element.25), custom_call_target="InvertDiagBlocksLowerTriangular" | custom-call | tf_op jit(solution)/shard_map/triangular_solve/custom-call.0 | solution.py:109
  115.9 1.9 collective-permute-start.2
  117.8 6.4 %collective-permute-start.3 = (f32[384,128]{0,1:T(8,128)S(1)}, f32[384,128]{0,1:T(8,128)S(1)}, u32[]{:S(2)}, u32[]{:S(2)}) collective-permute-start(f32[384,128]{0,1:T(8,128)S(1)} %get-tuple-element.56), channel_id=1, source_target_pairs={{1,0},{2,1},{3,2},{4,3},{5,4},{6,5},{7,6},{8,7},{9,8},{10,9},{11,1... | collective-permute-start | bytes 589832 | tf_op jit(solution)/shard_map/ppermute | solution.py:16
  124.2 11.8 %collective-permute-done.2 = f32[384,128]{0,1:T(8,128)S(1)} collective-permute-done((f32[384,128]{0,1:T(8,128)}, f32[384,128]{0,1:T(8,128)S(1)}, u32[]{:S(2)}, u32[]{:S(2)}) %collective-permute-start.2) | collective-permute-done | bytes 196640 | tf_op jit(solution)/shard_map/ppermute | solution.py:16
  136.0 2.6 %broadcast_select_fusion.1 = (f32[2048,256]{1,0:T(8,128)S(1)}, f32[2048,256]{1,0:T(8,128)S(1)}) fusion(f32[2048,256]{1,0:T(8,128)S(1)} %copy-done, f32[2048,256]{1,0:T(8,128)} %collective-permute-done, pred[]{:T(512)S(6)} %eq.23, f32[2048,256]{1,0:T(8,128)} %collective-permute-done.1, pred[]{:T(512)S(6)} %eq.24), kind=kLoop, calls=%fused_computation.13 | loop fusion | flops 1048576 | bytes 10485762 | tf_op jit(solution)/shard_map/jit(_where)/select_n | solution.py:133
  140.7 4.3 %fusion.51.g_ref = f32[256,256]{1,0:T(8,128)} fusion(f32[2048,256]{1,0:T(8,128)S(1)} %get-tuple-element.47, f32[2048,256]{1,0:T(8,128)S(1)} %get-tuple-element.48), kind=kOutput, calls=%fused_computation.98 | convolution fusion | flops 1610612736 | bytes 4456448 | tf_op jit(solution)/shard_map/dot_general | solution.py:20
  145.0 18.1 %shard_map.18 = f32[256,256]{1,0:T(8,128)} custom-call(f32[256,256]{1,0:T(8,128)} %fusion.51.g_ref), custom_call_target="tpu_custom_call" | custom-call | tf_op jit(solution)/shard_map/pallas_call | solution.py:89
  166.7 11.7 %cholesky.164 = f32[128,128]{1,0:T(8,128)S(1)} custom-call(f32[128,128]{1,0:T(8,128)S(1)} %cholesky.197), custom_call_target="Cholesky" | custom-call | tf_op jit(solution)/shard_map/jit(cholesky)/cholesky | solution.py:108
  178.5 9.8 %custom-call.15 = f32[1,128,128]{1,2,0:T(8,128)S(1)} custom-call(f32[1,128,128]{2,1,0:T(8,128)S(1)} %get-tuple-element.60), custom_call_target="InvertDiagBlocksLowerTriangular" | custom-call | tf_op jit(solution)/shard_map/jit(cholesky)/cholesky | solution.py:108
  188.8 11.8 %cholesky.181 = f32[128,128]{1,0:T(8,128)S(1)} custom-call(f32[128,128]{1,0:T(8,128)S(1)} %convolution_subtract_fusion.2), custom_call_target="Cholesky" | custom-call | tf_op jit(solution)/shard_map/jit(cholesky)/cholesky | solution.py:108
  203.2 3.9 %while.5 = (s32[]{:T(128)}, f32[256,256]{1,0:T(8,128)S(1)}, s32[2,2]{1,0:T(2,128)S(1)}, f32[2,128,128]{2,1,0:T(8,128)S(1)}, s32[]{:T(128)}) while((s32[]{:T(128)}, f32[256,256]{1,0:T(8,128)S(1)}, s32[2,2]{1,0:T(2,128)S(1)}, f32[2,128,128]{2,1,0:T(8,128)S(1)}, s32[]{:T(128)}) %tuple.56), condition=%wide.while_cond.clone, body=%wide.while_body.clone.sunk | while | flops 2 | bytes 131189 | solution.py:109
  203.8 1.3 bitcast_dynamic-update-slice_fusion.5
  207.1 19.7 %custom-call.16 = f32[2,128,128]{1,2,0:T(8,128)S(1)} custom-call(f32[2,128,128]{2,1,0:T(8,128)S(1)} %get-tuple-element.26), custom_call_target="InvertDiagBlocksLowerTriangular" | custom-call | tf_op jit(solution)/shard_map/triangular_solve/custom-call.0 | solution.py:109
  228.7 6.4 %fusion = f32[2048,256]{1,0:T(8,128)} fusion(f32[2048,256]{1,0:T(8,128)} %copy-done.3, f32[2048,256]{1,0:T(8,128)S(1)} %copy-done.2, f32[256,256]{1,0:T(8,128)S(1)} %fusion.15, f32[256,256]{1,0:T(8,128)S(1)} %fusion.17), kind=kOutput, calls=%fused_computation.4 | convolution fusion | flops 3222405120 | bytes 6815744 | tf_op jit(solution)/shard_map/dot_general | solution.py:114
  (74 shorter events, 18.8 us)
Async XLA Ops:
  0.0 25.5 %copy-start = (f32[2048,256]{1,0:T(8,128)S(1)}, f32[2048,256]{1,0:T(8,128)}, u32[]{:S(2)}) copy-start(f32[2048,256]{1,0:T(8,128)} %param.4) | copy-start | bytes 6291460
  25.5 110.5 %collective-permute-start = (f32[2048,256]{1,0:T(8,128)S(1)}, f32[2048,256]{1,0:T(8,128)}, u32[]{:S(2)}, u32[]{:S(2)}) collective-permute-start(f32[2048,256]{1,0:T(8,128)S(1)} %copy-done), channel_id=1, source_target_pairs={{0,1},{1,2},{2,3},{3,4},{4,5},{5,6},{6,7},{7,8},{8,9},{9,10},{10,1... | collective-permute-start | bytes 6291464 | tf_op jit(solution)/shard_map/ppermute | solution.py:16
  29.5 106.5 %collective-permute-start.1 = (f32[2048,256]{1,0:T(8,128)S(1)}, f32[2048,256]{1,0:T(8,128)}, u32[]{:S(2)}, u32[]{:S(2)}) collective-permute-start(f32[2048,256]{1,0:T(8,128)S(1)} %copy-done), channel_id=1, source_target_pairs={{1,0},{2,1},{3,2},{4,3},{5,4},{6,5},{7,6},{8,7},{9,8},{10,9},{11,1... | collective-permute-start | bytes 6291464 | tf_op jit(solution)/shard_map/ppermute | solution.py:16
  115.9 20.1 %collective-permute-start.2 = (f32[384,128]{0,1:T(8,128)}, f32[384,128]{0,1:T(8,128)S(1)}, u32[]{:S(2)}, u32[]{:S(2)}) collective-permute-start(f32[384,128]{0,1:T(8,128)} %get-tuple-element.55), channel_id=1, source_target_pairs={{0,1},{1,2},{2,3},{3,4},{4,5},{5,6},{6,7},{7,8},{8,9},{9,10},{10,1... | collective-permute-start | bytes 589832 | tf_op jit(solution)/shard_map/ppermute | solution.py:16
  117.8 18.1 %collective-permute-start.3 = (f32[384,128]{0,1:T(8,128)S(1)}, f32[384,128]{0,1:T(8,128)S(1)}, u32[]{:S(2)}, u32[]{:S(2)}) collective-permute-start(f32[384,128]{0,1:T(8,128)S(1)} %get-tuple-element.56), channel_id=1, source_target_pairs={{1,0},{2,1},{3,2},{4,3},{5,4},{6,5},{7,6},{8,7},{9,8},{10,9},{11,1... | collective-permute-start | bytes 589832 | tf_op jit(solution)/shard_map/ppermute | solution.py:16
  138.7 1.3 copy-start.1
  138.7 2.0 copy-start.3
  201.3 27.4 %copy-start.2 = (f32[2048,256]{1,0:T(8,128)S(1)}, f32[2048,256]{1,0:T(8,128)}, u32[]{:S(2)}) copy-start(f32[2048,256]{1,0:T(8,128)} %copy-done.1) | copy-start | bytes 6291460
where the time goes:
time: 239 us; the launch traced here: 235 us
  other arithmetic  113 us (47%)
  Pallas kernels  35.9 us (15%)
  matrix products  23.1 us (10%)
  starting transfers between devices  22.8 us (10%)
  local copies, waits for them, and re-layouts  12.6 us (5%)
  waiting for transfers between devices  11.8 us (5%)
  loops' own time  11.6 us (5%)
  between operations  4.47 us (2%)
    another operation x13, other arithmetic, whitener(): lower = jnp.linalg.cholesky(scaled + 0.1 * level * identity)  68.7 us
    another operation x5, other arithmetic, whitener(): lax.linalg.triangular_solve(lower, identity, left_side=True, lower=True)  39.4 us
    pallas_call x2, Pallas kernels, allreduce_rows(): pl.pallas_call(functools.partial(allreduce_kernel, n, chunk), out_shape=j...  35.9 us
    ppermute x4, starting transfers between devices, from_behind(): lax.ppermute(value, axis, [(source, source + steps) for source in range(l...  22.8 us
    ppermute x4, waiting for transfers between devices, from_behind(): lax.ppermute(value, axis, [(source, source + steps) for source in range(l...  11.8 us
    dot_general x4, matrix products, gram_of(): lax.dot_general(left, right, (((0,), (0,)), ((), ())), precision=lax.Prec...  11.7 us
    another operation x2, loops' own time, whitener(): lax.linalg.triangular_solve(lower, identity, left_side=True, lower=True)  11.6 us
    dot_general x5, matrix products, mm(): return jnp.dot(left, right, precision=lax.Precision.HIGHEST)  8.39 us
  transfers between devices with their start and end apart: 4, of which 1 were waited for; matrix products, arithmetic and copies ran while one was open for 26% of the time, Pallas kernels for 0%

commit v1 on v0

--- a/solution.py
+++ b/solution.py
@@ -102,12 +102,55 @@
     )(g)
 
 
+def inverse_kernel(a_ref, o_ref, work):
+    size = a_ref.shape[0]
+    rows_i = lax.broadcasted_iota(jnp.int32, (size, size), 0)
+    cols_i = lax.broadcasted_iota(jnp.int32, (size, size), 1)
+    diagonal = rows_i == cols_i
+    a = a_ref[...]
+    level = jnp.sum(jnp.where(diagonal, a, 0.0)) / size
+    work[:, :size] = a + jnp.where(diagonal, 0.1 * level, 0.0)
+    work[:, size:] = jnp.where(diagonal, 1.0, 0.0).astype(work.dtype)
+    tile = 8
+    lanes = 128
+    for block in range(size // tile):
+        top = block * tile
+        low = (top // lanes) * lanes
+        high = size + ((top + tile + lanes - 1) // lanes) * lanes
+        width = high - low
+        height = size - top
+        lane = lax.broadcasted_iota(jnp.int32, (1, width), 1) + low
+        row_id = lax.broadcasted_iota(jnp.int32, (height, 1), 0) + top
+
+        def step(t, carry, top=top, low=low, high=high, lane=lane, row_id=row_id):
+            k = top + t
+            row = work[pl.ds(k, 1), low:high]
+            pivot = jnp.sum(jnp.where(lane == k, row, 0.0), axis=1, keepdims=True)
+            scale = 1.0 / jnp.sqrt(pivot)
+            pivot_row = row * scale
+            part = work[top:, low:high]
+            column = jnp.sum(jnp.where(lane == k, part, 0.0), axis=1, keepdims=True) * scale
+            updated = jnp.where(row_id > k, part - column * pivot_row, part)
+            work[top:, low:high] = jnp.where(row_id == k, pivot_row, updated)
+            return carry
+
+        lax.fori_loop(0, tile, step, 0)
+    o_ref[...] = work[:, size:]
+
+
+def lower_inverse(scaled):
+    size = scaled.shape[0]
+    return pl.pallas_call(
+        inverse_kernel,
+        out_shape=jax.ShapeDtypeStruct((size, size), scaled.dtype),
+        in_specs=[pl.BlockSpec(memory_space=pltpu.VMEM)],
+        out_specs=pl.BlockSpec(memory_space=pltpu.VMEM),
+        scratch_shapes=[pltpu.VMEM((size, 2 * size), scaled.dtype)],
+    )(scaled)
+
+
 def whitener(scaled):
-    identity = jnp.eye(scaled.shape[0], dtype=scaled.dtype)
-    level = jnp.trace(scaled) / scaled.shape[0]
-    lower = jnp.linalg.cholesky(scaled + 0.1 * level * identity)
-    inverse = lax.linalg.triangular_solve(lower, identity, left_side=True, lower=True)
-    return inverse.T
+    return lower_inverse(scaled).T
 
 
 def mm(left, right):

time: 239 us -> 212 us (0.89); the launches traced: 235 us -> 212 us
  other arithmetic: 113 us -> 5.08 us
  Pallas kernels: 35.9 us -> 109 us
  waiting for transfers between devices: 11.8 us -> 47.3 us
  loops' own time: 11.6 us -> 0 us
  local copies, waits for them, and re-layouts: 12.6 us -> 3.22 us
  between operations: 4.47 us -> 0.22 us
    another operation x18 -> x0, other arithmetic: 108 us -> none  [the longest x13 68.7 us: whitener(): lower = jnp.linalg.cholesky(scaled + 0.1 * level * identity)]
    pallas_call x0 -> x2, Pallas kernels: none -> 73 us  [lower_inverse(): pl.pallas_call(inverse_kernel, out_shape=jax.ShapeDtypeStruct((size, size...]
    ppermute x4, waiting for transfers between devices: 11.8 us -> 47.3 us  [from_behind(): lax.ppermute(value, axis, [(source, source + steps) for source in range(l...]
    another operation x2 -> x0, loops' own time: 11.6 us -> none  [whitener(): lax.linalg.triangular_solve(lower, identity, left_side=True, lower=True)]
    another operation x19 -> x0, local copies, waits for them, and re-layouts: 7.99 us -> none  [the longest x15 7.94 us: whitener(): lax.linalg.triangular_solve(lower, identity, left_side=True, lower=True)]
    dot_general x5, matrix products: 8.39 us -> 11.7 us  [mm(): return jnp.dot(left, right, precision=lax.Precision.HIGHEST)]
    another operation x10 -> x0, matrix products: 2.97 us -> none  [the longest x6 2.02 us: whitener(): lax.linalg.triangular_solve(lower, identity, left_side=True, lower=True)]
  transfers between devices with their start and end apart: 4 -> 4, of which waited for: 1 -> 1; matrix products, arithmetic and copies ran while one was open for 26% -> 2% of each run, Pallas kernels for 0% -> 17%
where the time goes in v1:
time: 212 us
  Pallas kernels  109 us (51%)
  waiting for transfers between devices  47.3 us (22%)
  matrix products  24.2 us (11%)
  starting transfers between devices  22.6 us (11%)
  other arithmetic  5.08 us (2%)
  local copies, waits for them, and re-layouts  3.22 us (2%)
    pallas_call x2, Pallas kernels, lower_inverse(): pl.pallas_call(inverse_kernel, out_shape=jax.ShapeDtypeStruct((size, size...  73 us
    ppermute x4, waiting for transfers between devices, from_behind(): lax.ppermute(value, axis, [(source, source + steps) for source in range(l...  47.3 us
    pallas_call x2, Pallas kernels, allreduce_rows(): pl.pallas_call(functools.partial(allreduce_kernel, n, chunk), out_shape=j...  36 us
    ppermute x4, starting transfers between devices, from_behind(): lax.ppermute(value, axis, [(source, source + steps) for source in range(l...  22.6 us
    dot_general x4, matrix products, gram_of(): lax.dot_general(left, right, (((0,), (0,)), ((), ())), precision=lax.Prec...  12.5 us
    dot_general x5, matrix products, mm(): return jnp.dot(left, right, precision=lax.Precision.HIGHEST)  11.7 us
  transfers between devices with their start and end apart: 4, of which 1 were waited for; matrix products, arithmetic and copies ran while one was open for 2% of the time, Pallas kernels for 17%

profile of v1, /device:TPU:57, one launch (start us, length us, event | category | flops | bytes accessed | tf_op | source)
XLA Modules:
  0.0 211.8 jit_solution(2775678630785752379)
XLA Ops:
  0.0 6.5 %fusion.26.g_ref = f32[256,256]{1,0:T(8,128)} fusion(f32[2048,256]{1,0:T(8,128)} %param.1), kind=kOutput, calls=%fused_computation.32 | convolution fusion | flops 1610612736 | bytes 2359296 | tf_op jit(solution)/shard_map/dot_general | solution.py:20
  6.5 17.8 %shard_map.17 = f32[256,256]{1,0:T(8,128)} custom-call(f32[256,256]{1,0:T(8,128)} %fusion.26.g_ref), custom_call_target="tpu_custom_call" | custom-call | tf_op jit(solution)/shard_map/pallas_call | solution.py:89
  24.4 1.7 broadcast_multiply_fusion.a_ref
  26.1 4.0 %collective-permute-start = (f32[2048,256]{1,0:T(8,128)S(1)}, f32[2048,256]{1,0:T(8,128)}, u32[]{:S(2)}, u32[]{:S(2)}) collective-permute-start(f32[2048,256]{1,0:T(8,128)S(1)} %copy-done), channel_id=1, source_target_pairs={{0,1},{1,2},{2,3},{3,4},{4,5},{5,6},{6,7},{7,8},{8,9},{9,10},{10,1... | collective-permute-start | bytes 6291464 | tf_op jit(solution)/shard_map/ppermute | solution.py:16
  30.1 10.2 %collective-permute-start.1 = (f32[2048,256]{1,0:T(8,128)S(1)}, f32[2048,256]{1,0:T(8,128)}, u32[]{:S(2)}, u32[]{:S(2)}) collective-permute-start(f32[2048,256]{1,0:T(8,128)S(1)} %copy-done), channel_id=1, source_target_pairs={{1,0},{2,1},{3,2},{4,3},{5,4},{6,5},{7,6},{8,7},{9,8},{10,9},{11,1... | collective-permute-start | bytes 6291464 | tf_op jit(solution)/shard_map/ppermute | solution.py:16
  40.2 36.5 %shard_map.18 = f32[256,256]{1,0:T(8,128)} custom-call(f32[256,256]{1,0:T(8,128)} %broadcast_multiply_fusion.a_ref), custom_call_target="tpu_custom_call" | custom-call | tf_op jit(solution)/shard_map/pallas_call | solution.py:143
  76.8 1.1 copy.2
  77.9 1.4 fusion.27
  79.3 1.3 fusion.28
  80.7 1.9 collective-permute-start.2
  82.7 6.6 %collective-permute-start.3 = (f32[384,128]{1,0:T(8,128)S(1)}, f32[384,128]{1,0:T(8,128)S(1)}, u32[]{:S(2)}, u32[]{:S(2)}) collective-permute-start(f32[384,128]{1,0:T(8,128)S(1)} %get-tuple-element.18), channel_id=1, source_target_pairs={{1,0},{2,1},{3,2},{4,3},{5,4},{6,5},{7,6},{8,7},{9,8},{10,9},{11,1... | collective-permute-start | bytes 589832 | tf_op jit(solution)/shard_map/ppermute | solution.py:16
  89.2 47.3 %collective-permute-done.2 = f32[384,128]{1,0:T(8,128)S(1)} collective-permute-done((f32[384,128]{1,0:T(8,128)S(1)}, f32[384,128]{1,0:T(8,128)S(1)}, u32[]{:S(2)}, u32[]{:S(2)}) %collective-permute-start.2) | collective-permute-done | bytes 196640 | tf_op jit(solution)/shard_map/ppermute | solution.py:16
  136.6 2.6 %broadcast_select_fusion.1 = (f32[2048,256]{1,0:T(8,128)S(1)}, f32[2048,256]{1,0:T(8,128)S(1)}) fusion(f32[2048,256]{1,0:T(8,128)S(1)} %copy-done, f32[2048,256]{1,0:T(8,128)} %collective-permute-done, pred[]{:T(512)S(6)} %eq.6, f32[2048,256]{1,0:T(8,128)} %collective-permute-done.1, pred[]{:T(512)S(6)} %eq.7), kind=kLoop, calls=%fused_computation.5 | loop fusion | flops 1048576 | bytes 10485762 | tf_op jit(solution)/shard_map/jit(_where)/select_n | solution.py:176
  139.3 1.3 copy-done.1
  140.6 0.7 copy-done.3
  141.3 4.3 %fusion.29.g_ref = f32[256,256]{1,0:T(8,128)} fusion(f32[2048,256]{1,0:T(8,128)S(1)} %get-tuple-element.9, f32[2048,256]{1,0:T(8,128)S(1)} %get-tuple-element.10), kind=kOutput, calls=%fused_computation.35 | convolution fusion | flops 1610612736 | bytes 4456448 | tf_op jit(solution)/shard_map/dot_general | solution.py:20
  145.6 18.2 %shard_map.19 = f32[256,256]{1,0:T(8,128)} custom-call(f32[256,256]{1,0:T(8,128)} %fusion.29.g_ref), custom_call_target="tpu_custom_call" | custom-call | tf_op jit(solution)/shard_map/pallas_call | solution.py:89
  163.8 1.3 fusion.7
  165.1 0.4 fusion.20
  165.6 0.7 maximum_maximum_fusion.a_ref
  166.3 36.5 %shard_map.20 = f32[256,256]{1,0:T(8,128)} custom-call(f32[256,256]{1,0:T(8,128)} %maximum_maximum_fusion.a_ref), custom_call_target="tpu_custom_call" | custom-call | tf_op jit(solution)/shard_map/pallas_call | solution.py:143
  202.8 1.3 fusion.9
  204.1 1.3 fusion.11
  205.4 6.4 %fusion = f32[2048,256]{1,0:T(8,128)} fusion(f32[2048,256]{1,0:T(8,128)} %copy-done.3, f32[2048,256]{1,0:T(8,128)S(1)} %copy-done.2, f32[256,256]{1,0:T(8,128)S(1)} %fusion.9, f32[256,256]{1,0:T(8,128)S(1)} %fusion.11), kind=kOutput, calls=%fused_computation | convolution fusion | flops 3222405120 | bytes 6815744 | tf_op jit(solution)/shard_map/dot_general | solution.py:157
  (16 shorter events, 0.2 us)
Async XLA Ops:
  0.0 26.1 %copy-start = (f32[2048,256]{1,0:T(8,128)S(1)}, f32[2048,256]{1,0:T(8,128)}, u32[]{:S(2)}) copy-start(f32[2048,256]{1,0:T(8,128)} %param.1) | copy-start | bytes 6291460
  26.1 110.5 %collective-permute-start = (f32[2048,256]{1,0:T(8,128)S(1)}, f32[2048,256]{1,0:T(8,128)}, u32[]{:S(2)}, u32[]{:S(2)}) collective-permute-start(f32[2048,256]{1,0:T(8,128)S(1)} %copy-done), channel_id=1, source_target_pairs={{0,1},{1,2},{2,3},{3,4},{4,5},{5,6},{6,7},{7,8},{8,9},{9,10},{10,1... | collective-permute-start | bytes 6291464 | tf_op jit(solution)/shard_map/ppermute | solution.py:16
  30.1 106.5 %collective-permute-start.1 = (f32[2048,256]{1,0:T(8,128)S(1)}, f32[2048,256]{1,0:T(8,128)}, u32[]{:S(2)}, u32[]{:S(2)}) collective-permute-start(f32[2048,256]{1,0:T(8,128)S(1)} %copy-done), channel_id=1, source_target_pairs={{1,0},{2,1},{3,2},{4,3},{5,4},{6,5},{7,6},{8,7},{9,8},{10,9},{11,1... | collective-permute-start | bytes 6291464 | tf_op jit(solution)/shard_map/ppermute | solution.py:16
  80.7 55.8 %collective-permute-start.2 = (f32[384,128]{1,0:T(8,128)S(1)}, f32[384,128]{1,0:T(8,128)S(1)}, u32[]{:S(2)}, u32[]{:S(2)}) collective-permute-start(f32[384,128]{1,0:T(8,128)S(1)} %get-tuple-element.17), channel_id=1, source_target_pairs={{0,1},{1,2},{2,3},{3,4},{4,5},{5,6},{6,7},{7,8},{8,9},{9,10},{10,1... | collective-permute-start | bytes 589832 | tf_op jit(solution)/shard_map/ppermute | solution.py:16
  82.7 53.9 %collective-permute-start.3 = (f32[384,128]{1,0:T(8,128)S(1)}, f32[384,128]{1,0:T(8,128)S(1)}, u32[]{:S(2)}, u32[]{:S(2)}) collective-permute-start(f32[384,128]{1,0:T(8,128)S(1)} %get-tuple-element.18), channel_id=1, source_target_pairs={{1,0},{2,1},{3,2},{4,3},{5,4},{6,5},{7,6},{8,7},{9,8},{10,9},{11,1... | collective-permute-start | bytes 589832 | tf_op jit(solution)/shard_map/ppermute | solution.py:16
  139.3 1.3 copy-start.1
  139.3 2.0 copy-start.3
  145.6 59.8 %copy-start.2 = (f32[2048,256]{1,0:T(8,128)S(1)}, f32[2048,256]{1,0:T(8,128)}, u32[]{:S(2)}) copy-start(f32[2048,256]{1,0:T(8,128)} %copy-done.1) | copy-start | bytes 6291460

commit v2 on v1

--- a/solution.py
+++ b/solution.py
@@ -117,21 +117,21 @@
         top = block * tile
         low = (top // lanes) * lanes
         high = size + ((top + tile + lanes - 1) // lanes) * lanes
-        width = high - low
         height = size - top
-        lane = lax.broadcasted_iota(jnp.int32, (1, width), 1) + low
+        here = (top // lanes) * lanes
+        lane = lax.broadcasted_iota(jnp.int32, (1, lanes), 1) + here
         row_id = lax.broadcasted_iota(jnp.int32, (height, 1), 0) + top
 
-        def step(t, carry, top=top, low=low, high=high, lane=lane, row_id=row_id):
+        def step(t, carry, top=top, low=low, high=high, here=here, lane=lane, row_id=row_id):
             k = top + t
             row = work[pl.ds(k, 1), low:high]
-            pivot = jnp.sum(jnp.where(lane == k, row, 0.0), axis=1, keepdims=True)
+            pivot = jnp.sum(jnp.where(lane == k, row[:, here - low:here - low + lanes], 0.0), axis=1, keepdims=True)
             scale = 1.0 / jnp.sqrt(pivot)
             pivot_row = row * scale
-            part = work[top:, low:high]
-            column = jnp.sum(jnp.where(lane == k, part, 0.0), axis=1, keepdims=True) * scale
-            updated = jnp.where(row_id > k, part - column * pivot_row, part)
-            work[top:, low:high] = jnp.where(row_id == k, pivot_row, updated)
+            column = jnp.sum(jnp.where(lane == k, work[top:, here:here + lanes], 0.0), axis=1, keepdims=True)
+            column = jnp.where(row_id > k, column * scale, 0.0)
+            work[top:, low:high] = work[top:, low:high] - column * pivot_row
+            work[pl.ds(k, 1), low:high] = pivot_row
             return carry
 
         lax.fori_loop(0, tile, step, 0)

time: 212 us -> 209 us (0.986)
  Pallas kernels: 109 us -> 102 us
  waiting for transfers between devices: 47.3 us -> 51.1 us
    pallas_call x2, Pallas kernels: 73 us -> 65.6 us  [lower_inverse(): pl.pallas_call(inverse_kernel, out_shape=jax.ShapeDtypeStruct((size, size...]
    ppermute x4, waiting for transfers between devices: 47.3 us -> 51.1 us  [from_behind(): lax.ppermute(value, axis, [(source, source + steps) for source in range(l...]
  transfers between devices with their start and end apart: 4 -> 4, of which waited for: 1 -> 1; matrix products, arithmetic and copies ran while one was open for 2% -> 2% of each run, Pallas kernels for 17% -> 16%
where the time goes in v2:
time: 209 us; the launch traced here: 208 us
  Pallas kernels  102 us (49%)
  waiting for transfers between devices  51.1 us (24%)
  matrix products  24.2 us (12%)
  starting transfers between devices  22.6 us (11%)
  other arithmetic  5.08 us (2%)
  local copies, waits for them, and re-layouts  3.22 us (2%)
    pallas_call x2, Pallas kernels, lower_inverse(): pl.pallas_call(inverse_kernel, out_shape=jax.ShapeDtypeStruct((size, size...  65.6 us
    ppermute x4, waiting for transfers between devices, from_behind(): lax.ppermute(value, axis, [(source, source + steps) for source in range(l...  51.1 us
    pallas_call x2, Pallas kernels, allreduce_rows(): pl.pallas_call(functools.partial(allreduce_kernel, n, chunk), out_shape=j...  35.9 us
    ppermute x4, starting transfers between devices, from_behind(): lax.ppermute(value, axis, [(source, source + steps) for source in range(l...  22.6 us
    dot_general x4, matrix products, gram_of(): lax.dot_general(left, right, (((0,), (0,)), ((), ())), precision=lax.Prec...  12.5 us
    dot_general x5, matrix products, mm(): return jnp.dot(left, right, precision=lax.Precision.HIGHEST)  11.7 us
  transfers between devices with their start and end apart: 4, of which 1 were waited for; matrix products, arithmetic and copies ran while one was open for 2% of the time, Pallas kernels for 16%

profile of v2, /device:TPU:57, one launch (start us, length us, event | category | flops | bytes accessed | tf_op | source)
XLA Modules:
  0.0 208.1 jit_solution(3037783504617072887)
XLA Ops:
  0.0 6.5 %fusion.26.g_ref = f32[256,256]{1,0:T(8,128)} fusion(f32[2048,256]{1,0:T(8,128)} %param.1), kind=kOutput, calls=%fused_computation.32 | convolution fusion | flops 1610612736 | bytes 2359296 | tf_op jit(solution)/shard_map/dot_general | solution.py:20
  6.5 17.8 %shard_map.17 = f32[256,256]{1,0:T(8,128)} custom-call(f32[256,256]{1,0:T(8,128)} %fusion.26.g_ref), custom_call_target="tpu_custom_call" | custom-call | tf_op jit(solution)/shard_map/pallas_call | solution.py:89
  24.4 1.7 broadcast_multiply_fusion.a_ref
  26.1 4.0 %collective-permute-start = (f32[2048,256]{1,0:T(8,128)S(1)}, f32[2048,256]{1,0:T(8,128)}, u32[]{:S(2)}, u32[]{:S(2)}) collective-permute-start(f32[2048,256]{1,0:T(8,128)S(1)} %copy-done), channel_id=1, source_target_pairs={{0,1},{1,2},{2,3},{3,4},{4,5},{5,6},{6,7},{7,8},{8,9},{9,10},{10,1... | collective-permute-start | bytes 6291464 | tf_op jit(solution)/shard_map/ppermute | solution.py:16
  30.1 10.2 %collective-permute-start.1 = (f32[2048,256]{1,0:T(8,128)S(1)}, f32[2048,256]{1,0:T(8,128)}, u32[]{:S(2)}, u32[]{:S(2)}) collective-permute-start(f32[2048,256]{1,0:T(8,128)S(1)} %copy-done), channel_id=1, source_target_pairs={{1,0},{2,1},{3,2},{4,3},{5,4},{6,5},{7,6},{8,7},{9,8},{10,9},{11,1... | collective-permute-start | bytes 6291464 | tf_op jit(solution)/shard_map/ppermute | solution.py:16
  40.2 32.8 %shard_map.18 = f32[256,256]{1,0:T(8,128)} custom-call(f32[256,256]{1,0:T(8,128)} %broadcast_multiply_fusion.a_ref), custom_call_target="tpu_custom_call" | custom-call | tf_op jit(solution)/shard_map/pallas_call | solution.py:143
  73.1 1.1 copy.2
  74.2 1.4 fusion.27
  75.6 1.3 fusion.28
  77.0 1.9 collective-permute-start.2
  78.9 6.6 %collective-permute-start.3 = (f32[384,128]{1,0:T(8,128)S(1)}, f32[384,128]{1,0:T(8,128)S(1)}, u32[]{:S(2)}, u32[]{:S(2)}) collective-permute-start(f32[384,128]{1,0:T(8,128)S(1)} %get-tuple-element.18), channel_id=1, source_target_pairs={{1,0},{2,1},{3,2},{4,3},{5,4},{6,5},{7,6},{8,7},{9,8},{10,9},{11,1... | collective-permute-start | bytes 589832 | tf_op jit(solution)/shard_map/ppermute | solution.py:16
  85.5 51.1 %collective-permute-done.2 = f32[384,128]{1,0:T(8,128)S(1)} collective-permute-done((f32[384,128]{1,0:T(8,128)S(1)}, f32[384,128]{1,0:T(8,128)S(1)}, u32[]{:S(2)}, u32[]{:S(2)}) %collective-permute-start.2) | collective-permute-done | bytes 196640 | tf_op jit(solution)/shard_map/ppermute | solution.py:16
  136.7 2.6 %broadcast_select_fusion.1 = (f32[2048,256]{1,0:T(8,128)S(1)}, f32[2048,256]{1,0:T(8,128)S(1)}) fusion(f32[2048,256]{1,0:T(8,128)S(1)} %copy-done, f32[2048,256]{1,0:T(8,128)} %collective-permute-done, pred[]{:T(512)S(6)} %eq.6, f32[2048,256]{1,0:T(8,128)} %collective-permute-done.1, pred[]{:T(512)S(6)} %eq.7), kind=kLoop, calls=%fused_computation.5 | loop fusion | flops 1048576 | bytes 10485762 | tf_op jit(solution)/shard_map/jit(_where)/select_n | solution.py:176
  139.4 1.3 copy-done.1
  140.7 0.7 copy-done.3
  141.4 4.3 %fusion.29.g_ref = f32[256,256]{1,0:T(8,128)} fusion(f32[2048,256]{1,0:T(8,128)S(1)} %get-tuple-element.9, f32[2048,256]{1,0:T(8,128)S(1)} %get-tuple-element.10), kind=kOutput, calls=%fused_computation.35 | convolution fusion | flops 1610612736 | bytes 4456448 | tf_op jit(solution)/shard_map/dot_general | solution.py:20
  145.7 18.1 %shard_map.19 = f32[256,256]{1,0:T(8,128)} custom-call(f32[256,256]{1,0:T(8,128)} %fusion.29.g_ref), custom_call_target="tpu_custom_call" | custom-call | tf_op jit(solution)/shard_map/pallas_call | solution.py:89
  163.8 1.3 fusion.7
  165.1 0.4 fusion.20
  165.6 0.7 maximum_maximum_fusion.a_ref
  166.3 32.8 %shard_map.20 = f32[256,256]{1,0:T(8,128)} custom-call(f32[256,256]{1,0:T(8,128)} %maximum_maximum_fusion.a_ref), custom_call_target="tpu_custom_call" | custom-call | tf_op jit(solution)/shard_map/pallas_call | solution.py:143
  199.1 1.3 fusion.9
  200.4 1.3 fusion.11
  201.7 6.4 %fusion = f32[2048,256]{1,0:T(8,128)} fusion(f32[2048,256]{1,0:T(8,128)} %copy-done.3, f32[2048,256]{1,0:T(8,128)S(1)} %copy-done.2, f32[256,256]{1,0:T(8,128)S(1)} %fusion.9, f32[256,256]{1,0:T(8,128)S(1)} %fusion.11), kind=kOutput, calls=%fused_computation | convolution fusion | flops 3222405120 | bytes 6815744 | tf_op jit(solution)/shard_map/dot_general | solution.py:157
  (16 shorter events, 0.2 us)
Async XLA Ops:
  0.0 26.1 %copy-start = (f32[2048,256]{1,0:T(8,128)S(1)}, f32[2048,256]{1,0:T(8,128)}, u32[]{:S(2)}) copy-start(f32[2048,256]{1,0:T(8,128)} %param.1) | copy-start | bytes 6291460
  26.1 110.6 %collective-permute-start = (f32[2048,256]{1,0:T(8,128)S(1)}, f32[2048,256]{1,0:T(8,128)}, u32[]{:S(2)}, u32[]{:S(2)}) collective-permute-start(f32[2048,256]{1,0:T(8,128)S(1)} %copy-done), channel_id=1, source_target_pairs={{0,1},{1,2},{2,3},{3,4},{4,5},{5,6},{6,7},{7,8},{8,9},{9,10},{10,1... | collective-permute-start | bytes 6291464 | tf_op jit(solution)/shard_map/ppermute | solution.py:16
  30.1 106.6 %collective-permute-start.1 = (f32[2048,256]{1,0:T(8,128)S(1)}, f32[2048,256]{1,0:T(8,128)}, u32[]{:S(2)}, u32[]{:S(2)}) collective-permute-start(f32[2048,256]{1,0:T(8,128)S(1)} %copy-done), channel_id=1, source_target_pairs={{1,0},{2,1},{3,2},{4,3},{5,4},{6,5},{7,6},{8,7},{9,8},{10,9},{11,1... | collective-permute-start | bytes 6291464 | tf_op jit(solution)/shard_map/ppermute | solution.py:16
  77.0 59.6 %collective-permute-start.2 = (f32[384,128]{1,0:T(8,128)S(1)}, f32[384,128]{1,0:T(8,128)S(1)}, u32[]{:S(2)}, u32[]{:S(2)}) collective-permute-start(f32[384,128]{1,0:T(8,128)S(1)} %get-tuple-element.17), channel_id=1, source_target_pairs={{0,1},{1,2},{2,3},{3,4},{4,5},{5,6},{6,7},{7,8},{8,9},{9,10},{10,1... | collective-permute-start | bytes 589832 | tf_op jit(solution)/shard_map/ppermute | solution.py:16
  78.9 57.7 %collective-permute-start.3 = (f32[384,128]{1,0:T(8,128)S(1)}, f32[384,128]{1,0:T(8,128)S(1)}, u32[]{:S(2)}, u32[]{:S(2)}) collective-permute-start(f32[384,128]{1,0:T(8,128)S(1)} %get-tuple-element.18), channel_id=1, source_target_pairs={{1,0},{2,1},{3,2},{4,3},{5,4},{6,5},{7,6},{8,7},{9,8},{10,9},{11,1... | collective-permute-start | bytes 589832 | tf_op jit(solution)/shard_map/ppermute | solution.py:16
  139.3 1.3 copy-start.1
  139.4 2.0 copy-start.3
  145.7 56.0 %copy-start.2 = (f32[2048,256]{1,0:T(8,128)S(1)}, f32[2048,256]{1,0:T(8,128)}, u32[]{:S(2)}) copy-start(f32[2048,256]{1,0:T(8,128)} %copy-done.1) | copy-start | bytes 6291460

commit v3 on v2

--- a/solution.py
+++ b/solution.py
@@ -82,7 +82,7 @@
         copy.wait_send()
 
 
-def allreduce_rows(g):
+def allreduce_rows(g, key):
     n = lax.axis_size("rows")
     rows, cols = g.shape
     chunk = rows // n
@@ -98,7 +98,7 @@
             pltpu.SemaphoreType.DMA((n,)),
             pltpu.SemaphoreType.DMA((n,)),
         ],
-        compiler_params=pltpu.CompilerParams(collective_id=0, has_side_effects=True),
+        compiler_params=pltpu.CompilerParams(collective_id=key, has_side_effects=True),
     )(g)
 
 
@@ -161,7 +161,7 @@
     return gram_of(left, right)
 
 
-def per_device(snapshots):
+def per_device(far, snapshots):
     local_rows = snapshots.shape[0]
     total = local_rows * lax.axis_size("rows")
     width = snapshots.shape[1] // 2
@@ -171,12 +171,12 @@
     last = index == count - 1
     pair = snapshots
 
-    gram = allreduce_rows(gram_of(pair, pair)) / total
+    gram = allreduce_rows(gram_of(pair, pair), 0) / total
     sent, gram = lax.optimization_barrier((pair, gram))
-    raw_a = jnp.where(first, pair, from_behind(sent, "pairs", 1))
-    raw_b = jnp.where(last, pair, from_behind(sent, "pairs", -1))
-
-    cross = allreduce_rows(gram_of(raw_a, raw_b)) / total
+    near_up = [(j, j + 1) for j in range(count - 1) if j not in far]
+    near_down = [(j + 1, j) for j in range(count - 1) if j not in far]
+    raw_a = jnp.where(first, pair, lax.ppermute(sent, "pairs", near_up))
+    raw_b = jnp.where(last, pair, lax.ppermute(sent, "pairs", near_down))
 
     whiten = whitener(gram)
     moment = tmm(whiten, mm(gram, whiten))
@@ -191,18 +191,41 @@
     x_a, m_a = side_a[:rows], side_a[rows:]
     x_b, m_b = side_b[:rows], side_b[rows:]
 
-    off = tmm(x_a, mm(cross, x_b))
+    top_next = mm(raw_a, x_a)
+    bottom_next = mm(raw_b, x_b)
+    if far:
+        far_a = jnp.asarray([j - 1 in far for j in range(count)])[index]
+        far_b = jnp.asarray([j in far for j in range(count)])[index]
+        half_a = jnp.where(first, whiten[:, width:], whiten[:, :width])
+        late_a = lax.ppermute(mm(pair, half_a), "pairs", [(j, j + 1) for j in sorted(far)])
+        late_b = lax.ppermute(mm(pair, whiten[:, width:]), "pairs", [(j + 1, j) for j in sorted(far)])
+        top_next = jnp.where(far_a, late_a, top_next)
+        bottom_next = jnp.where(far_b, late_b, bottom_next)
+
+    off = allreduce_rows(gram_of(top_next, bottom_next), 1) / total
     gram2 = jnp.concatenate(
         [jnp.concatenate([m_a, off], axis=1), jnp.concatenate([off.T, m_b], axis=1)], axis=0
     )
     whiten2 = whitener(gram2)
-    combined = jnp.concatenate([mm(x_a, whiten2[:width]), mm(x_b, whiten2[width:])], axis=0)
-    return mm(jnp.concatenate([raw_a, raw_b], axis=1), combined)
+    return mm(top_next, whiten2[:width]) + mm(bottom_next, whiten2[width:])
+
+
+def far_links(mesh):
+    far = set()
+    line = mesh.devices[0]
+    for j in range(len(line) - 1):
+        here, there = getattr(line[j], "coords", None), getattr(line[j + 1], "coords", None)
+        if here is None or there is None:
+            continue
+        gaps = [abs(p - q) for p, q in zip(here, there)]
+        if sum(gaps) > 1:
+            far.add(j)
+    return frozenset(far)
 
 
 def solution(mesh):
     return jax.shard_map(
-        per_device,
+        functools.partial(per_device, far_links(mesh)),
         mesh=mesh,
         in_specs=(P("rows", "pairs"),),
         out_specs=P("rows", "pairs"),

time: 209 us -> 221 us (1.057)
  waiting for transfers between devices: 51.1 us -> 61.2 us
  matrix products: 24.2 us -> 31.2 us
  Pallas kernels: 102 us -> 97 us
    ppermute x0 -> x4, starting transfers between devices: none -> 19.5 us  [the longest x1 10.9 us: per_device(): lax.ppermute(mm(pair, whiten[:, width:]), 'pairs', [(j + 1, j) for j in s...]
    ppermute x4 -> x2, starting transfers between devices: 22.6 us -> 4.01 us  [from_behind(): lax.ppermute(value, axis, [(source, source + steps) for source in range(l...]
    dot_general x5 -> x7, matrix products: 11.7 us -> 22.6 us  [mm(): return jnp.dot(left, right, precision=lax.Precision.HIGHEST)]
    ppermute x4 -> x2, waiting for transfers between devices: 51.1 us -> 61.2 us  [from_behind(): lax.ppermute(value, axis, [(source, source + steps) for source in range(l...]
    pallas_call x2, Pallas kernels: 35.9 us -> 31.4 us  [allreduce_rows(): pl.pallas_call(functools.partial(allreduce_kernel, n, chunk), out_shape=j...]
    dot_general x4 -> x3, matrix products: 12.5 us -> 8.56 us  [gram_of(): lax.dot_general(left, right, (((0,), (0,)), ((), ())), precision=lax.Prec...]
    select_n x1 -> x0, other arithmetic: 2.64 us -> none  [per_device(): raw_a = jnp.where(first, pair, from_behind(sent, 'pairs', 1))]
  transfers between devices with their start and end apart: 4 -> 6, of which waited for: 1 -> 2; matrix products, arithmetic and copies ran while one was open for 2% -> 7% of each run, Pallas kernels for 16% -> 15%
where the time goes in v3:
time: 221 us; the launch traced here: 220 us
  Pallas kernels  97 us (44%)
  waiting for transfers between devices  61.2 us (28%)
  matrix products  31.2 us (14%)
  starting transfers between devices  23.5 us (11%)
  local copies, waits for them, and re-layouts  3.44 us (2%)
  other arithmetic  3.32 us (2%)
    pallas_call x2, Pallas kernels, lower_inverse(): pl.pallas_call(inverse_kernel, out_shape=jax.ShapeDtypeStruct((size, size...  65.6 us
    ppermute x2, waiting for transfers between devices, from_behind(): lax.ppermute(value, axis, [(source, source + steps) for source in range(l...  61.2 us
    pallas_call x2, Pallas kernels, allreduce_rows(): pl.pallas_call(functools.partial(allreduce_kernel, n, chunk), out_shape=j...  31.4 us
    dot_general x7, matrix products, mm(): return jnp.dot(left, right, precision=lax.Precision.HIGHEST)  22.6 us
    ppermute x1, starting transfers between devices, per_device(): lax.ppermute(mm(pair, whiten[:, width:]), 'pairs', [(j + 1, j) for j in s...  10.9 us
    dot_general x3, matrix products, gram_of(): lax.dot_general(left, right, (((0,), (0,)), ((), ())), precision=lax.Prec...  8.56 us
    ppermute x1, starting transfers between devices, per_device(): raw_a = jnp.where(first, pair, lax.ppermute(sent, 'pairs', near_up))  5.97 us
  transfers between devices with their start and end apart: 6, of which 2 were waited for; matrix products, arithmetic and copies ran while one was open for 7% of the time, Pallas kernels for 15%

profile of v3, /device:TPU:57, one launch (start us, length us, event | category | flops | bytes accessed | tf_op | source)
XLA Modules:
  0.0 220.0 jit_solution(17640946320836470039)
XLA Ops:
  0.0 6.5 %fusion.20.g_ref = f32[256,256]{1,0:T(8,128)} fusion(f32[2048,256]{1,0:T(8,128)} %param.3), kind=kOutput, calls=%fused_computation.30 | convolution fusion | flops 1610612736 | bytes 2359296 | tf_op jit(solution)/shard_map/dot_general | solution.py:20
  6.5 17.9 %shard_map.37 = f32[256,256]{1,0:T(8,128)} custom-call(f32[256,256]{1,0:T(8,128)} %fusion.20.g_ref), custom_call_target="tpu_custom_call" | custom-call | tf_op jit(solution)/shard_map/pallas_call | solution.py:89
  24.4 1.7 broadcast_multiply_fusion.a_ref
  26.1 1.3 collective-permute-start.4
  27.4 6.0 %collective-permute-start.1 = (f32[2048,256]{1,0:T(8,128)S(1)}, f32[2048,256]{1,0:T(8,128)}, u32[]{:S(2)}, u32[]{:S(2)}) collective-permute-start(f32[2048,256]{1,0:T(8,128)S(1)} %copy-done), channel_id=1, source_target_pairs={{0,1},{1,2},{2,3},{3,4},{4,5},{5,6},{6,7},{8,9},{9,10},{10,11},{11... | collective-permute-start | bytes 6291464 | tf_op jit(solution)/shard_map/ppermute | solution.py:178
  33.3 32.8 %shard_map.38 = f32[256,256]{1,0:T(8,128)} custom-call(f32[256,256]{1,0:T(8,128)} %broadcast_multiply_fusion.a_ref), custom_call_target="tpu_custom_call" | custom-call | tf_op jit(solution)/shard_map/pallas_call | solution.py:143
  66.2 1.1 copy.4
  67.2 3.3 %convolution_bitcast_fusion = f32[2048,128]{0,1:T(8,128)} fusion(f32[2048,256]{1,0:T(8,128)S(1)} %copy-done, f32[256,256]{1,0:T(8,128)S(1)} %bitcast.22), kind=kOutput, calls=%fused_computation.3 | convolution fusion | flops 805306368 | bytes 3276800 | tf_op jit(solution)/shard_map/dot_general | solution.py:157
  70.5 10.9 %collective-permute-start.3 = (f32[2048,128]{0,1:T(8,128)}, f32[2048,128]{0,1:T(8,128)}, u32[]{:S(2)}, u32[]{:S(2)}) collective-permute-start(f32[2048,128]{0,1:T(8,128)} %convolution_bitcast_fusion), channel_id=1, source_target_pairs={{8,7},{16,15},{24,23},{40,39},{48,47},{56,55},{72,71},{80,79},{88,... | collective-permute-start | bytes 3145736 | tf_op jit(solution)/shard_map/ppermute | solution.py:201
  81.4 3.3 %convolution_bitcast_fusion.1 = f32[2048,128]{0,1:T(8,128)} fusion(f32[2048,256]{1,0:T(8,128)S(1)} %copy-done, pred[]{:T(512)S(6)} %eq.6, f32[256,256]{1,0:T(8,128)S(1)} %bitcast.23), kind=kOutput, calls=%fused_computation.4 | convolution fusion | flops 805339136 | bytes 3407873 | tf_op jit(solution)/shard_map/dot_general | solution.py:157
  84.7 1.4 collective-permute-start
  87.1 1.9 collective-permute-start.2
  89.0 56.9 %collective-permute-done.2 = f32[384,128]{1,0:T(8,128)S(1)} collective-permute-done((f32[384,128]{1,0:T(8,128)S(1)}, f32[384,128]{1,0:T(8,128)S(1)}, u32[]{:S(2)}, u32[]{:S(2)}) %collective-permute-start.2) | collective-permute-done | bytes 196640 | tf_op jit(solution)/shard_map/ppermute | solution.py:16
  145.9 2.1 collective-permute-start.5
  149.2 4.3 %collective-permute-done.5 = f32[384,128]{1,0:T(8,128)S(1)} collective-permute-done((f32[384,128]{1,0:T(8,128)S(1)}, f32[384,128]{1,0:T(8,128)S(1)}, u32[]{:S(2)}, u32[]{:S(2)}) %collective-permute-start.5) | collective-permute-done | bytes 196640 | tf_op jit(solution)/shard_map/ppermute | solution.py:16
  153.6 4.6 %convolution_select_fusion = f32[2048,128]{0,1:T(8,128)S(1)} fusion(f32[2048,128]{0,1:T(8,128)} %collective-permute-done.3, f32[2048,256]{1,0:T(8,128)S(1)} %copy-done, f32[2048,256]{1,0:T(8,128)} %collective-permute-done.4, pred[]{:T(512)S(6)} %eq.7, pred[]{:T(512)} %bitcast.3, f32[384,128]{1,0:T(8,128)S(1)} %get-tuple-element.14), kind=kOutput, calls=%fused_computation.1 | convolution fusion | flops 806092800 | bytes 6422530 | tf_op jit(solution)/shard_map/dot_general | solution.py:157
  158.3 4.9 %convolution_select_fusion.1 = f32[2048,128]{0,1:T(8,128)S(1)} fusion(f32[2048,128]{0,1:T(8,128)} %collective-permute-done, f32[2048,256]{1,0:T(8,128)S(1)} %copy-done, f32[2048,256]{1,0:T(8,128)} %collective-permute-done.1, pred[]{:T(512)S(6)} %eq.6, pred[]{:T(512)} %bitcast, f32[384,128]{1,0:T(8,128)S(1)} %get-tuple-element.13), kind=kOutput, calls=%fused_computation.2 | convolution fusion | flops 806092800 | bytes 6422530 | tf_op jit(solution)/shard_map/dot_general | solution.py:157
  163.2 1.0 copy-done.1
  164.2 1.6 fusion.23.g_ref
  165.8 13.6 %shard_map.39 = f32[128,128]{1,0:T(8,128)} custom-call(f32[128,128]{1,0:T(8,128)} %fusion.23.g_ref), custom_call_target="tpu_custom_call" | custom-call | tf_op jit(solution)/shard_map/pallas_call | solution.py:89
  179.4 0.9 broadcast_multiply_fusion.1
  181.1 32.8 %shard_map.40 = f32[256,256]{1,0:T(8,128)} custom-call(f32[256,256]{1,0:T(8,128)} %maximum_maximum_fusion.a_ref), custom_call_target="tpu_custom_call" | custom-call | tf_op jit(solution)/shard_map/pallas_call | solution.py:143
  213.9 2.8 %fusion.4 = f32[2048,256]{1,0:T(8,128)S(1)} fusion(f32[2048,128]{0,1:T(8,128)S(1)} %convolution_select_fusion, f32[256,256]{0,1:T(8,128)} %bitcast.25), kind=kOutput, calls=%fused_computation.12 | convolution fusion | flops 805306368 | bytes 3276800 | tf_op jit(solution)/shard_map/dot_general | solution.py:157
  216.8 3.2 %convolution_add_fusion = f32[2048,256]{1,0:T(8,128)} fusion(f32[2048,256]{1,0:T(8,128)S(1)} %fusion.4, f32[2048,128]{0,1:T(8,128)S(1)} %copy-done.2, f32[256,256]{0,1:T(8,128)S(1)} %bitcast.26), kind=kOutput, calls=%fused_computation | convolution fusion | flops 805830656 | bytes 5373952 | tf_op jit(solution)/shard_map/dot_general | solution.py:157
  (31 shorter events, 3.0 us)
Async XLA Ops:
  0.0 26.1 %copy-start = (f32[2048,256]{1,0:T(8,128)S(1)}, f32[2048,256]{1,0:T(8,128)}, u32[]{:S(2)}) copy-start(f32[2048,256]{1,0:T(8,128)} %param.3) | copy-start | bytes 6291460
  26.1 127.6 %collective-permute-start.4 = (f32[2048,256]{1,0:T(8,128)S(1)}, f32[2048,256]{1,0:T(8,128)}, u32[]{:S(2)}, u32[]{:S(2)}) collective-permute-start(f32[2048,256]{1,0:T(8,128)S(1)} %copy-done), channel_id=1, source_target_pairs={{1,0},{2,1},{3,2},{4,3},{5,4},{6,5},{7,6},{9,8},{10,9},{11,10},{12... | collective-permute-start | bytes 6291464 | tf_op jit(solution)/shard_map/ppermute | solution.py:179
  27.4 130.9 %collective-permute-start.1 = (f32[2048,256]{1,0:T(8,128)S(1)}, f32[2048,256]{1,0:T(8,128)}, u32[]{:S(2)}, u32[]{:S(2)}) collective-permute-start(f32[2048,256]{1,0:T(8,128)S(1)} %copy-done), channel_id=1, source_target_pairs={{0,1},{1,2},{2,3},{3,4},{4,5},{5,6},{6,7},{8,9},{9,10},{10,11},{11... | collective-permute-start | bytes 6291464 | tf_op jit(solution)/shard_map/ppermute | solution.py:178
  70.5 15.6 %copy-start.3 = (f32[256,256]{1,0:T(8,128)S(1)}, f32[256,256]{1,0:T(8,128)}, u32[]{:S(2)}) copy-start(f32[256,256]{1,0:T(8,128)} %shard_map.38) | copy-start | bytes 786436
  70.5 15.6 %copy-start.4 = (f32[256,256]{1,0:T(8,128)S(1)}, f32[256,256]{1,0:T(8,128)}, u32[]{:S(2)}) copy-start(f32[256,256]{1,0:T(8,128)} %broadcast_multiply_fusion.a_ref) | copy-start | bytes 786436
  70.5 83.1 %collective-permute-start.3 = (f32[2048,128]{0,1:T(8,128)}, f32[2048,128]{0,1:T(8,128)}, u32[]{:S(2)}, u32[]{:S(2)}) collective-permute-start(f32[2048,128]{0,1:T(8,128)} %convolution_bitcast_fusion), channel_id=1, source_target_pairs={{8,7},{16,15},{24,23},{40,39},{48,47},{56,55},{72,71},{80,79},{88,... | collective-permute-start | bytes 3145736 | tf_op jit(solution)/shard_map/ppermute | solution.py:201
  84.7 63.3 %copy-start.7 = (pred[32]{0:T(512)(128)(4,1)S(1)}, pred[32]{0:T(512)(128)(4,1)}, u32[]{:S(2)}) copy-start(pred[32]{0:T(512)(128)(4,1)} %constant.20.clone) | copy-start | bytes 100
  84.7 63.9 %copy-start.6 = (pred[32]{0:T(512)(128)(4,1)S(1)}, pred[32]{0:T(512)(128)(4,1)}, u32[]{:S(2)}) copy-start(pred[32]{0:T(512)(128)(4,1)} %constant.19.clone) | copy-start | bytes 100
  84.7 73.5 %collective-permute-start = (f32[2048,128]{0,1:T(8,128)}, f32[2048,128]{0,1:T(8,128)}, u32[]{:S(2)}, u32[]{:S(2)}) collective-permute-start(f32[2048,128]{0,1:T(8,128)} %convolution_bitcast_fusion.1), channel_id=1, source_target_pairs={{7,8},{15,16},{23,24},{39,40},{47,48},{55,56},{71,72},{79,80},{87,... | collective-permute-start | bytes 3145736 | tf_op jit(solution)/shard_map/ppermute | solution.py:200
  87.1 58.8 %collective-permute-start.2 = (f32[384,128]{1,0:T(8,128)S(1)}, f32[384,128]{1,0:T(8,128)S(1)}, u32[]{:S(2)}, u32[]{:S(2)}) collective-permute-start(f32[384,128]{1,0:T(8,128)S(1)} %get-tuple-element.15), channel_id=1, source_target_pairs={{0,1},{1,2},{2,3},{3,4},{4,5},{5,6},{6,7},{7,8},{8,9},{9,10},{10,1... | collective-permute-start | bytes 589832 | tf_op jit(solution)/shard_map/ppermute | solution.py:16
  145.9 7.7 %collective-permute-start.5 = (f32[384,128]{1,0:T(8,128)S(1)}, f32[384,128]{1,0:T(8,128)S(1)}, u32[]{:S(2)}, u32[]{:S(2)}) collective-permute-start(f32[384,128]{1,0:T(8,128)S(1)} %get-tuple-element.16), channel_id=1, source_target_pairs={{1,0},{2,1},{3,2},{4,3},{5,4},{6,5},{7,6},{8,7},{9,8},{10,9},{11,1... | collective-permute-start | bytes 589832 | tf_op jit(solution)/shard_map/ppermute | solution.py:16
  163.2 1.0 copy-start.1
  180.3 36.4 %copy-start.2 = (f32[2048,128]{0,1:T(8,128)S(1)}, f32[2048,128]{0,1:T(8,128)}, u32[]{:S(2)}) copy-start(f32[2048,128]{0,1:T(8,128)} %copy-done.1) | copy-start | bytes 3145732
  213.9 2.9 %copy-start.5 = (f32[256,256]{1,0:T(8,128)S(1)}, f32[256,256]{1,0:T(8,128)}, u32[]{:S(2)}) copy-start(f32[256,256]{1,0:T(8,128)} %shard_map.40) | copy-start | bytes 786436

commit v4 on v2

--- a/solution.py
+++ b/solution.py
@@ -102,21 +102,13 @@
     )(g)
 
 
-def inverse_kernel(a_ref, o_ref, work):
-    size = a_ref.shape[0]
-    rows_i = lax.broadcasted_iota(jnp.int32, (size, size), 0)
-    cols_i = lax.broadcasted_iota(jnp.int32, (size, size), 1)
-    diagonal = rows_i == cols_i
-    a = a_ref[...]
-    level = jnp.sum(jnp.where(diagonal, a, 0.0)) / size
-    work[:, :size] = a + jnp.where(diagonal, 0.1 * level, 0.0)
-    work[:, size:] = jnp.where(diagonal, 1.0, 0.0).astype(work.dtype)
+def eliminate(work, size):
     tile = 8
     lanes = 128
     for block in range(size // tile):
         top = block * tile
         low = (top // lanes) * lanes
-        high = size + ((top + tile + lanes - 1) // lanes) * lanes
+        high = size + min(size, ((top + tile + lanes - 1) // lanes) * lanes)
         height = size - top
         here = (top // lanes) * lanes
         lane = lax.broadcasted_iota(jnp.int32, (1, lanes), 1) + here
@@ -135,7 +127,37 @@
             return carry
 
         lax.fori_loop(0, tile, step, 0)
-    o_ref[...] = work[:, size:]
+
+
+def inverse_kernel(a_ref, o_ref, work):
+    size = a_ref.shape[0]
+    half = size // 2
+    rows_i = lax.broadcasted_iota(jnp.int32, (size, size), 0)
+    cols_i = lax.broadcasted_iota(jnp.int32, (size, size), 1)
+    diagonal = rows_i == cols_i
+    a = a_ref[...]
+    level = jnp.sum(jnp.where(diagonal, a, 0.0)) / size
+    a = a + jnp.where(diagonal, 0.1 * level, 0.0)
+    eye = jnp.where(diagonal[:half, :half], 1.0, 0.0).astype(a.dtype)
+    hi = lax.Precision.HIGHEST
+    nt = (((1,), (1,)), ((), ()))
+
+    work[:, :half] = a[:half, :half]
+    work[:, half:] = eye
+    eliminate(work, half)
+    inv11 = work[:, half:]
+    low21 = lax.dot_general(a[half:, :half], inv11, nt, precision=hi, preferred_element_type=jnp.float32)
+    schur = a[half:, half:] - lax.dot_general(low21, low21, nt, precision=hi, preferred_element_type=jnp.float32)
+    work[:, :half] = schur
+    work[:, half:] = eye
+    eliminate(work, half)
+    inv22 = work[:, half:]
+    mid = jnp.dot(inv22, low21, precision=hi, preferred_element_type=jnp.float32)
+    inv21 = -jnp.dot(mid, inv11, precision=hi, preferred_element_type=jnp.float32)
+    o_ref[:half, :half] = inv11
+    o_ref[:half, half:] = jnp.zeros((half, half), a.dtype)
+    o_ref[half:, :half] = inv21
+    o_ref[half:, half:] = inv22
 
 
 def lower_inverse(scaled):
@@ -145,7 +167,7 @@
         out_shape=jax.ShapeDtypeStruct((size, size), scaled.dtype),
         in_specs=[pl.BlockSpec(memory_space=pltpu.VMEM)],
         out_specs=pl.BlockSpec(memory_space=pltpu.VMEM),
-        scratch_shapes=[pltpu.VMEM((size, 2 * size), scaled.dtype)],
+        scratch_shapes=[pltpu.VMEM((size // 2, size), scaled.dtype)],
     )(scaled)
 
 

time: 209 us -> 206 us (0.986)
  Pallas kernels: 102 us -> 95.4 us
  waiting for transfers between devices: 51.1 us -> 54.7 us
    pallas_call x2, Pallas kernels: 65.6 us -> 60.5 us  [lower_inverse(): pl.pallas_call(inverse_kernel, out_shape=jax.ShapeDtypeStruct((size, size...]
    ppermute x4, waiting for transfers between devices: 51.1 us -> 54.7 us  [from_behind(): lax.ppermute(value, axis, [(source, source + steps) for source in range(l...]
  transfers between devices with their start and end apart: 4 -> 4, of which waited for: 1 -> 1; matrix products, arithmetic and copies ran while one was open for 2% -> 2% of each run, Pallas kernels for 16% -> 15%
where the time goes in v4:
time: 206 us
  Pallas kernels  95.4 us (46%)
  waiting for transfers between devices  54.7 us (27%)
  matrix products  24.3 us (12%)
  starting transfers between devices  22.6 us (11%)
  other arithmetic  5.08 us (2%)
  local copies, waits for them, and re-layouts  3.22 us (2%)
    pallas_call x2, Pallas kernels, lower_inverse(): pl.pallas_call(inverse_kernel, out_shape=jax.ShapeDtypeStruct((size, size...  60.5 us
    ppermute x4, waiting for transfers between devices, from_behind(): lax.ppermute(value, axis, [(source, source + steps) for source in range(l...  54.7 us
    pallas_call x2, Pallas kernels, allreduce_rows(): pl.pallas_call(functools.partial(allreduce_kernel, n, chunk), out_shape=j...  34.9 us
    ppermute x4, starting transfers between devices, from_behind(): lax.ppermute(value, axis, [(source, source + steps) for source in range(l...  22.6 us
    dot_general x4, matrix products, gram_of(): lax.dot_general(left, right, (((0,), (0,)), ((), ())), precision=lax.Prec...  12.5 us
    dot_general x5, matrix products, mm(): return jnp.dot(left, right, precision=lax.Precision.HIGHEST)  11.7 us
  transfers between devices with their start and end apart: 4, of which 1 were waited for; matrix products, arithmetic and copies ran while one was open for 2% of the time, Pallas kernels for 15%

profile of v4, /device:TPU:57, one launch (start us, length us, event | category | flops | bytes accessed | tf_op | source)
XLA Modules:
  0.0 205.5 jit_solution(7755514004536937516)
XLA Ops:
  0.0 6.5 %fusion.26.g_ref = f32[256,256]{1,0:T(8,128)} fusion(f32[2048,256]{1,0:T(8,128)} %param.1), kind=kOutput, calls=%fused_computation.32 | convolution fusion | flops 1610612736 | bytes 2359296 | tf_op jit(solution)/shard_map/dot_general | solution.py:20
  6.5 17.8 %shard_map.17 = f32[256,256]{1,0:T(8,128)} custom-call(f32[256,256]{1,0:T(8,128)} %fusion.26.g_ref), custom_call_target="tpu_custom_call" | custom-call | tf_op jit(solution)/shard_map/pallas_call | solution.py:89
  24.4 1.7 broadcast_multiply_fusion.a_ref
  26.1 4.0 %collective-permute-start = (f32[2048,256]{1,0:T(8,128)S(1)}, f32[2048,256]{1,0:T(8,128)}, u32[]{:S(2)}, u32[]{:S(2)}) collective-permute-start(f32[2048,256]{1,0:T(8,128)S(1)} %copy-done), channel_id=1, source_target_pairs={{0,1},{1,2},{2,3},{3,4},{4,5},{5,6},{6,7},{7,8},{8,9},{9,10},{10,1... | collective-permute-start | bytes 6291464 | tf_op jit(solution)/shard_map/ppermute | solution.py:16
  30.1 10.2 %collective-permute-start.1 = (f32[2048,256]{1,0:T(8,128)S(1)}, f32[2048,256]{1,0:T(8,128)}, u32[]{:S(2)}, u32[]{:S(2)}) collective-permute-start(f32[2048,256]{1,0:T(8,128)S(1)} %copy-done), channel_id=1, source_target_pairs={{1,0},{2,1},{3,2},{4,3},{5,4},{6,5},{7,6},{8,7},{9,8},{10,9},{11,1... | collective-permute-start | bytes 6291464 | tf_op jit(solution)/shard_map/ppermute | solution.py:16
  40.2 30.3 %shard_map.18 = f32[256,256]{1,0:T(8,128)} custom-call(f32[256,256]{1,0:T(8,128)} %broadcast_multiply_fusion.a_ref), custom_call_target="tpu_custom_call" | custom-call | tf_op jit(solution)/shard_map/pallas_call | solution.py:165
  70.5 1.1 copy.2
  71.6 1.4 fusion.27
  73.0 1.3 fusion.28
  74.5 1.9 collective-permute-start.2
  76.4 6.6 %collective-permute-start.3 = (f32[384,128]{1,0:T(8,128)S(1)}, f32[384,128]{1,0:T(8,128)S(1)}, u32[]{:S(2)}, u32[]{:S(2)}) collective-permute-start(f32[384,128]{1,0:T(8,128)S(1)} %get-tuple-element.18), channel_id=1, source_target_pairs={{1,0},{2,1},{3,2},{4,3},{5,4},{6,5},{7,6},{8,7},{9,8},{10,9},{11,1... | collective-permute-start | bytes 589832 | tf_op jit(solution)/shard_map/ppermute | solution.py:16
  83.0 54.7 %collective-permute-done.2 = f32[384,128]{1,0:T(8,128)S(1)} collective-permute-done((f32[384,128]{1,0:T(8,128)S(1)}, f32[384,128]{1,0:T(8,128)S(1)}, u32[]{:S(2)}, u32[]{:S(2)}) %collective-permute-start.2) | collective-permute-done | bytes 196640 | tf_op jit(solution)/shard_map/ppermute | solution.py:16
  137.8 2.6 %broadcast_select_fusion.1 = (f32[2048,256]{1,0:T(8,128)S(1)}, f32[2048,256]{1,0:T(8,128)S(1)}) fusion(f32[2048,256]{1,0:T(8,128)S(1)} %copy-done, f32[2048,256]{1,0:T(8,128)} %collective-permute-done, pred[]{:T(512)S(6)} %eq.6, f32[2048,256]{1,0:T(8,128)} %collective-permute-done.1, pred[]{:T(512)S(6)} %eq.7), kind=kLoop, calls=%fused_computation.5 | loop fusion | flops 1048576 | bytes 10485762 | tf_op jit(solution)/shard_map/jit(_where)/select_n | solution.py:198
  140.4 1.3 copy-done.1
  141.7 0.7 copy-done.3
  142.4 4.3 %fusion.29.g_ref = f32[256,256]{1,0:T(8,128)} fusion(f32[2048,256]{1,0:T(8,128)S(1)} %get-tuple-element.9, f32[2048,256]{1,0:T(8,128)S(1)} %get-tuple-element.10), kind=kOutput, calls=%fused_computation.35 | convolution fusion | flops 1610612736 | bytes 4456448 | tf_op jit(solution)/shard_map/dot_general | solution.py:20
  146.7 17.0 %shard_map.19 = f32[256,256]{1,0:T(8,128)} custom-call(f32[256,256]{1,0:T(8,128)} %fusion.29.g_ref), custom_call_target="tpu_custom_call" | custom-call | tf_op jit(solution)/shard_map/pallas_call | solution.py:89
  163.8 1.3 fusion.7
  165.1 0.4 fusion.20
  165.6 0.7 maximum_maximum_fusion.a_ref
  166.3 30.3 %shard_map.20 = f32[256,256]{1,0:T(8,128)} custom-call(f32[256,256]{1,0:T(8,128)} %maximum_maximum_fusion.a_ref), custom_call_target="tpu_custom_call" | custom-call | tf_op jit(solution)/shard_map/pallas_call | solution.py:165
  196.6 1.3 fusion.9
  197.8 1.3 fusion.11
  199.1 6.4 %fusion = f32[2048,256]{1,0:T(8,128)} fusion(f32[2048,256]{1,0:T(8,128)} %copy-done.3, f32[2048,256]{1,0:T(8,128)S(1)} %copy-done.2, f32[256,256]{1,0:T(8,128)S(1)} %fusion.9, f32[256,256]{1,0:T(8,128)S(1)} %fusion.11), kind=kOutput, calls=%fused_computation | convolution fusion | flops 3222405120 | bytes 6815744 | tf_op jit(solution)/shard_map/dot_general | solution.py:179
  (16 shorter events, 0.2 us)
Async XLA Ops:
  0.0 26.1 %copy-start = (f32[2048,256]{1,0:T(8,128)S(1)}, f32[2048,256]{1,0:T(8,128)}, u32[]{:S(2)}) copy-start(f32[2048,256]{1,0:T(8,128)} %param.1) | copy-start | bytes 6291460
  26.1 111.7 %collective-permute-start = (f32[2048,256]{1,0:T(8,128)S(1)}, f32[2048,256]{1,0:T(8,128)}, u32[]{:S(2)}, u32[]{:S(2)}) collective-permute-start(f32[2048,256]{1,0:T(8,128)S(1)} %copy-done), channel_id=1, source_target_pairs={{0,1},{1,2},{2,3},{3,4},{4,5},{5,6},{6,7},{7,8},{8,9},{9,10},{10,1... | collective-permute-start | bytes 6291464 | tf_op jit(solution)/shard_map/ppermute | solution.py:16
  30.1 107.7 %collective-permute-start.1 = (f32[2048,256]{1,0:T(8,128)S(1)}, f32[2048,256]{1,0:T(8,128)}, u32[]{:S(2)}, u32[]{:S(2)}) collective-permute-start(f32[2048,256]{1,0:T(8,128)S(1)} %copy-done), channel_id=1, source_target_pairs={{1,0},{2,1},{3,2},{4,3},{5,4},{6,5},{7,6},{8,7},{9,8},{10,9},{11,1... | collective-permute-start | bytes 6291464 | tf_op jit(solution)/shard_map/ppermute | solution.py:16
  74.5 63.2 %collective-permute-start.2 = (f32[384,128]{1,0:T(8,128)S(1)}, f32[384,128]{1,0:T(8,128)S(1)}, u32[]{:S(2)}, u32[]{:S(2)}) collective-permute-start(f32[384,128]{1,0:T(8,128)S(1)} %get-tuple-element.17), channel_id=1, source_target_pairs={{0,1},{1,2},{2,3},{3,4},{4,5},{5,6},{6,7},{7,8},{8,9},{9,10},{10,1... | collective-permute-start | bytes 589832 | tf_op jit(solution)/shard_map/ppermute | solution.py:16
  76.4 61.3 %collective-permute-start.3 = (f32[384,128]{1,0:T(8,128)S(1)}, f32[384,128]{1,0:T(8,128)S(1)}, u32[]{:S(2)}, u32[]{:S(2)}) collective-permute-start(f32[384,128]{1,0:T(8,128)S(1)} %get-tuple-element.18), channel_id=1, source_target_pairs={{1,0},{2,1},{3,2},{4,3},{5,4},{6,5},{7,6},{8,7},{9,8},{10,9},{11,1... | collective-permute-start | bytes 589832 | tf_op jit(solution)/shard_map/ppermute | solution.py:16
  140.4 1.3 copy-start.1
  140.4 2.0 copy-start.3
  146.7 52.4 %copy-start.2 = (f32[2048,256]{1,0:T(8,128)S(1)}, f32[2048,256]{1,0:T(8,128)}, u32[]{:S(2)}) copy-start(f32[2048,256]{1,0:T(8,128)} %copy-done.1) | copy-start | bytes 6291460

commit v5 on v4

--- a/solution.py
+++ b/solution.py
@@ -82,7 +82,7 @@
         copy.wait_send()
 
 
-def allreduce_rows(g):
+def allreduce_rows(g, key):
     n = lax.axis_size("rows")
     rows, cols = g.shape
     chunk = rows // n
@@ -98,7 +98,7 @@
             pltpu.SemaphoreType.DMA((n,)),
             pltpu.SemaphoreType.DMA((n,)),
         ],
-        compiler_params=pltpu.CompilerParams(collective_id=0, has_side_effects=True),
+        compiler_params=pltpu.CompilerParams(collective_id=key, has_side_effects=True),
     )(g)
 
 
@@ -183,7 +183,7 @@
     return gram_of(left, right)
 
 
-def per_device(snapshots):
+def per_device(far, snapshots):
     local_rows = snapshots.shape[0]
     total = local_rows * lax.axis_size("rows")
     width = snapshots.shape[1] // 2
@@ -193,12 +193,18 @@
     last = index == count - 1
     pair = snapshots
 
-    gram = allreduce_rows(gram_of(pair, pair)) / total
+    gram = allreduce_rows(gram_of(pair, pair), 0) / total
     sent, gram = lax.optimization_barrier((pair, gram))
-    raw_a = jnp.where(first, pair, from_behind(sent, "pairs", 1))
-    raw_b = jnp.where(last, pair, from_behind(sent, "pairs", -1))
-
-    cross = allreduce_rows(gram_of(raw_a, raw_b)) / total
+    near_up = [(j, j + 1) for j in range(count - 1) if j not in far]
+    near_down = [(j + 1, j) for j in range(count - 1) if j not in far]
+    raw_a = jnp.where(first, pair, lax.ppermute(sent, "pairs", near_up))
+    raw_b = jnp.where(last, pair, lax.ppermute(sent, "pairs", near_down))
+    head = local_rows // 2
+    far_up = [(j, j + 1) for j in sorted(far)]
+    far_down = [(j + 1, j) for j in sorted(far)]
+    if far:
+        head_a = lax.ppermute(sent[:head], "pairs", far_up)
+        head_b = lax.ppermute(sent[:head], "pairs", far_down)
 
     whiten = whitener(gram)
     moment = tmm(whiten, mm(gram, whiten))
@@ -213,18 +219,43 @@
     x_a, m_a = side_a[:rows], side_a[rows:]
     x_b, m_b = side_b[:rows], side_b[rows:]
 
-    off = tmm(x_a, mm(cross, x_b))
+    top_next = mm(raw_a, x_a)
+    bottom_next = mm(raw_b, x_b)
+    if far:
+        far_a = jnp.asarray([j - 1 in far for j in range(count)])[index]
+        far_b = jnp.asarray([j in far for j in range(count)])[index]
+        half_a = jnp.where(first, whiten[:, width:], whiten[:, :width])
+        tail_a = lax.ppermute(mm(pair[head:], half_a), "pairs", far_up)
+        tail_b = lax.ppermute(mm(pair[head:], whiten[:, width:]), "pairs", far_down)
+        split_a = jnp.concatenate([mm(head_a, x_a), tail_a], axis=0)
+        split_b = jnp.concatenate([mm(head_b, x_b), tail_b], axis=0)
+        top_next = jnp.where(far_a, split_a, top_next)
+        bottom_next = jnp.where(far_b, split_b, bottom_next)
+
+    off = allreduce_rows(gram_of(top_next, bottom_next), 1) / total
     gram2 = jnp.concatenate(
         [jnp.concatenate([m_a, off], axis=1), jnp.concatenate([off.T, m_b], axis=1)], axis=0
     )
     whiten2 = whitener(gram2)
-    combined = jnp.concatenate([mm(x_a, whiten2[:width]), mm(x_b, whiten2[width:])], axis=0)
-    return mm(jnp.concatenate([raw_a, raw_b], axis=1), combined)
+    return mm(top_next, whiten2[:width]) + mm(bottom_next, whiten2[width:])
+
+
+def far_links(mesh):
+    far = set()
+    line = mesh.devices[0]
+    for j in range(len(line) - 1):
+        here, there = getattr(line[j], "coords", None), getattr(line[j + 1], "coords", None)
+        if here is None or there is None:
+            continue
+        gaps = [abs(p - q) for p, q in zip(here, there)]
+        if sum(gaps) > 1:
+            far.add(j)
+    return frozenset(far)
 
 
 def solution(mesh):
     return jax.shard_map(
-        per_device,
+        functools.partial(per_device, far_links(mesh)),
         mesh=mesh,
         in_specs=(P("rows", "pairs"),),
         out_specs=P("rows", "pairs"),

time: 206 us -> 207 us (level)
  waiting for transfers between devices: 54.7 us -> 23.6 us
  Pallas kernels: 95.4 us -> 109 us
  starting transfers between devices: 22.6 us -> 32.7 us
  matrix products: 24.3 us -> 32.2 us
    ppermute x4 -> x2, waiting for transfers between devices: 54.7 us -> 18.3 us  [from_behind(): lax.ppermute(value, axis, [(source, source + steps) for source in range(l...]
    ppermute x0 -> x6, starting transfers between devices: none -> 27.7 us  [the longest x1 13.3 us: per_device(): head_b = lax.ppermute(sent[:head], 'pairs', far_down)]
    ppermute x4 -> x2, starting transfers between devices: 22.6 us -> 5.08 us  [from_behind(): lax.ppermute(value, axis, [(source, source + steps) for source in range(l...]
    pallas_call x2, Pallas kernels: 34.9 us -> 48.3 us  [allreduce_rows(): pl.pallas_call(functools.partial(allreduce_kernel, n, chunk), out_shape=j...]
    dot_general x5 -> x9, matrix products: 11.7 us -> 21.9 us  [mm(): return jnp.dot(left, right, precision=lax.Precision.HIGHEST)]
    ppermute x0 -> x6, waiting for transfers between devices: none -> 5.32 us  [the longest x1 3.06 us: per_device(): tail_a = lax.ppermute(mm(pair[head:], half_a), 'pairs', far_up)]
    select_n x1 -> x0, other arithmetic: 2.64 us -> none  [per_device(): raw_a = jnp.where(first, pair, from_behind(sent, 'pairs', 1))]
    dot_general x4 -> x3, matrix products: 12.5 us -> 10.4 us  [gram_of(): lax.dot_general(left, right, (((0,), (0,)), ((), ())), precision=lax.Prec...]
  transfers between devices with their start and end apart: 4 -> 8, of which waited for: 1 -> 4; matrix products, arithmetic and copies ran while one was open for 2% -> 8% of each run, Pallas kernels for 15% -> 15%
where the time goes in v5:
time: 207 us; the launch traced here: 206 us
  Pallas kernels  109 us (53%)
  starting transfers between devices  32.7 us (16%)
  matrix products  32.2 us (16%)
  waiting for transfers between devices  23.6 us (11%)
  local copies, waits for them, and re-layouts  4.46 us (2%)
  other arithmetic  3.32 us (2%)
    pallas_call x2, Pallas kernels, lower_inverse(): pl.pallas_call(inverse_kernel, out_shape=jax.ShapeDtypeStruct((size, size...  60.7 us
    pallas_call x2, Pallas kernels, allreduce_rows(): pl.pallas_call(functools.partial(allreduce_kernel, n, chunk), out_shape=j...  48.3 us
    dot_general x9, matrix products, mm(): return jnp.dot(left, right, precision=lax.Precision.HIGHEST)  21.9 us
    ppermute x2, waiting for transfers between devices, from_behind(): lax.ppermute(value, axis, [(source, source + steps) for source in range(l...  18.3 us
    ppermute x1, starting transfers between devices, per_device(): head_b = lax.ppermute(sent[:head], 'pairs', far_down)  13.3 us
    dot_general x3, matrix products, gram_of(): lax.dot_general(left, right, (((0,), (0,)), ((), ())), precision=lax.Prec...  10.4 us
    ppermute x1, starting transfers between devices, per_device(): raw_a = jnp.where(first, pair, lax.ppermute(sent, 'pairs', near_up))  5.34 us
    ppermute x2, starting transfers between devices, from_behind(): lax.ppermute(value, axis, [(source, source + steps) for source in range(l...  5.08 us
  transfers between devices with their start and end apart: 8, of which 4 were waited for; matrix products, arithmetic and copies ran while one was open for 8% of the time, Pallas kernels for 15%

profile of v5, /device:TPU:57, one launch (start us, length us, event | category | flops | bytes accessed | tf_op | source)
XLA Modules:
  0.0 205.7 jit_solution(3663636453977108937)
XLA Ops:
  0.0 6.5 %fusion.32.g_ref = f32[256,256]{1,0:T(8,128)} fusion(f32[2048,256]{1,0:T(8,128)} %param.3), kind=kOutput, calls=%fused_computation.38 | convolution fusion | flops 1610612736 | bytes 2359296 | tf_op jit(solution)/shard_map/dot_general | solution.py:20
  6.5 17.9 %shard_map.37 = f32[256,256]{1,0:T(8,128)} custom-call(f32[256,256]{1,0:T(8,128)} %fusion.32.g_ref), custom_call_target="tpu_custom_call" | custom-call | tf_op jit(solution)/shard_map/pallas_call | solution.py:89
  24.4 1.7 broadcast_multiply_fusion.a_ref
  27.1 13.3 %collective-permute-start.4 = (f32[1024,256]{1,0:T(8,128)}, f32[1024,256]{1,0:T(8,128)}, u32[]{:S(2)}, u32[]{:S(2)}) collective-permute-start(f32[1024,256]{1,0:T(8,128)} %slice.41), channel_id=1, source_target_pairs={{8,7},{16,15},{24,23},{40,39},{48,47},{56,55},{72,71},{80,79},{88,... | collective-permute-start | bytes 3145736 | tf_op jit(solution)/shard_map/ppermute | solution.py:207
  43.1 5.3 %collective-permute-start.3 = (f32[2048,256]{1,0:T(8,128)S(1)}, f32[2048,256]{1,0:T(8,128)}, u32[]{:S(2)}, u32[]{:S(2)}) collective-permute-start(f32[2048,256]{1,0:T(8,128)S(1)} %copy-done), channel_id=1, source_target_pairs={{0,1},{1,2},{2,3},{3,4},{4,5},{5,6},{6,7},{8,9},{9,10},{10,11},{11... | collective-permute-start | bytes 6291464 | tf_op jit(solution)/shard_map/ppermute | solution.py:200
  48.4 30.3 %shard_map.38 = f32[256,256]{1,0:T(8,128)} custom-call(f32[256,256]{1,0:T(8,128)} %broadcast_multiply_fusion.a_ref), custom_call_target="tpu_custom_call" | custom-call | tf_op jit(solution)/shard_map/pallas_call | solution.py:165
  78.7 1.4 fusion.33
  82.5 1.9 collective-permute-start.1
  86.7 14.8 %collective-permute-done.1 = f32[384,128]{1,0:T(8,128)S(1)} collective-permute-done((f32[384,128]{1,0:T(8,128)S(1)}, f32[384,128]{1,0:T(8,128)S(1)}, u32[]{:S(2)}, u32[]{:S(2)}) %collective-permute-start.1) | collective-permute-done | bytes 196640 | tf_op jit(solution)/shard_map/ppermute | solution.py:16
  101.5 3.2 %collective-permute-start.5 = (f32[384,128]{1,0:T(8,128)S(1)}, f32[384,128]{1,0:T(8,128)S(1)}, u32[]{:S(2)}, u32[]{:S(2)}) collective-permute-start(f32[384,128]{1,0:T(8,128)S(1)} %get-tuple-element.16), channel_id=1, source_target_pairs={{1,0},{2,1},{3,2},{4,3},{5,4},{6,5},{7,6},{8,7},{9,8},{10,9},{11,1... | collective-permute-start | bytes 589832 | tf_op jit(solution)/shard_map/ppermute | solution.py:16
  105.6 3.6 %collective-permute-done.5 = f32[384,128]{1,0:T(8,128)S(1)} collective-permute-done((f32[384,128]{1,0:T(8,128)S(1)}, f32[384,128]{1,0:T(8,128)S(1)}, u32[]{:S(2)}, u32[]{:S(2)}) %collective-permute-start.5) | collective-permute-done | bytes 196640 | tf_op jit(solution)/shard_map/ppermute | solution.py:16
  109.2 5.0 %collective-permute-start.6 = (f32[1024,128]{1,0:T(8,128)S(1)}, f32[1024,128]{1,0:T(8,128)S(1)}, u32[]{:S(2)}, u32[]{:S(2)}) collective-permute-start(f32[1024,128]{1,0:T(8,128)S(1)} %convolution_bitcast_fusion), channel_id=1, source_target_pairs={{8,7},{16,15},{24,23},{40,39},{48,47},{56,55},{72,71},{80,79},{88,... | collective-permute-start | bytes 1572872 | tf_op jit(solution)/shard_map/ppermute | solution.py:229
  114.3 1.5 collective-permute-start.2
  115.7 2.2 %fusion.20 = f32[1024,128]{1,0:T(8,128)S(1)} fusion(f32[1024,256]{1,0:T(8,128)} %collective-permute-done.4, f32[384,128]{1,0:T(8,128)S(1)} %get-tuple-element.14), kind=kOutput, calls=%fused_computation.25 | convolution fusion | flops 402653184 | bytes 1703936 | tf_op jit(solution)/shard_map/dot_general | solution.py:179
  118.0 2.2 %fusion.23 = f32[1024,128]{1,0:T(8,128)S(1)} fusion(f32[1024,256]{1,0:T(8,128)} %collective-permute-done, f32[384,128]{1,0:T(8,128)S(1)} %get-tuple-element.13), kind=kOutput, calls=%fused_computation.28 | convolution fusion | flops 402653184 | bytes 1703936 | tf_op jit(solution)/shard_map/dot_general | solution.py:179
  120.2 2.2 %collective-permute-done.6 = f32[1024,128]{1,0:T(8,128)S(1)} collective-permute-done((f32[1024,128]{1,0:T(8,128)S(1)}, f32[1024,128]{1,0:T(8,128)S(1)}, u32[]{:S(2)}, u32[]{:S(2)}) %collective-permute-start.6) | collective-permute-done | bytes 524320 | tf_op jit(solution)/shard_map/ppermute | solution.py:229
  122.4 4.0 %maximum_select_fusion.1 = f32[2048,128]{1,0:T(8,128)S(1)} fusion(f32[1024,128]{1,0:T(8,128)S(1)} %collective-permute-done.6, f32[1024,128]{1,0:T(8,128)S(1)} %fusion.20, f32[2048,256]{1,0:T(8,128)S(1)} %copy-done, f32[2048,256]{1,0:T(8,128)} %collective-permute-done.7, pred[]{:T(512)S(6)} %eq.7, pred[]{:T(512)} %bitcast.3, f32[384,128]{1,0:T(8,128)S(1)} %get-tuple-element.14), kind=kOutput, calls=%fused_computation.8 | convolution fusion | flops 806354944 | bytes 6422530 | tf_op jit(solution)/shard_map/dot_general | solution.py:179
  126.5 3.1 %collective-permute-done.2 = f32[1024,128]{1,0:T(8,128)S(1)} collective-permute-done((f32[1024,128]{1,0:T(8,128)S(1)}, f32[1024,128]{1,0:T(8,128)S(1)}, u32[]{:S(2)}, u32[]{:S(2)}) %collective-permute-start.2) | collective-permute-done | bytes 524320 | tf_op jit(solution)/shard_map/ppermute | solution.py:228
  129.6 4.1 %maximum_select_fusion = f32[2048,128]{1,0:T(8,128)S(1)} fusion(f32[1024,128]{1,0:T(8,128)S(1)} %collective-permute-done.2, f32[1024,128]{1,0:T(8,128)S(1)} %fusion.23, f32[2048,256]{1,0:T(8,128)S(1)} %copy-done, f32[2048,256]{1,0:T(8,128)} %collective-permute-done.3, pred[]{:T(512)S(6)} %eq.6, pred[]{:T(512)} %bitcast, f32[384,128]{1,0:T(8,128)S(1)} %get-tuple-element.13), kind=kOutput, calls=%fused_computation.7 | convolution fusion | flops 806354944 | bytes 6422530 | tf_op jit(solution)/shard_map/dot_general | solution.py:179
  134.6 2.5 %fusion.35.g_ref = f32[128,128]{1,0:T(8,128)} fusion(f32[2048,128]{1,0:T(8,128)S(1)} %maximum_select_fusion, f32[2048,128]{1,0:T(8,128)S(1)} %maximum_select_fusion.1), kind=kOutput, calls=%fused_computation.41 | convolution fusion | flops 402653184 | bytes 2162688 | tf_op jit(solution)/shard_map/dot_general | solution.py:20
  137.1 30.5 %shard_map.39 = f32[128,128]{1,0:T(8,128)} custom-call(f32[128,128]{1,0:T(8,128)} %fusion.35.g_ref), custom_call_target="tpu_custom_call" | custom-call | tf_op jit(solution)/shard_map/pallas_call | solution.py:89
  169.3 30.5 %shard_map.40 = f32[256,256]{1,0:T(8,128)} custom-call(f32[256,256]{1,0:T(8,128)} %maximum_maximum_fusion.a_ref), custom_call_target="tpu_custom_call" | custom-call | tf_op jit(solution)/shard_map/pallas_call | solution.py:165
  199.7 2.8 %fusion.12 = f32[2048,256]{1,0:T(8,128)S(1)} fusion(f32[2048,128]{1,0:T(8,128)S(1)} %maximum_select_fusion.1, f32[256,256]{0,1:T(8,128)} %bitcast.25), kind=kOutput, calls=%fused_computation.16 | convolution fusion | flops 805306368 | bytes 3276800 | tf_op jit(solution)/shard_map/dot_general | solution.py:179
  202.5 3.2 %convolution_add_fusion = f32[2048,256]{1,0:T(8,128)} fusion(f32[2048,256]{1,0:T(8,128)S(1)} %fusion.12, f32[2048,128]{1,0:T(8,128)S(1)} %copy-done.2, f32[256,256]{0,1:T(8,128)S(1)} %bitcast.26), kind=kOutput, calls=%fused_computation | convolution fusion | flops 805830656 | bytes 5373952 | tf_op jit(solution)/shard_map/dot_general | solution.py:179
  (36 shorter events, 12.0 us)
Async XLA Ops:
  0.0 26.1 %copy-start = (f32[2048,256]{1,0:T(8,128)S(1)}, f32[2048,256]{1,0:T(8,128)}, u32[]{:S(2)}) copy-start(f32[2048,256]{1,0:T(8,128)} %param.3) | copy-start | bytes 6291460
  26.1 52.6 %copy-start.3 = (f32[256,256]{1,0:T(8,128)S(1)}, f32[256,256]{1,0:T(8,128)}, u32[]{:S(2)}) copy-start(f32[256,256]{1,0:T(8,128)} %broadcast_multiply_fusion.a_ref) | copy-start | bytes 786436
  27.1 57.3 %copy-start.6 = (pred[32]{0:T(512)(128)(4,1)S(1)}, pred[32]{0:T(512)(128)(4,1)}, u32[]{:S(2)}) copy-start(pred[32]{0:T(512)(128)(4,1)} %constant.20.clone) | copy-start | bytes 100
  27.1 58.0 %copy-start.5 = (pred[32]{0:T(512)(128)(4,1)S(1)}, pred[32]{0:T(512)(128)(4,1)}, u32[]{:S(2)}) copy-start(pred[32]{0:T(512)(128)(4,1)} %constant.19.clone) | copy-start | bytes 100
  27.1 87.1 %collective-permute-start.4 = (f32[1024,256]{1,0:T(8,128)}, f32[1024,256]{1,0:T(8,128)}, u32[]{:S(2)}, u32[]{:S(2)}) collective-permute-start(f32[1024,256]{1,0:T(8,128)} %slice.41), channel_id=1, source_target_pairs={{8,7},{16,15},{24,23},{40,39},{48,47},{56,55},{72,71},{80,79},{88,... | collective-permute-start | bytes 3145736 | tf_op jit(solution)/shard_map/ppermute | solution.py:207
  40.5 77.5 %collective-permute-start = (f32[1024,256]{1,0:T(8,128)}, f32[1024,256]{1,0:T(8,128)}, u32[]{:S(2)}, u32[]{:S(2)}) collective-permute-start(f32[1024,256]{1,0:T(8,128)} %slice.41), channel_id=1, source_target_pairs={{7,8},{15,16},{23,24},{39,40},{47,48},{55,56},{71,72},{79,80},{87,... | collective-permute-start | bytes 3145736 | tf_op jit(solution)/shard_map/ppermute | solution.py:206
  41.8 80.7 %collective-permute-start.7 = (f32[2048,256]{1,0:T(8,128)S(1)}, f32[2048,256]{1,0:T(8,128)}, u32[]{:S(2)}, u32[]{:S(2)}) collective-permute-start(f32[2048,256]{1,0:T(8,128)S(1)} %copy-done), channel_id=1, source_target_pairs={{1,0},{2,1},{3,2},{4,3},{5,4},{6,5},{7,6},{9,8},{10,9},{11,10},{12... | collective-permute-start | bytes 6291464 | tf_op jit(solution)/shard_map/ppermute | solution.py:201
  43.1 86.5 %collective-permute-start.3 = (f32[2048,256]{1,0:T(8,128)S(1)}, f32[2048,256]{1,0:T(8,128)}, u32[]{:S(2)}, u32[]{:S(2)}) collective-permute-start(f32[2048,256]{1,0:T(8,128)S(1)} %copy-done), channel_id=1, source_target_pairs={{0,1},{1,2},{2,3},{3,4},{4,5},{5,6},{6,7},{8,9},{9,10},{10,11},{11... | collective-permute-start | bytes 6291464 | tf_op jit(solution)/shard_map/ppermute | solution.py:200
  82.5 18.9 %collective-permute-start.1 = (f32[384,128]{1,0:T(8,128)S(1)}, f32[384,128]{1,0:T(8,128)S(1)}, u32[]{:S(2)}, u32[]{:S(2)}) collective-permute-start(f32[384,128]{1,0:T(8,128)S(1)} %get-tuple-element.15), channel_id=1, source_target_pairs={{0,1},{1,2},{2,3},{3,4},{4,5},{5,6},{6,7},{7,8},{8,9},{9,10},{10,1... | collective-permute-start | bytes 589832 | tf_op jit(solution)/shard_map/ppermute | solution.py:16
  101.5 7.8 %collective-permute-start.5 = (f32[384,128]{1,0:T(8,128)S(1)}, f32[384,128]{1,0:T(8,128)S(1)}, u32[]{:S(2)}, u32[]{:S(2)}) collective-permute-start(f32[384,128]{1,0:T(8,128)S(1)} %get-tuple-element.16), channel_id=1, source_target_pairs={{1,0},{2,1},{3,2},{4,3},{5,4},{6,5},{7,6},{8,7},{9,8},{10,9},{11,1... | collective-permute-start | bytes 589832 | tf_op jit(solution)/shard_map/ppermute | solution.py:16
  109.2 13.2 %collective-permute-start.6 = (f32[1024,128]{1,0:T(8,128)S(1)}, f32[1024,128]{1,0:T(8,128)S(1)}, u32[]{:S(2)}, u32[]{:S(2)}) collective-permute-start(f32[1024,128]{1,0:T(8,128)S(1)} %convolution_bitcast_fusion), channel_id=1, source_target_pairs={{8,7},{16,15},{24,23},{40,39},{48,47},{56,55},{72,71},{80,79},{88,... | collective-permute-start | bytes 1572872 | tf_op jit(solution)/shard_map/ppermute | solution.py:229
  114.3 15.3 %collective-permute-start.2 = (f32[1024,128]{1,0:T(8,128)S(1)}, f32[1024,128]{1,0:T(8,128)S(1)}, u32[]{:S(2)}, u32[]{:S(2)}) collective-permute-start(f32[1024,128]{1,0:T(8,128)S(1)} %convolution_bitcast_fusion.1), channel_id=1, source_target_pairs={{7,8},{15,16},{23,24},{39,40},{47,48},{55,56},{71,72},{79,80},{87,... | collective-permute-start | bytes 1572872 | tf_op jit(solution)/shard_map/ppermute | solution.py:228
  133.6 1.0 copy-start.1
  168.5 34.0 %copy-start.2 = (f32[2048,128]{1,0:T(8,128)S(1)}, f32[2048,128]{1,0:T(8,128)}, u32[]{:S(2)}) copy-start(f32[2048,128]{1,0:T(8,128)} %copy-done.1) | copy-start | bytes 3145732
  199.7 2.8 %copy-start.4 = (f32[256,256]{1,0:T(8,128)S(1)}, f32[256,256]{1,0:T(8,128)}, u32[]{:S(2)}) copy-start(f32[256,256]{1,0:T(8,128)} %shard_map.40) | copy-start | bytes 786436

commit v6 on v5

--- a/solution.py
+++ b/solution.py
@@ -211,11 +211,17 @@
     top = jnp.concatenate([whiten[:, :width], moment[:width, :width]], axis=0)
     bottom = jnp.concatenate([whiten[:, width:], moment[width:, width:]], axis=0)
     outgoing = jnp.where(first, bottom, top)
-    arrived_a = from_behind(outgoing, "pairs", 1)
-    arrived_b = from_behind(bottom, "pairs", -1)
-    side_a = jnp.where(first, top, arrived_a)
-    side_b = jnp.where(last, top, arrived_b)
     rows = whiten.shape[0]
+    if far:
+        up = jnp.concatenate([outgoing, mm(pair[head:], outgoing[:rows])], axis=0)
+        down = jnp.concatenate([bottom, mm(pair[head:], bottom[:rows])], axis=0)
+    else:
+        up, down = outgoing, bottom
+    arrived_a = from_behind(up, "pairs", 1)
+    arrived_b = from_behind(down, "pairs", -1)
+    info = top.shape[0]
+    side_a = jnp.where(first, top, arrived_a[:info])
+    side_b = jnp.where(last, top, arrived_b[:info])
     x_a, m_a = side_a[:rows], side_a[rows:]
     x_b, m_b = side_b[:rows], side_b[rows:]
 
@@ -224,11 +230,8 @@
     if far:
         far_a = jnp.asarray([j - 1 in far for j in range(count)])[index]
         far_b = jnp.asarray([j in far for j in range(count)])[index]
-        half_a = jnp.where(first, whiten[:, width:], whiten[:, :width])
-        tail_a = lax.ppermute(mm(pair[head:], half_a), "pairs", far_up)
-        tail_b = lax.ppermute(mm(pair[head:], whiten[:, width:]), "pairs", far_down)
-        split_a = jnp.concatenate([mm(head_a, x_a), tail_a], axis=0)
-        split_b = jnp.concatenate([mm(head_b, x_b), tail_b], axis=0)
+        split_a = jnp.concatenate([mm(head_a, x_a), arrived_a[info:]], axis=0)
+        split_b = jnp.concatenate([mm(head_b, x_b), arrived_b[info:]], axis=0)
         top_next = jnp.where(far_a, split_a, top_next)
         bottom_next = jnp.where(far_b, split_b, bottom_next)
 

time: 207 us -> 228 us (1.10)
  waiting for transfers between devices: 23.6 us -> 65.8 us
  Pallas kernels: 109 us -> 94.4 us
  starting transfers between devices: 32.7 us -> 23.4 us
    ppermute x2, waiting for transfers between devices: 18.3 us -> 43.7 us  [from_behind(): lax.ppermute(value, axis, [(source, source + steps) for source in range(l...]
    ppermute x1, waiting for transfers between devices: 0.01 us -> 22.1 us  [per_device(): head_a = lax.ppermute(sent[:head], 'pairs', far_up)]
    pallas_call x2, Pallas kernels: 48.3 us -> 33.7 us  [allreduce_rows(): pl.pallas_call(functools.partial(allreduce_kernel, n, chunk), out_shape=j...]
    ppermute x2 -> x0, starting transfers between devices: 6.42 us -> none  [the longest x1 4.95 us: per_device(): tail_b = lax.ppermute(mm(pair[head:], whiten[:, width:]), 'pairs', far_down)]
    ppermute x2 -> x0, waiting for transfers between devices: 5.31 us -> none  [the longest x1 3.06 us: per_device(): tail_a = lax.ppermute(mm(pair[head:], half_a), 'pairs', far_up)]
    ppermute x1, starting transfers between devices: 13.3 us -> 8.82 us  [per_device(): head_b = lax.ppermute(sent[:head], 'pairs', far_down)]
  transfers between devices with their start and end apart: 8 -> 6, of which waited for: 4 -> 2; matrix products, arithmetic and copies ran while one was open for 8% -> 9% of each run, Pallas kernels for 15% -> 13%
where the time goes in v6:
time: 228 us; the launch traced here: 227 us
  Pallas kernels  94.4 us (41%)
  waiting for transfers between devices  65.8 us (29%)
  matrix products  32.3 us (14%)
  starting transfers between devices  23.4 us (10%)
  local copies, waits for them, and re-layouts  5.51 us (2%)
  other arithmetic  5.19 us (2%)
    pallas_call x2, Pallas kernels, lower_inverse(): pl.pallas_call(inverse_kernel, out_shape=jax.ShapeDtypeStruct((size, size...  60.7 us
    ppermute x2, waiting for transfers between devices, from_behind(): lax.ppermute(value, axis, [(source, source + steps) for source in range(l...  43.7 us
    pallas_call x2, Pallas kernels, allreduce_rows(): pl.pallas_call(functools.partial(allreduce_kernel, n, chunk), out_shape=j...  33.7 us
    ppermute x1, waiting for transfers between devices, per_device(): head_a = lax.ppermute(sent[:head], 'pairs', far_up)  22.1 us
    dot_general x9, matrix products, mm(): return jnp.dot(left, right, precision=lax.Precision.HIGHEST)  21.9 us
    dot_general x3, matrix products, gram_of(): lax.dot_general(left, right, (((0,), (0,)), ((), ())), precision=lax.Prec...  10.4 us
    ppermute x1, starting transfers between devices, per_device(): head_b = lax.ppermute(sent[:head], 'pairs', far_down)  8.82 us
    ppermute x2, starting transfers between devices, from_behind(): lax.ppermute(value, axis, [(source, source + steps) for source in range(l...  6.54 us
  transfers between devices with their start and end apart: 6, of which 2 were waited for; matrix products, arithmetic and copies ran while one was open for 9% of the time, Pallas kernels for 13%

profile of v6, /device:TPU:57, one launch (start us, length us, event | category | flops | bytes accessed | tf_op | source)
XLA Modules:
  0.0 226.9 jit_solution(17490917553492281938)
XLA Ops:
  0.0 6.5 %fusion.26.g_ref = f32[256,256]{1,0:T(8,128)} fusion(f32[2048,256]{1,0:T(8,128)} %param.3), kind=kOutput, calls=%fused_computation.36 | convolution fusion | flops 1610612736 | bytes 2359296 | tf_op jit(solution)/shard_map/dot_general | solution.py:20
  6.5 17.9 %shard_map.37 = f32[256,256]{1,0:T(8,128)} custom-call(f32[256,256]{1,0:T(8,128)} %fusion.26.g_ref), custom_call_target="tpu_custom_call" | custom-call | tf_op jit(solution)/shard_map/pallas_call | solution.py:89
  24.4 1.7 broadcast_multiply_fusion.a_ref
  26.1 1.3 collective-permute-start.5
  27.4 30.3 %shard_map.38 = f32[256,256]{1,0:T(8,128)} custom-call(f32[256,256]{1,0:T(8,128)} %broadcast_multiply_fusion.a_ref), custom_call_target="tpu_custom_call" | custom-call | tf_op jit(solution)/shard_map/pallas_call | solution.py:165
  57.6 1.4 fusion.27
  59.1 1.1 copy.4
  60.2 1.3 fusion.28
  62.6 4.6 %collective-permute-start.1 = (f32[1408,128]{1,0:T(8,128)S(1)}, f32[1408,128]{1,0:T(8,128)S(1)}, u32[]{:S(2)}, u32[]{:S(2)}) collective-permute-start(f32[1408,128]{1,0:T(8,128)S(1)} %pad_maximum_fusion), channel_id=1, source_target_pairs={{0,1},{1,2},{2,3},{3,4},{4,5},{5,6},{6,7},{7,8},{8,9},{9,10},{10,1... | collective-permute-start | bytes 2162696 | tf_op jit(solution)/shard_map/ppermute | solution.py:16
  67.3 5.3 %collective-permute-start.2 = (f32[2048,256]{1,0:T(8,128)S(1)}, f32[2048,256]{1,0:T(8,128)}, u32[]{:S(2)}, u32[]{:S(2)}) collective-permute-start(f32[2048,256]{1,0:T(8,128)S(1)} %copy-done), channel_id=1, source_target_pairs={{0,1},{1,2},{2,3},{3,4},{4,5},{5,6},{6,7},{8,9},{9,10},{10,11},{11... | collective-permute-start | bytes 6291464 | tf_op jit(solution)/shard_map/ppermute | solution.py:200
  73.6 8.8 %collective-permute-start.3 = (f32[1024,256]{1,0:T(8,128)}, f32[1024,256]{1,0:T(8,128)}, u32[]{:S(2)}, u32[]{:S(2)}) collective-permute-start(f32[1024,256]{1,0:T(8,128)} %slice.53), channel_id=1, source_target_pairs={{8,7},{16,15},{24,23},{40,39},{48,47},{56,55},{72,71},{80,79},{88,... | collective-permute-start | bytes 3145736 | tf_op jit(solution)/shard_map/ppermute | solution.py:207
  84.4 1.9 collective-permute-start.4
  86.3 43.7 %collective-permute-done.1 = f32[1408,128]{1,0:T(8,128)S(1)} collective-permute-done((f32[1408,128]{1,0:T(8,128)S(1)}, f32[1408,128]{1,0:T(8,128)S(1)}, u32[]{:S(2)}, u32[]{:S(2)}) %collective-permute-start.1) | collective-permute-done | bytes 720928 | tf_op jit(solution)/shard_map/ppermute | solution.py:16
  130.0 1.5 collective-permute-start
  134.8 2.2 fusion.17
  137.0 22.1 %collective-permute-done = f32[1024,256]{1,0:T(8,128)} collective-permute-done((f32[1024,256]{1,0:T(8,128)}, f32[1024,256]{1,0:T(8,128)}, u32[]{:S(2)}, u32[]{:S(2)}) %collective-permute-start) | collective-permute-done | bytes 1048608 | tf_op jit(solution)/shard_map/ppermute | solution.py:206
  159.0 2.2 fusion.20
  161.3 4.1 %maximum_select_fusion.1 = f32[2048,128]{1,0:T(8,128)S(1)} fusion(f32[1024,128]{1,0:T(8,128)S(1)} %slice.81, f32[1024,128]{1,0:T(8,128)S(1)} %fusion.17, f32[2048,256]{1,0:T(8,128)S(1)} %copy-done, f32[2048,256]{1,0:T(8,128)} %collective-permute-done.5, pred[]{:T(512)S(6)} %eq.7, pred[]{:T(512)} %bitcast.3, f32[384,128]{1,0:T(8,128)S(1)} %get-tuple-element.14), kind=kOutput, calls=%fused_computation.8 | convolution fusion | flops 806354944 | bytes 6422530 | tf_op jit(solution)/shard_map/dot_general | solution.py:179
  165.4 4.0 %maximum_select_fusion = f32[2048,128]{1,0:T(8,128)S(1)} fusion(f32[1024,128]{1,0:T(8,128)S(1)} %slice-done, f32[1024,128]{1,0:T(8,128)S(1)} %fusion.20, f32[2048,256]{1,0:T(8,128)S(1)} %copy-done, f32[2048,256]{1,0:T(8,128)} %collective-permute-done.2, pred[]{:T(512)S(6)} %eq.6, pred[]{:T(512)} %bitcast, f32[384,128]{1,0:T(8,128)S(1)} %get-tuple-element.13), kind=kOutput, calls=%fused_computation.7 | convolution fusion | flops 806354944 | bytes 6422530 | tf_op jit(solution)/shard_map/dot_general | solution.py:179
  170.4 2.5 %fusion.29.g_ref = f32[128,128]{1,0:T(8,128)} fusion(f32[2048,128]{1,0:T(8,128)S(1)} %maximum_select_fusion, f32[2048,128]{1,0:T(8,128)S(1)} %maximum_select_fusion.1), kind=kOutput, calls=%fused_computation.39 | convolution fusion | flops 402653184 | bytes 2162688 | tf_op jit(solution)/shard_map/dot_general | solution.py:20
  172.9 15.9 %shard_map.39 = f32[128,128]{1,0:T(8,128)} custom-call(f32[128,128]{1,0:T(8,128)} %fusion.29.g_ref), custom_call_target="tpu_custom_call" | custom-call | tf_op jit(solution)/shard_map/pallas_call | solution.py:89
  190.5 30.5 %shard_map.40 = f32[256,256]{1,0:T(8,128)} custom-call(f32[256,256]{1,0:T(8,128)} %maximum_maximum_fusion.a_ref), custom_call_target="tpu_custom_call" | custom-call | tf_op jit(solution)/shard_map/pallas_call | solution.py:165
  220.9 2.8 %fusion.12 = f32[2048,256]{1,0:T(8,128)S(1)} fusion(f32[2048,128]{1,0:T(8,128)S(1)} %maximum_select_fusion.1, f32[256,256]{0,1:T(8,128)} %bitcast.24), kind=kOutput, calls=%fused_computation.20 | convolution fusion | flops 805306368 | bytes 3276800 | tf_op jit(solution)/shard_map/dot_general | solution.py:179
  223.8 3.2 %convolution_add_fusion = f32[2048,256]{1,0:T(8,128)} fusion(f32[2048,256]{1,0:T(8,128)S(1)} %fusion.12, f32[2048,128]{1,0:T(8,128)S(1)} %copy-done.2, f32[256,256]{0,1:T(8,128)S(1)} %bitcast.25), kind=kOutput, calls=%fused_computation | convolution fusion | flops 805830656 | bytes 5373952 | tf_op jit(solution)/shard_map/dot_general | solution.py:179
  (37 shorter events, 9.9 us)
Async XLA Ops:
  0.0 26.1 %copy-start = (f32[2048,256]{1,0:T(8,128)S(1)}, f32[2048,256]{1,0:T(8,128)}, u32[]{:S(2)}) copy-start(f32[2048,256]{1,0:T(8,128)} %param.3) | copy-start | bytes 6291460
  26.1 135.2 %collective-permute-start.5 = (f32[2048,256]{1,0:T(8,128)S(1)}, f32[2048,256]{1,0:T(8,128)}, u32[]{:S(2)}, u32[]{:S(2)}) collective-permute-start(f32[2048,256]{1,0:T(8,128)S(1)} %copy-done), channel_id=1, source_target_pairs={{1,0},{2,1},{3,2},{4,3},{5,4},{6,5},{7,6},{9,8},{10,9},{11,10},{12... | collective-permute-start | bytes 6291464 | tf_op jit(solution)/shard_map/ppermute | solution.py:201
  62.6 67.3 %collective-permute-start.1 = (f32[1408,128]{1,0:T(8,128)S(1)}, f32[1408,128]{1,0:T(8,128)S(1)}, u32[]{:S(2)}, u32[]{:S(2)}) collective-permute-start(f32[1408,128]{1,0:T(8,128)S(1)} %pad_maximum_fusion), channel_id=1, source_target_pairs={{0,1},{1,2},{2,3},{3,4},{4,5},{5,6},{6,7},{7,8},{8,9},{9,10},{10,1... | collective-permute-start | bytes 2162696 | tf_op jit(solution)/shard_map/ppermute | solution.py:16
  67.3 98.1 %collective-permute-start.2 = (f32[2048,256]{1,0:T(8,128)S(1)}, f32[2048,256]{1,0:T(8,128)}, u32[]{:S(2)}, u32[]{:S(2)}) collective-permute-start(f32[2048,256]{1,0:T(8,128)S(1)} %copy-done), channel_id=1, source_target_pairs={{0,1},{1,2},{2,3},{3,4},{4,5},{5,6},{6,7},{8,9},{9,10},{10,11},{11... | collective-permute-start | bytes 6291464 | tf_op jit(solution)/shard_map/ppermute | solution.py:200
  73.6 57.8 %copy-start.6 = (pred[32]{0:T(512)(128)(4,1)S(1)}, pred[32]{0:T(512)(128)(4,1)}, u32[]{:S(2)}) copy-start(pred[32]{0:T(512)(128)(4,1)} %constant.20.clone) | copy-start | bytes 100
  73.6 58.5 %copy-start.5 = (pred[32]{0:T(512)(128)(4,1)S(1)}, pred[32]{0:T(512)(128)(4,1)}, u32[]{:S(2)}) copy-start(pred[32]{0:T(512)(128)(4,1)} %constant.19.clone) | copy-start | bytes 100
  73.6 61.1 %collective-permute-start.3 = (f32[1024,256]{1,0:T(8,128)}, f32[1024,256]{1,0:T(8,128)}, u32[]{:S(2)}, u32[]{:S(2)}) collective-permute-start(f32[1024,256]{1,0:T(8,128)} %slice.53), channel_id=1, source_target_pairs={{8,7},{16,15},{24,23},{40,39},{48,47},{56,55},{72,71},{80,79},{88,... | collective-permute-start | bytes 3145736 | tf_op jit(solution)/shard_map/ppermute | solution.py:207
  84.4 48.3 %collective-permute-start.4 = (f32[1408,128]{1,0:T(8,128)}, f32[1408,128]{1,0:T(8,128)}, u32[]{:S(2)}, u32[]{:S(2)}) collective-permute-start(f32[1408,128]{1,0:T(8,128)} %pad_maximum_fusion.1), channel_id=1, source_target_pairs={{1,0},{2,1},{3,2},{4,3},{5,4},{6,5},{7,6},{8,7},{9,8},{10,9},{11,1... | collective-permute-start | bytes 2162696 | tf_op jit(solution)/shard_map/ppermute | solution.py:16
  130.0 7.0 %copy-start.3 = (f32[1408,128]{1,0:T(8,128)}, f32[1408,128]{1,0:T(8,128)S(1)}, u32[]{:S(2)}) copy-start(f32[1408,128]{1,0:T(8,128)S(1)} %collective-permute-done.1) | copy-start | bytes 2162692
  130.0 29.1 %collective-permute-start = (f32[1024,256]{1,0:T(8,128)}, f32[1024,256]{1,0:T(8,128)}, u32[]{:S(2)}, u32[]{:S(2)}) collective-permute-start(f32[1024,256]{1,0:T(8,128)} %slice.53), channel_id=1, source_target_pairs={{7,8},{15,16},{23,24},{39,40},{47,48},{55,56},{71,72},{79,80},{87,... | collective-permute-start | bytes 3145736 | tf_op jit(solution)/shard_map/ppermute | solution.py:206
  161.3 4.1 %slice-start = ((f32[1408,128]{1,0:T(8,128)}), f32[1024,128]{1,0:T(8,128)S(1)}, s32[]{:S(2)}) async-start(f32[1408,128]{1,0:T(8,128)} %copy-done.3), calls=%async_computation | async-start | bytes 1048576 | tf_op jit(solution)/shard_map/slice | solution.py:233
  169.4 1.0 copy-start.1
  189.7 34.0 %copy-start.2 = (f32[2048,128]{1,0:T(8,128)S(1)}, f32[2048,128]{1,0:T(8,128)}, u32[]{:S(2)}) copy-start(f32[2048,128]{1,0:T(8,128)} %copy-done.1) | copy-start | bytes 3145732
  220.9 2.8 %copy-start.4 = (f32[256,256]{1,0:T(8,128)S(1)}, f32[256,256]{1,0:T(8,128)}, u32[]{:S(2)}) copy-start(f32[256,256]{1,0:T(8,128)} %shard_map.40) | copy-start | bytes 786436

commit v7 on v4

--- a/solution.py
+++ b/solution.py
@@ -118,7 +118,7 @@
             k = top + t
             row = work[pl.ds(k, 1), low:high]
             pivot = jnp.sum(jnp.where(lane == k, row[:, here - low:here - low + lanes], 0.0), axis=1, keepdims=True)
-            scale = 1.0 / jnp.sqrt(pivot)
+            scale = lax.rsqrt(pivot)
             pivot_row = row * scale
             column = jnp.sum(jnp.where(lane == k, work[top:, here:here + lanes], 0.0), axis=1, keepdims=True)
             column = jnp.where(row_id > k, column * scale, 0.0)

time: 206 us -> 204 us (level)
  Pallas kernels: 95.4 us -> 91.9 us
    pallas_call x2, Pallas kernels: 60.5 us -> 57 us  [lower_inverse(): pl.pallas_call(inverse_kernel, out_shape=jax.ShapeDtypeStruct((size, size...]
  transfers between devices with their start and end apart: 4 -> 4, of which waited for: 1 -> 1; matrix products, arithmetic and copies ran while one was open for 2% -> 2% of each run, Pallas kernels for 15% -> 14%
where the time goes in v7:
time: 204 us
  Pallas kernels  91.9 us (45%)
  waiting for transfers between devices  56.5 us (28%)
  matrix products  24.2 us (12%)
  starting transfers between devices  22.6 us (11%)
  other arithmetic  5.08 us (2%)
  local copies, waits for them, and re-layouts  3.22 us (2%)
    pallas_call x2, Pallas kernels, lower_inverse(): pl.pallas_call(inverse_kernel, out_shape=jax.ShapeDtypeStruct((size, size...  57 us
    ppermute x4, waiting for transfers between devices, from_behind(): lax.ppermute(value, axis, [(source, source + steps) for source in range(l...  56.5 us
    pallas_call x2, Pallas kernels, allreduce_rows(): pl.pallas_call(functools.partial(allreduce_kernel, n, chunk), out_shape=j...  34.9 us
    ppermute x4, starting transfers between devices, from_behind(): lax.ppermute(value, axis, [(source, source + steps) for source in range(l...  22.6 us
    dot_general x4, matrix products, gram_of(): lax.dot_general(left, right, (((0,), (0,)), ((), ())), precision=lax.Prec...  12.5 us
    dot_general x5, matrix products, mm(): return jnp.dot(left, right, precision=lax.Precision.HIGHEST)  11.7 us
  transfers between devices with their start and end apart: 4, of which 1 were waited for; matrix products, arithmetic and copies ran while one was open for 2% of the time, Pallas kernels for 14%

profile of v7, /device:TPU:57, one launch (start us, length us, event | category | flops | bytes accessed | tf_op | source)
XLA Modules:
  0.0 203.8 jit_solution(11748528576020204456)
XLA Ops:
  0.0 6.5 %fusion.26.g_ref = f32[256,256]{1,0:T(8,128)} fusion(f32[2048,256]{1,0:T(8,128)} %param.1), kind=kOutput, calls=%fused_computation.32 | convolution fusion | flops 1610612736 | bytes 2359296 | tf_op jit(solution)/shard_map/dot_general | solution.py:20
  6.5 17.8 %shard_map.17 = f32[256,256]{1,0:T(8,128)} custom-call(f32[256,256]{1,0:T(8,128)} %fusion.26.g_ref), custom_call_target="tpu_custom_call" | custom-call | tf_op jit(solution)/shard_map/pallas_call | solution.py:89
  24.4 1.7 broadcast_multiply_fusion.a_ref
  26.1 4.0 %collective-permute-start = (f32[2048,256]{1,0:T(8,128)S(1)}, f32[2048,256]{1,0:T(8,128)}, u32[]{:S(2)}, u32[]{:S(2)}) collective-permute-start(f32[2048,256]{1,0:T(8,128)S(1)} %copy-done), channel_id=1, source_target_pairs={{0,1},{1,2},{2,3},{3,4},{4,5},{5,6},{6,7},{7,8},{8,9},{9,10},{10,1... | collective-permute-start | bytes 6291464 | tf_op jit(solution)/shard_map/ppermute | solution.py:16
  30.1 10.2 %collective-permute-start.1 = (f32[2048,256]{1,0:T(8,128)S(1)}, f32[2048,256]{1,0:T(8,128)}, u32[]{:S(2)}, u32[]{:S(2)}) collective-permute-start(f32[2048,256]{1,0:T(8,128)S(1)} %copy-done), channel_id=1, source_target_pairs={{1,0},{2,1},{3,2},{4,3},{5,4},{6,5},{7,6},{8,7},{9,8},{10,9},{11,1... | collective-permute-start | bytes 6291464 | tf_op jit(solution)/shard_map/ppermute | solution.py:16
  40.2 28.5 %shard_map.18 = f32[256,256]{1,0:T(8,128)} custom-call(f32[256,256]{1,0:T(8,128)} %broadcast_multiply_fusion.a_ref), custom_call_target="tpu_custom_call" | custom-call | tf_op jit(solution)/shard_map/pallas_call | solution.py:165
  68.8 1.1 copy.2
  69.8 1.4 fusion.27
  71.3 1.3 fusion.28
  72.7 1.9 collective-permute-start.2
  74.6 6.6 %collective-permute-start.3 = (f32[384,128]{1,0:T(8,128)S(1)}, f32[384,128]{1,0:T(8,128)S(1)}, u32[]{:S(2)}, u32[]{:S(2)}) collective-permute-start(f32[384,128]{1,0:T(8,128)S(1)} %get-tuple-element.18), channel_id=1, source_target_pairs={{1,0},{2,1},{3,2},{4,3},{5,4},{6,5},{7,6},{8,7},{9,8},{10,9},{11,1... | collective-permute-start | bytes 589832 | tf_op jit(solution)/shard_map/ppermute | solution.py:16
  81.2 56.5 %collective-permute-done.2 = f32[384,128]{1,0:T(8,128)S(1)} collective-permute-done((f32[384,128]{1,0:T(8,128)S(1)}, f32[384,128]{1,0:T(8,128)S(1)}, u32[]{:S(2)}, u32[]{:S(2)}) %collective-permute-start.2) | collective-permute-done | bytes 196640 | tf_op jit(solution)/shard_map/ppermute | solution.py:16
  137.8 2.6 %broadcast_select_fusion.1 = (f32[2048,256]{1,0:T(8,128)S(1)}, f32[2048,256]{1,0:T(8,128)S(1)}) fusion(f32[2048,256]{1,0:T(8,128)S(1)} %copy-done, f32[2048,256]{1,0:T(8,128)} %collective-permute-done, pred[]{:T(512)S(6)} %eq.6, f32[2048,256]{1,0:T(8,128)} %collective-permute-done.1, pred[]{:T(512)S(6)} %eq.7), kind=kLoop, calls=%fused_computation.5 | loop fusion | flops 1048576 | bytes 10485762 | tf_op jit(solution)/shard_map/jit(_where)/select_n | solution.py:198
  140.4 1.3 copy-done.1
  141.7 0.7 copy-done.3
  142.4 4.3 %fusion.29.g_ref = f32[256,256]{1,0:T(8,128)} fusion(f32[2048,256]{1,0:T(8,128)S(1)} %get-tuple-element.9, f32[2048,256]{1,0:T(8,128)S(1)} %get-tuple-element.10), kind=kOutput, calls=%fused_computation.35 | convolution fusion | flops 1610612736 | bytes 4456448 | tf_op jit(solution)/shard_map/dot_general | solution.py:20
  146.7 17.0 %shard_map.19 = f32[256,256]{1,0:T(8,128)} custom-call(f32[256,256]{1,0:T(8,128)} %fusion.29.g_ref), custom_call_target="tpu_custom_call" | custom-call | tf_op jit(solution)/shard_map/pallas_call | solution.py:89
  163.8 1.3 fusion.7
  165.1 0.4 fusion.20
  165.6 0.7 maximum_maximum_fusion.a_ref
  166.3 28.5 %shard_map.20 = f32[256,256]{1,0:T(8,128)} custom-call(f32[256,256]{1,0:T(8,128)} %maximum_maximum_fusion.a_ref), custom_call_target="tpu_custom_call" | custom-call | tf_op jit(solution)/shard_map/pallas_call | solution.py:165
  194.8 1.3 fusion.9
  196.1 1.3 fusion.11
  197.4 6.4 %fusion = f32[2048,256]{1,0:T(8,128)} fusion(f32[2048,256]{1,0:T(8,128)} %copy-done.3, f32[2048,256]{1,0:T(8,128)S(1)} %copy-done.2, f32[256,256]{1,0:T(8,128)S(1)} %fusion.9, f32[256,256]{1,0:T(8,128)S(1)} %fusion.11), kind=kOutput, calls=%fused_computation | convolution fusion | flops 3222405120 | bytes 6815744 | tf_op jit(solution)/shard_map/dot_general | solution.py:179
  (16 shorter events, 0.2 us)
Async XLA Ops:
  0.0 26.1 %copy-start = (f32[2048,256]{1,0:T(8,128)S(1)}, f32[2048,256]{1,0:T(8,128)}, u32[]{:S(2)}) copy-start(f32[2048,256]{1,0:T(8,128)} %param.1) | copy-start | bytes 6291460
  26.1 111.7 %collective-permute-start = (f32[2048,256]{1,0:T(8,128)S(1)}, f32[2048,256]{1,0:T(8,128)}, u32[]{:S(2)}, u32[]{:S(2)}) collective-permute-start(f32[2048,256]{1,0:T(8,128)S(1)} %copy-done), channel_id=1, source_target_pairs={{0,1},{1,2},{2,3},{3,4},{4,5},{5,6},{6,7},{7,8},{8,9},{9,10},{10,1... | collective-permute-start | bytes 6291464 | tf_op jit(solution)/shard_map/ppermute | solution.py:16
  30.1 107.7 %collective-permute-start.1 = (f32[2048,256]{1,0:T(8,128)S(1)}, f32[2048,256]{1,0:T(8,128)}, u32[]{:S(2)}, u32[]{:S(2)}) collective-permute-start(f32[2048,256]{1,0:T(8,128)S(1)} %copy-done), channel_id=1, source_target_pairs={{1,0},{2,1},{3,2},{4,3},{5,4},{6,5},{7,6},{8,7},{9,8},{10,9},{11,1... | collective-permute-start | bytes 6291464 | tf_op jit(solution)/shard_map/ppermute | solution.py:16
  72.7 65.0 %collective-permute-start.2 = (f32[384,128]{1,0:T(8,128)S(1)}, f32[384,128]{1,0:T(8,128)S(1)}, u32[]{:S(2)}, u32[]{:S(2)}) collective-permute-start(f32[384,128]{1,0:T(8,128)S(1)} %get-tuple-element.17), channel_id=1, source_target_pairs={{0,1},{1,2},{2,3},{3,4},{4,5},{5,6},{6,7},{7,8},{8,9},{9,10},{10,1... | collective-permute-start | bytes 589832 | tf_op jit(solution)/shard_map/ppermute | solution.py:16
  74.6 63.0 %collective-permute-start.3 = (f32[384,128]{1,0:T(8,128)S(1)}, f32[384,128]{1,0:T(8,128)S(1)}, u32[]{:S(2)}, u32[]{:S(2)}) collective-permute-start(f32[384,128]{1,0:T(8,128)S(1)} %get-tuple-element.18), channel_id=1, source_target_pairs={{1,0},{2,1},{3,2},{4,3},{5,4},{6,5},{7,6},{8,7},{9,8},{10,9},{11,1... | collective-permute-start | bytes 589832 | tf_op jit(solution)/shard_map/ppermute | solution.py:16
  140.4 1.3 copy-start.1
  140.4 2.0 copy-start.3
  146.7 50.7 %copy-start.2 = (f32[2048,256]{1,0:T(8,128)S(1)}, f32[2048,256]{1,0:T(8,128)}, u32[]{:S(2)}) copy-start(f32[2048,256]{1,0:T(8,128)} %copy-done.1) | copy-start | bytes 6291460

commit v8 on v7

--- a/solution.py
+++ b/solution.py
@@ -82,7 +82,7 @@
         copy.wait_send()
 
 
-def allreduce_rows(g):
+def allreduce_rows(g, key=0):
     n = lax.axis_size("rows")
     rows, cols = g.shape
     chunk = rows // n
@@ -98,7 +98,7 @@
             pltpu.SemaphoreType.DMA((n,)),
             pltpu.SemaphoreType.DMA((n,)),
         ],
-        compiler_params=pltpu.CompilerParams(collective_id=0, has_side_effects=True),
+        compiler_params=pltpu.CompilerParams(collective_id=key, has_side_effects=True),
     )(g)
 
 
@@ -198,7 +198,6 @@
     raw_a = jnp.where(first, pair, from_behind(sent, "pairs", 1))
     raw_b = jnp.where(last, pair, from_behind(sent, "pairs", -1))
 
-    cross = allreduce_rows(gram_of(raw_a, raw_b)) / total
 
     whiten = whitener(gram)
     moment = tmm(whiten, mm(gram, whiten))
@@ -213,7 +212,7 @@
     x_a, m_a = side_a[:rows], side_a[rows:]
     x_b, m_b = side_b[:rows], side_b[rows:]
 
-    off = tmm(x_a, mm(cross, x_b))
+    off = allreduce_rows(tmm(x_a, mm(gram_of(raw_a, raw_b), x_b)), 1) / total
     gram2 = jnp.concatenate(
         [jnp.concatenate([m_a, off], axis=1), jnp.concatenate([off.T, m_b], axis=1)], axis=0
     )

time: 204 us -> 199 us (0.975)
  Pallas kernels: 91.9 us -> 88.7 us
    pallas_call x2, Pallas kernels: 34.9 us -> 31.6 us  [allreduce_rows(): pl.pallas_call(functools.partial(allreduce_kernel, n, chunk), out_shape=j...]
where the time goes in v8:
time: 199 us; the launch traced here: 198 us
  Pallas kernels  88.7 us (45%)
  waiting for transfers between devices  56.5 us (28%)
  matrix products  23.2 us (12%)
  starting transfers between devices  22.6 us (11%)
  other arithmetic  5.94 us (3%)
    pallas_call x2, Pallas kernels, lower_inverse(): pl.pallas_call(inverse_kernel, out_shape=jax.ShapeDtypeStruct((size, size...  57 us
    ppermute x4, waiting for transfers between devices, from_behind(): lax.ppermute(value, axis, [(source, source + steps) for source in range(l...  56.5 us
    pallas_call x2, Pallas kernels, allreduce_rows(): pl.pallas_call(functools.partial(allreduce_kernel, n, chunk), out_shape=j...  31.6 us
    ppermute x4, starting transfers between devices, from_behind(): lax.ppermute(value, axis, [(source, source + steps) for source in range(l...  22.6 us
    dot_general x4, matrix products, gram_of(): lax.dot_general(left, right, (((0,), (0,)), ((), ())), precision=lax.Prec...  12.5 us
    dot_general x5, matrix products, mm(): return jnp.dot(left, right, precision=lax.Precision.HIGHEST)  10.7 us
  transfers between devices with their start and end apart: 4, of which 1 were waited for; matrix products, arithmetic and copies ran while one was open for 2% of the time, Pallas kernels for 14%

profile of v8, /device:TPU:57, one launch (start us, length us, event | category | flops | bytes accessed | tf_op | source)
XLA Modules:
  0.0 198.4 jit_solution(9230367031771025291)
XLA Ops:
  0.0 6.5 %fusion.24.g_ref = f32[256,256]{1,0:T(8,128)} fusion(f32[2048,256]{1,0:T(8,128)} %param.1), kind=kOutput, calls=%fused_computation.31 | convolution fusion | flops 1610612736 | bytes 2359296 | tf_op jit(solution)/shard_map/dot_general | solution.py:20
  6.5 17.8 %shard_map.17 = f32[256,256]{1,0:T(8,128)} custom-call(f32[256,256]{1,0:T(8,128)} %fusion.24.g_ref), custom_call_target="tpu_custom_call" | custom-call | tf_op jit(solution)/shard_map/pallas_call | solution.py:89
  24.4 1.7 broadcast_multiply_fusion.a_ref
  26.1 4.0 %collective-permute-start = (f32[2048,256]{1,0:T(8,128)S(1)}, f32[2048,256]{1,0:T(8,128)}, u32[]{:S(2)}, u32[]{:S(2)}) collective-permute-start(f32[2048,256]{1,0:T(8,128)S(1)} %copy-done), channel_id=1, source_target_pairs={{0,1},{1,2},{2,3},{3,4},{4,5},{5,6},{6,7},{7,8},{8,9},{9,10},{10,1... | collective-permute-start | bytes 6291464 | tf_op jit(solution)/shard_map/ppermute | solution.py:16
  30.1 10.2 %collective-permute-start.1 = (f32[2048,256]{1,0:T(8,128)S(1)}, f32[2048,256]{1,0:T(8,128)}, u32[]{:S(2)}, u32[]{:S(2)}) collective-permute-start(f32[2048,256]{1,0:T(8,128)S(1)} %copy-done), channel_id=1, source_target_pairs={{1,0},{2,1},{3,2},{4,3},{5,4},{6,5},{7,6},{8,7},{9,8},{10,9},{11,1... | collective-permute-start | bytes 6291464 | tf_op jit(solution)/shard_map/ppermute | solution.py:16
  40.2 28.5 %shard_map.18 = f32[256,256]{1,0:T(8,128)} custom-call(f32[256,256]{1,0:T(8,128)} %broadcast_multiply_fusion.a_ref), custom_call_target="tpu_custom_call" | custom-call | tf_op jit(solution)/shard_map/pallas_call | solution.py:165
  68.7 1.1 copy.2
  69.8 1.4 fusion.25
  71.3 1.3 fusion.26
  72.7 1.9 collective-permute-start.2
  74.6 6.6 %collective-permute-start.3 = (f32[384,128]{1,0:T(8,128)S(1)}, f32[384,128]{1,0:T(8,128)S(1)}, u32[]{:S(2)}, u32[]{:S(2)}) collective-permute-start(f32[384,128]{1,0:T(8,128)S(1)} %get-tuple-element.18), channel_id=1, source_target_pairs={{1,0},{2,1},{3,2},{4,3},{5,4},{6,5},{7,6},{8,7},{9,8},{10,9},{11,1... | collective-permute-start | bytes 589832 | tf_op jit(solution)/shard_map/ppermute | solution.py:16
  81.2 56.5 %collective-permute-done.2 = f32[384,128]{1,0:T(8,128)S(1)} collective-permute-done((f32[384,128]{1,0:T(8,128)S(1)}, f32[384,128]{1,0:T(8,128)S(1)}, u32[]{:S(2)}, u32[]{:S(2)}) %collective-permute-start.2) | collective-permute-done | bytes 196640 | tf_op jit(solution)/shard_map/ppermute | solution.py:16
  137.8 2.6 %broadcast_select_fusion.1 = (f32[2048,256]{1,0:T(8,128)S(1)}, f32[2048,256]{1,0:T(8,128)S(1)}) fusion(f32[2048,256]{1,0:T(8,128)S(1)} %copy-done, f32[2048,256]{1,0:T(8,128)} %collective-permute-done, pred[]{:T(512)S(6)} %eq.6, f32[2048,256]{1,0:T(8,128)} %collective-permute-done.1, pred[]{:T(512)S(6)} %eq.7), kind=kLoop, calls=%fused_computation.5 | loop fusion | flops 1048576 | bytes 10485762 | tf_op jit(solution)/shard_map/jit(_where)/select_n | solution.py:198
  140.4 3.6 %fusion.27 = f32[256,256]{1,0:T(8,128)S(1)} fusion(f32[2048,256]{1,0:T(8,128)S(1)} %get-tuple-element.9, f32[2048,256]{1,0:T(8,128)S(1)} %get-tuple-element.10), kind=kOutput, calls=%fused_computation.34 | convolution fusion | flops 1610612736 | bytes 4456448 | tf_op jit(solution)/shard_map/dot_general | solution.py:20
  144.1 0.4 fusion.15
  144.5 1.0 fusion.18.g_ref
  145.5 13.8 %shard_map.19 = f32[128,128]{1,0:T(8,128)} custom-call(f32[128,128]{1,0:T(8,128)} %fusion.18.g_ref), custom_call_target="tpu_custom_call" | custom-call | tf_op jit(solution)/shard_map/pallas_call | solution.py:89
  159.3 0.9 broadcast_multiply_fusion.1
  160.1 0.1 copy.3
  160.2 0.7 maximum_maximum_fusion.a_ref
  161.0 28.5 %shard_map.20 = f32[256,256]{1,0:T(8,128)} custom-call(f32[256,256]{1,0:T(8,128)} %maximum_maximum_fusion.a_ref), custom_call_target="tpu_custom_call" | custom-call | tf_op jit(solution)/shard_map/pallas_call | solution.py:165
  189.5 1.3 fusion.7
  190.7 1.3 fusion.9
  192.0 6.4 %fusion = f32[2048,256]{1,0:T(8,128)} fusion(f32[2048,256]{1,0:T(8,128)} %copy-done.3, f32[2048,256]{1,0:T(8,128)S(1)} %copy-done.2, f32[256,256]{1,0:T(8,128)S(1)} %fusion.7, f32[256,256]{1,0:T(8,128)S(1)} %fusion.9), kind=kOutput, calls=%fused_computation | convolution fusion | flops 3222405120 | bytes 6815744 | tf_op jit(solution)/shard_map/dot_general | solution.py:179
  (17 shorter events, 0.1 us)
Async XLA Ops:
  0.0 26.1 %copy-start = (f32[2048,256]{1,0:T(8,128)S(1)}, f32[2048,256]{1,0:T(8,128)}, u32[]{:S(2)}) copy-start(f32[2048,256]{1,0:T(8,128)} %param.1) | copy-start | bytes 6291460
  26.1 111.7 %collective-permute-start = (f32[2048,256]{1,0:T(8,128)S(1)}, f32[2048,256]{1,0:T(8,128)}, u32[]{:S(2)}, u32[]{:S(2)}) collective-permute-start(f32[2048,256]{1,0:T(8,128)S(1)} %copy-done), channel_id=1, source_target_pairs={{0,1},{1,2},{2,3},{3,4},{4,5},{5,6},{6,7},{7,8},{8,9},{9,10},{10,1... | collective-permute-start | bytes 6291464 | tf_op jit(solution)/shard_map/ppermute | solution.py:16
  30.1 107.7 %collective-permute-start.1 = (f32[2048,256]{1,0:T(8,128)S(1)}, f32[2048,256]{1,0:T(8,128)}, u32[]{:S(2)}, u32[]{:S(2)}) collective-permute-start(f32[2048,256]{1,0:T(8,128)S(1)} %copy-done), channel_id=1, source_target_pairs={{1,0},{2,1},{3,2},{4,3},{5,4},{6,5},{7,6},{8,7},{9,8},{10,9},{11,1... | collective-permute-start | bytes 6291464 | tf_op jit(solution)/shard_map/ppermute | solution.py:16
  72.7 65.0 %collective-permute-start.2 = (f32[384,128]{1,0:T(8,128)S(1)}, f32[384,128]{1,0:T(8,128)S(1)}, u32[]{:S(2)}, u32[]{:S(2)}) collective-permute-start(f32[384,128]{1,0:T(8,128)S(1)} %get-tuple-element.17), channel_id=1, source_target_pairs={{0,1},{1,2},{2,3},{3,4},{4,5},{5,6},{6,7},{7,8},{8,9},{9,10},{10,1... | collective-permute-start | bytes 589832 | tf_op jit(solution)/shard_map/ppermute | solution.py:16
  74.6 63.0 %collective-permute-start.3 = (f32[384,128]{1,0:T(8,128)S(1)}, f32[384,128]{1,0:T(8,128)S(1)}, u32[]{:S(2)}, u32[]{:S(2)}) collective-permute-start(f32[384,128]{1,0:T(8,128)S(1)} %get-tuple-element.18), channel_id=1, source_target_pairs={{1,0},{2,1},{3,2},{4,3},{5,4},{6,5},{7,6},{8,7},{9,8},{10,9},{11,1... | collective-permute-start | bytes 589832 | tf_op jit(solution)/shard_map/ppermute | solution.py:16
  140.4 3.6 %copy-start.1 = (f32[2048,256]{1,0:T(8,128)}, f32[2048,256]{1,0:T(8,128)S(1)}, u32[]{:S(2)}) copy-start(f32[2048,256]{1,0:T(8,128)S(1)} %get-tuple-element.9) | copy-start | bytes 6291460
  140.4 3.6 %copy-start.3 = (f32[2048,256]{1,0:T(8,128)}, f32[2048,256]{1,0:T(8,128)S(1)}, u32[]{:S(2)}) copy-start(f32[2048,256]{1,0:T(8,128)S(1)} %get-tuple-element.10) | copy-start | bytes 6291460
  144.4 47.6 %copy-start.2 = (f32[2048,256]{1,0:T(8,128)S(1)}, f32[2048,256]{1,0:T(8,128)}, u32[]{:S(2)}) copy-start(f32[2048,256]{1,0:T(8,128)} %copy-done.1) | copy-start | bytes 6291460

commit v9 on v8

--- a/solution.py
+++ b/solution.py
@@ -160,6 +160,58 @@
     o_ref[half:, half:] = inv22
 
 
+def head_kernel(a_ref, o_ref, work):
+    half = a_ref.shape[0]
+    rows_i = lax.broadcasted_iota(jnp.int32, (half, half), 0)
+    cols_i = lax.broadcasted_iota(jnp.int32, (half, half), 1)
+    work[:, :half] = a_ref[...]
+    work[:, half:] = jnp.where(rows_i == cols_i, 1.0, 0.0).astype(work.dtype)
+    eliminate(work, half)
+    o_ref[...] = work[:, half:]
+
+
+def tail_kernel(a21_ref, inv11_ref, a22_ref, o_ref, work):
+    half = a22_ref.shape[0]
+    rows_i = lax.broadcasted_iota(jnp.int32, (half, half), 0)
+    cols_i = lax.broadcasted_iota(jnp.int32, (half, half), 1)
+    hi = lax.Precision.HIGHEST
+    nt = (((1,), (1,)), ((), ()))
+    inv11 = inv11_ref[...]
+    low21 = lax.dot_general(a21_ref[...], inv11, nt, precision=hi, preferred_element_type=jnp.float32)
+    schur = a22_ref[...] - lax.dot_general(low21, low21, nt, precision=hi, preferred_element_type=jnp.float32)
+    work[:, :half] = schur
+    work[:, half:] = jnp.where(rows_i == cols_i, 1.0, 0.0).astype(work.dtype)
+    eliminate(work, half)
+    inv22 = work[:, half:]
+    mid = jnp.dot(inv22, low21, precision=hi, preferred_element_type=jnp.float32)
+    o_ref[:half, :half] = inv11
+    o_ref[:half, half:] = jnp.zeros((half, half), inv11.dtype)
+    o_ref[half:, :half] = -jnp.dot(mid, inv11, precision=hi, preferred_element_type=jnp.float32)
+    o_ref[half:, half:] = inv22
+
+
+def head_inverse(a11):
+    half = a11.shape[0]
+    return pl.pallas_call(
+        head_kernel,
+        out_shape=jax.ShapeDtypeStruct((half, half), a11.dtype),
+        in_specs=[pl.BlockSpec(memory_space=pltpu.VMEM)],
+        out_specs=pl.BlockSpec(memory_space=pltpu.VMEM),
+        scratch_shapes=[pltpu.VMEM((half, 2 * half), a11.dtype)],
+    )(a11)
+
+
+def tail_inverse(a21, inv11, a22):
+    half = a22.shape[0]
+    return pl.pallas_call(
+        tail_kernel,
+        out_shape=jax.ShapeDtypeStruct((2 * half, 2 * half), a22.dtype),
+        in_specs=[pl.BlockSpec(memory_space=pltpu.VMEM)] * 3,
+        out_specs=pl.BlockSpec(memory_space=pltpu.VMEM),
+        scratch_shapes=[pltpu.VMEM((half, 2 * half), a22.dtype)],
+    )(a21, inv11, a22)
+
+
 def lower_inverse(scaled):
     size = scaled.shape[0]
     return pl.pallas_call(
@@ -212,11 +264,11 @@
     x_a, m_a = side_a[:rows], side_a[rows:]
     x_b, m_b = side_b[:rows], side_b[rows:]
 
+    level = (jnp.trace(m_a) + jnp.trace(m_b)) / (2 * width)
+    shift = 0.1 * level * jnp.eye(width, dtype=m_a.dtype)
+    inv11 = head_inverse(m_a + shift)
     off = allreduce_rows(tmm(x_a, mm(gram_of(raw_a, raw_b), x_b)), 1) / total
-    gram2 = jnp.concatenate(
-        [jnp.concatenate([m_a, off], axis=1), jnp.concatenate([off.T, m_b], axis=1)], axis=0
-    )
-    whiten2 = whitener(gram2)
+    whiten2 = tail_inverse(off.T, inv11, m_b + shift).T
     combined = jnp.concatenate([mm(x_a, whiten2[:width]), mm(x_b, whiten2[width:])], axis=0)
     return mm(jnp.concatenate([raw_a, raw_b], axis=1), combined)
 

time: 199 us -> 203 us (1.020)
    pallas_call x0 -> x2, Pallas kernels: none -> 29.7 us  [the longest x1 15.5 us: tail_inverse(): pl.pallas_call(tail_kernel, out_shape=jax.ShapeDtypeStruct((2 * half, 2 *...]
    pallas_call x2 -> x1, Pallas kernels: 57 us -> 28.5 us  [lower_inverse(): pl.pallas_call(inverse_kernel, out_shape=jax.ShapeDtypeStruct((size, size...]
  transfers between devices with their start and end apart: 4 -> 4, of which waited for: 1 -> 1; matrix products, arithmetic and copies ran while one was open for 2% -> 3% of each run, Pallas kernels for 14% -> 21%
where the time goes in v9:
time: 203 us
  Pallas kernels  89.8 us (44%)
  waiting for transfers between devices  56.5 us (28%)
  matrix products  23.2 us (11%)
  starting transfers between devices  22.6 us (11%)
  other arithmetic  6.92 us (3%)
  local copies, waits for them, and re-layouts  2.05 us (1%)
    ppermute x4, waiting for transfers between devices, from_behind(): lax.ppermute(value, axis, [(source, source + steps) for source in range(l...  56.5 us
    pallas_call x2, Pallas kernels, allreduce_rows(): pl.pallas_call(functools.partial(allreduce_kernel, n, chunk), out_shape=j...  31.6 us
    pallas_call x1, Pallas kernels, lower_inverse(): pl.pallas_call(inverse_kernel, out_shape=jax.ShapeDtypeStruct((size, size...  28.5 us
    ppermute x4, starting transfers between devices, from_behind(): lax.ppermute(value, axis, [(source, source + steps) for source in range(l...  22.6 us
    pallas_call x1, Pallas kernels, tail_inverse(): pl.pallas_call(tail_kernel, out_shape=jax.ShapeDtypeStruct((2 * half, 2 *...  15.5 us
    pallas_call x1, Pallas kernels, head_inverse(): pl.pallas_call(head_kernel, out_shape=jax.ShapeDtypeStruct((half, half),...  14.2 us
    dot_general x4, matrix products, gram_of(): lax.dot_general(left, right, (((0,), (0,)), ((), ())), precision=lax.Prec...  12.5 us
    dot_general x5, matrix products, mm(): return jnp.dot(left, right, precision=lax.Precision.HIGHEST)  10.8 us
  transfers between devices with their start and end apart: 4, of which 1 were waited for; matrix products, arithmetic and copies ran while one was open for 3% of the time, Pallas kernels for 21%

profile of v9, /device:TPU:57, one launch (start us, length us, event | category | flops | bytes accessed | tf_op | source)
XLA Modules:
  0.0 202.6 jit_solution(11806960239395341791)
XLA Ops:
  0.0 6.5 %fusion.23.g_ref = f32[256,256]{1,0:T(8,128)} fusion(f32[2048,256]{1,0:T(8,128)} %param.1), kind=kOutput, calls=%fused_computation.34 | convolution fusion | flops 1610612736 | bytes 2359296 | tf_op jit(solution)/shard_map/dot_general | solution.py:20
  6.5 17.8 %shard_map.17 = f32[256,256]{1,0:T(8,128)} custom-call(f32[256,256]{1,0:T(8,128)} %fusion.23.g_ref), custom_call_target="tpu_custom_call" | custom-call | tf_op jit(solution)/shard_map/pallas_call | solution.py:89
  24.4 1.7 broadcast_multiply_fusion.a_ref
  26.1 4.0 %collective-permute-start = (f32[2048,256]{1,0:T(8,128)S(1)}, f32[2048,256]{1,0:T(8,128)}, u32[]{:S(2)}, u32[]{:S(2)}) collective-permute-start(f32[2048,256]{1,0:T(8,128)S(1)} %copy-done), channel_id=1, source_target_pairs={{0,1},{1,2},{2,3},{3,4},{4,5},{5,6},{6,7},{7,8},{8,9},{9,10},{10,1... | collective-permute-start | bytes 6291464 | tf_op jit(solution)/shard_map/ppermute | solution.py:16
  30.1 10.2 %collective-permute-start.1 = (f32[2048,256]{1,0:T(8,128)S(1)}, f32[2048,256]{1,0:T(8,128)}, u32[]{:S(2)}, u32[]{:S(2)}) collective-permute-start(f32[2048,256]{1,0:T(8,128)S(1)} %copy-done), channel_id=1, source_target_pairs={{1,0},{2,1},{3,2},{4,3},{5,4},{6,5},{7,6},{8,7},{9,8},{10,9},{11,1... | collective-permute-start | bytes 6291464 | tf_op jit(solution)/shard_map/ppermute | solution.py:16
  40.2 28.5 %shard_map.18 = f32[256,256]{1,0:T(8,128)} custom-call(f32[256,256]{1,0:T(8,128)} %broadcast_multiply_fusion.a_ref), custom_call_target="tpu_custom_call" | custom-call | tf_op jit(solution)/shard_map/pallas_call | solution.py:217
  68.7 1.1 copy.2
  69.8 1.4 fusion.24
  71.3 1.3 fusion.25
  72.7 1.9 collective-permute-start.2
  74.6 6.6 %collective-permute-start.3 = (f32[384,128]{1,0:T(8,128)S(1)}, f32[384,128]{1,0:T(8,128)S(1)}, u32[]{:S(2)}, u32[]{:S(2)}) collective-permute-start(f32[384,128]{1,0:T(8,128)S(1)} %get-tuple-element.18), channel_id=1, source_target_pairs={{1,0},{2,1},{3,2},{4,3},{5,4},{6,5},{7,6},{8,7},{9,8},{10,9},{11,1... | collective-permute-start | bytes 589832 | tf_op jit(solution)/shard_map/ppermute | solution.py:16
  81.2 56.5 %collective-permute-done.2 = f32[384,128]{1,0:T(8,128)S(1)} collective-permute-done((f32[384,128]{1,0:T(8,128)S(1)}, f32[384,128]{1,0:T(8,128)S(1)}, u32[]{:S(2)}, u32[]{:S(2)}) %collective-permute-start.2) | collective-permute-done | bytes 196640 | tf_op jit(solution)/shard_map/ppermute | solution.py:16
  140.2 0.7 select_add_fusion
  140.9 14.2 %shard_map.20.inv11_ref = f32[128,128]{1,0:T(8,128)} custom-call(f32[128,128]{1,0:T(8,128)} %get-tuple-element.20.a_ref), custom_call_target="tpu_custom_call" | custom-call | tf_op jit(solution)/shard_map/pallas_call | solution.py:195
  155.1 2.6 %broadcast_select_fusion.1 = (f32[2048,256]{1,0:T(8,128)S(1)}, f32[2048,256]{1,0:T(8,128)S(1)}) fusion(f32[2048,256]{1,0:T(8,128)S(1)} %copy-done, f32[2048,256]{1,0:T(8,128)} %collective-permute-done, pred[]{:T(512)S(6)} %eq.16, f32[2048,256]{1,0:T(8,128)} %collective-permute-done.1, pred[]{:T(512)S(6)} %eq.17), kind=kLoop, calls=%fused_computation.5 | loop fusion | flops 1048576 | bytes 10485762 | tf_op jit(solution)/shard_map/jit(_where)/select_n | solution.py:250
  157.8 3.6 %fusion.26 = f32[256,256]{1,0:T(8,128)S(1)} fusion(f32[2048,256]{1,0:T(8,128)S(1)} %get-tuple-element.9, f32[2048,256]{1,0:T(8,128)S(1)} %get-tuple-element.10), kind=kOutput, calls=%fused_computation.37 | convolution fusion | flops 1610612736 | bytes 4456448 | tf_op jit(solution)/shard_map/dot_general | solution.py:20
  161.8 1.0 fusion.18.g_ref
  162.8 13.8 %shard_map.19 = f32[128,128]{1,0:T(8,128)} custom-call(f32[128,128]{1,0:T(8,128)} %fusion.18.g_ref), custom_call_target="tpu_custom_call" | custom-call | tf_op jit(solution)/shard_map/pallas_call | solution.py:89
  176.6 0.9 copy.3
  177.6 0.6 multiply_bitcast_fusion.a21_ref
  178.2 15.5 %shard_map.21 = f32[256,256]{1,0:T(8,128)} custom-call(f32[128,128]{1,0:T(8,128)} %multiply_bitcast_fusion.a21_ref, f32[128,128]{1,0:T(8,128)} %shard_map.20.inv11_ref, f32[128,128]{1,0:T(8,128)} %get-tuple-element.19.a22_ref), custom_call_target="tpu_custom_call" | custom-call | tf_op jit(solution)/shard_map/pallas_call | solution.py:206
  193.7 1.3 fusion.7
  194.9 1.3 fusion.9
  196.2 6.4 %fusion = f32[2048,256]{1,0:T(8,128)} fusion(f32[2048,256]{1,0:T(8,128)} %copy-done.3, f32[2048,256]{1,0:T(8,128)S(1)} %copy-done.2, f32[256,256]{1,0:T(8,128)S(1)} %fusion.7, f32[256,256]{1,0:T(8,128)S(1)} %fusion.9), kind=kOutput, calls=%fused_computation | convolution fusion | flops 3222405120 | bytes 6815744 | tf_op jit(solution)/shard_map/dot_general | solution.py:231
  (18 shorter events, 1.7 us)
Async XLA Ops:
  0.0 26.1 %copy-start = (f32[2048,256]{1,0:T(8,128)S(1)}, f32[2048,256]{1,0:T(8,128)}, u32[]{:S(2)}) copy-start(f32[2048,256]{1,0:T(8,128)} %param.1) | copy-start | bytes 6291460
  26.1 129.0 %collective-permute-start = (f32[2048,256]{1,0:T(8,128)S(1)}, f32[2048,256]{1,0:T(8,128)}, u32[]{:S(2)}, u32[]{:S(2)}) collective-permute-start(f32[2048,256]{1,0:T(8,128)S(1)} %copy-done), channel_id=1, source_target_pairs={{0,1},{1,2},{2,3},{3,4},{4,5},{5,6},{6,7},{7,8},{8,9},{9,10},{10,1... | collective-permute-start | bytes 6291464 | tf_op jit(solution)/shard_map/ppermute | solution.py:16
  30.1 125.1 %collective-permute-start.1 = (f32[2048,256]{1,0:T(8,128)S(1)}, f32[2048,256]{1,0:T(8,128)}, u32[]{:S(2)}, u32[]{:S(2)}) collective-permute-start(f32[2048,256]{1,0:T(8,128)S(1)} %copy-done), channel_id=1, source_target_pairs={{1,0},{2,1},{3,2},{4,3},{5,4},{6,5},{7,6},{8,7},{9,8},{10,9},{11,1... | collective-permute-start | bytes 6291464 | tf_op jit(solution)/shard_map/ppermute | solution.py:16
  72.7 65.0 %collective-permute-start.2 = (f32[384,128]{1,0:T(8,128)S(1)}, f32[384,128]{1,0:T(8,128)S(1)}, u32[]{:S(2)}, u32[]{:S(2)}) collective-permute-start(f32[384,128]{1,0:T(8,128)S(1)} %get-tuple-element.17), channel_id=1, source_target_pairs={{0,1},{1,2},{2,3},{3,4},{4,5},{5,6},{6,7},{7,8},{8,9},{9,10},{10,1... | collective-permute-start | bytes 589832 | tf_op jit(solution)/shard_map/ppermute | solution.py:16
  74.6 63.0 %collective-permute-start.3 = (f32[384,128]{1,0:T(8,128)S(1)}, f32[384,128]{1,0:T(8,128)S(1)}, u32[]{:S(2)}, u32[]{:S(2)}) collective-permute-start(f32[384,128]{1,0:T(8,128)S(1)} %get-tuple-element.18), channel_id=1, source_target_pairs={{1,0},{2,1},{3,2},{4,3},{5,4},{6,5},{7,6},{8,7},{9,8},{10,9},{11,1... | collective-permute-start | bytes 589832 | tf_op jit(solution)/shard_map/ppermute | solution.py:16
  157.7 3.6 %copy-start.1 = (f32[2048,256]{1,0:T(8,128)}, f32[2048,256]{1,0:T(8,128)S(1)}, u32[]{:S(2)}) copy-start(f32[2048,256]{1,0:T(8,128)S(1)} %get-tuple-element.9) | copy-start | bytes 6291460
  157.8 3.6 %copy-start.3 = (f32[2048,256]{1,0:T(8,128)}, f32[2048,256]{1,0:T(8,128)S(1)}, u32[]{:S(2)}) copy-start(f32[2048,256]{1,0:T(8,128)S(1)} %get-tuple-element.10) | copy-start | bytes 6291460
  161.8 34.4 %copy-start.2 = (f32[2048,256]{1,0:T(8,128)S(1)}, f32[2048,256]{1,0:T(8,128)}, u32[]{:S(2)}) copy-start(f32[2048,256]{1,0:T(8,128)} %copy-done.1) | copy-start | bytes 6291460

commit v10 on v8

--- a/solution.py
+++ b/solution.py
@@ -195,7 +195,9 @@
 
     gram = allreduce_rows(gram_of(pair, pair)) / total
     sent, gram = lax.optimization_barrier((pair, gram))
-    raw_a = jnp.where(first, pair, from_behind(sent, "pairs", 1))
+    left = from_behind(sent[:, :width], "pairs", 1)
+    right = lax.ppermute(sent[:, width:], "pairs", [(0, 1)])
+    raw_a = jnp.where(first, pair, jnp.concatenate([left, right], axis=1))
     raw_b = jnp.where(last, pair, from_behind(sent, "pairs", -1))
 
 

time: 199 us -> 197 us (0.990)
  waiting for transfers between devices: 56.5 us -> 18.2 us
  Pallas kernels: 88.7 us -> 122 us
    ppermute x4, waiting for transfers between devices: 56.5 us -> 18.2 us  [from_behind(): lax.ppermute(value, axis, [(source, source + steps) for source in range(l...]
    pallas_call x2, Pallas kernels: 31.6 us -> 65 us  [allreduce_rows(): pl.pallas_call(functools.partial(allreduce_kernel, n, chunk), out_shape=j...]
  transfers between devices with their start and end apart: 4 -> 5, of which waited for: 1 -> 1; matrix products, arithmetic and copies ran while one was open for 2% -> 3% of each run, Pallas kernels for 14% -> 15%
where the time goes in v10:
time: 197 us
  Pallas kernels  122 us (62%)
  starting transfers between devices  24.4 us (12%)
  matrix products  23.1 us (12%)
  waiting for transfers between devices  18.2 us (9%)
  other arithmetic  5.93 us (3%)
  local copies, waits for them, and re-layouts  2.7 us (1%)
    pallas_call x2, Pallas kernels, allreduce_rows(): pl.pallas_call(functools.partial(allreduce_kernel, n, chunk), out_shape=j...  65 us
    pallas_call x2, Pallas kernels, lower_inverse(): pl.pallas_call(inverse_kernel, out_shape=jax.ShapeDtypeStruct((size, size...  57 us
    ppermute x4, starting transfers between devices, from_behind(): lax.ppermute(value, axis, [(source, source + steps) for source in range(l...  22.7 us
    ppermute x4, waiting for transfers between devices, from_behind(): lax.ppermute(value, axis, [(source, source + steps) for source in range(l...  18.2 us
    dot_general x4, matrix products, gram_of(): lax.dot_general(left, right, (((0,), (0,)), ((), ())), precision=lax.Prec...  12.5 us
    dot_general x5, matrix products, mm(): return jnp.dot(left, right, precision=lax.Precision.HIGHEST)  10.7 us
  transfers between devices with their start and end apart: 5, of which 1 were waited for; matrix products, arithmetic and copies ran while one was open for 3% of the time, Pallas kernels for 15%

profile of v10, /device:TPU:57, one launch (start us, length us, event | category | flops | bytes accessed | tf_op | source)
XLA Modules:
  0.0 196.7 jit_solution(11267856685983746090)
XLA Ops:
  0.0 6.5 %fusion.25.g_ref = f32[256,256]{1,0:T(8,128)} fusion(f32[2048,256]{1,0:T(8,128)} %param.1), kind=kOutput, calls=%fused_computation.32 | convolution fusion | flops 1610612736 | bytes 2359296 | tf_op jit(solution)/shard_map/dot_general | solution.py:20
  6.5 17.9 %shard_map.17 = f32[256,256]{1,0:T(8,128)} custom-call(f32[256,256]{1,0:T(8,128)} %fusion.25.g_ref), custom_call_target="tpu_custom_call" | custom-call | tf_op jit(solution)/shard_map/pallas_call | solution.py:89
  24.4 1.7 broadcast_multiply_fusion.a_ref
  26.1 12.4 %collective-permute-start.2 = (f32[2048,256]{1,0:T(8,128)S(1)}, f32[2048,256]{1,0:T(8,128)}, u32[]{:S(2)}, u32[]{:S(2)}) collective-permute-start(f32[2048,256]{1,0:T(8,128)S(1)} %copy-done), channel_id=1, source_target_pairs={{1,0},{2,1},{3,2},{4,3},{5,4},{6,5},{7,6},{8,7},{9,8},{10,9},{11,1... | collective-permute-start | bytes 6291464 | tf_op jit(solution)/shard_map/ppermute | solution.py:16
  38.5 1.5 fusion.22
  40.0 1.6 collective-permute-start.1
  41.6 1.9 collective-permute-start
  43.5 28.5 %shard_map.18 = f32[256,256]{1,0:T(8,128)} custom-call(f32[256,256]{1,0:T(8,128)} %broadcast_multiply_fusion.a_ref), custom_call_target="tpu_custom_call" | custom-call | tf_op jit(solution)/shard_map/pallas_call | solution.py:165
  72.0 1.4 fusion.26
  73.4 1.3 fusion.27
  74.7 1.1 copy.2
  75.9 1.9 collective-permute-start.3
  77.8 6.6 %collective-permute-start.4 = (f32[384,128]{1,0:T(8,128)S(1)}, f32[384,128]{1,0:T(8,128)S(1)}, u32[]{:S(2)}, u32[]{:S(2)}) collective-permute-start(f32[384,128]{1,0:T(8,128)S(1)} %get-tuple-element.20), channel_id=1, source_target_pairs={{1,0},{2,1},{3,2},{4,3},{5,4},{6,5},{7,6},{8,7},{9,8},{10,9},{11,1... | collective-permute-start | bytes 589832 | tf_op jit(solution)/shard_map/ppermute | solution.py:16
  84.4 18.2 %collective-permute-done.3 = f32[384,128]{1,0:T(8,128)S(1)} collective-permute-done((f32[384,128]{1,0:T(8,128)S(1)}, f32[384,128]{1,0:T(8,128)S(1)}, u32[]{:S(2)}, u32[]{:S(2)}) %collective-permute-start.3) | collective-permute-done | bytes 196640 | tf_op jit(solution)/shard_map/ppermute | solution.py:16
  102.7 2.6 %maximum_select_fusion = (f32[2048,256]{1,0:T(8,128)S(1)}, f32[2048,256]{1,0:T(8,128)S(1)}) fusion(f32[2048,256]{1,0:T(8,128)S(1)} %copy-done, f32[2048,128]{1,0:T(8,128)} %collective-permute-done.1, f32[2048,128]{1,0:T(8,128)} %collective-permute-done, pred[]{:T(512)S(6)} %eq.6, f32[2048,256]{1,0:T(8,128)} %collective-permute-done.2, pred[]{:T(512)S(6)} %eq.7), kind=kLoop, calls=%fused_computation.4 | loop fusion | flops 1572864 | bytes 10485762 | tf_op jit(solution)/shard_map/jit(_where)/select_n | solution.py:200
  105.3 3.6 %fusion.28 = f32[256,256]{1,0:T(8,128)S(1)} fusion(f32[2048,256]{1,0:T(8,128)S(1)} %get-tuple-element.9, f32[2048,256]{1,0:T(8,128)S(1)} %get-tuple-element.10), kind=kOutput, calls=%fused_computation.35 | convolution fusion | flops 1610612736 | bytes 4456448 | tf_op jit(solution)/shard_map/dot_general | solution.py:20
  109.3 1.0 fusion.18.g_ref
  110.3 47.1 %shard_map.19 = f32[128,128]{1,0:T(8,128)} custom-call(f32[128,128]{1,0:T(8,128)} %fusion.18.g_ref), custom_call_target="tpu_custom_call" | custom-call | tf_op jit(solution)/shard_map/pallas_call | solution.py:89
  157.5 0.9 broadcast_multiply_fusion.1
  158.4 0.7 maximum_maximum_fusion.a_ref
  159.2 28.5 %shard_map.20 = f32[256,256]{1,0:T(8,128)} custom-call(f32[256,256]{1,0:T(8,128)} %maximum_maximum_fusion.a_ref), custom_call_target="tpu_custom_call" | custom-call | tf_op jit(solution)/shard_map/pallas_call | solution.py:165
  187.7 1.3 fusion.7
  189.0 1.3 fusion.9
  190.3 6.4 %fusion = f32[2048,256]{1,0:T(8,128)} fusion(f32[2048,256]{1,0:T(8,128)} %copy-done.3, f32[2048,256]{1,0:T(8,128)S(1)} %copy-done.2, f32[256,256]{1,0:T(8,128)S(1)} %fusion.7, f32[256,256]{1,0:T(8,128)S(1)} %fusion.9), kind=kOutput, calls=%fused_computation | convolution fusion | flops 3222405120 | bytes 6815744 | tf_op jit(solution)/shard_map/dot_general | solution.py:179
  (22 shorter events, 0.6 us)
Async XLA Ops:
  0.0 26.1 %copy-start = (f32[2048,256]{1,0:T(8,128)S(1)}, f32[2048,256]{1,0:T(8,128)}, u32[]{:S(2)}) copy-start(f32[2048,256]{1,0:T(8,128)} %param.1) | copy-start | bytes 6291460
  26.1 45.9 %copy-start.4 = (f32[256,256]{1,0:T(8,128)S(1)}, f32[256,256]{1,0:T(8,128)}, u32[]{:S(2)}) copy-start(f32[256,256]{1,0:T(8,128)} %broadcast_multiply_fusion.a_ref) | copy-start | bytes 786436
  26.1 76.6 %collective-permute-start.2 = (f32[2048,256]{1,0:T(8,128)S(1)}, f32[2048,256]{1,0:T(8,128)}, u32[]{:S(2)}, u32[]{:S(2)}) collective-permute-start(f32[2048,256]{1,0:T(8,128)S(1)} %copy-done), channel_id=1, source_target_pairs={{1,0},{2,1},{3,2},{4,3},{5,4},{6,5},{7,6},{8,7},{9,8},{10,9},{11,1... | collective-permute-start | bytes 6291464 | tf_op jit(solution)/shard_map/ppermute | solution.py:16
  40.0 62.7 %collective-permute-start.1 = (f32[2048,128]{1,0:T(8,128)}, f32[2048,128]{1,0:T(8,128)}, u32[]{:S(2)}, u32[]{:S(2)}) collective-permute-start(f32[2048,128]{1,0:T(8,128)} %get-tuple-element.12), channel_id=1, source_target_pairs={{0,1},{32,33},{64,65},{96,97},{128,129},{160,161},{192,193},{224,2... | collective-permute-start | bytes 3145736 | tf_op jit(solution)/shard_map/ppermute | solution.py:199
  41.6 61.1 %collective-permute-start = (f32[2048,128]{1,0:T(8,128)}, f32[2048,128]{1,0:T(8,128)}, u32[]{:S(2)}, u32[]{:S(2)}) collective-permute-start(f32[2048,128]{1,0:T(8,128)} %get-tuple-element.11), channel_id=1, source_target_pairs={{0,1},{1,2},{2,3},{3,4},{4,5},{5,6},{6,7},{7,8},{8,9},{9,10},{10,1... | collective-permute-start | bytes 3145736 | tf_op jit(solution)/shard_map/ppermute | solution.py:16
  75.9 26.7 %collective-permute-start.3 = (f32[384,128]{1,0:T(8,128)S(1)}, f32[384,128]{1,0:T(8,128)S(1)}, u32[]{:S(2)}, u32[]{:S(2)}) collective-permute-start(f32[384,128]{1,0:T(8,128)S(1)} %get-tuple-element.19), channel_id=1, source_target_pairs={{0,1},{1,2},{2,3},{3,4},{4,5},{5,6},{6,7},{7,8},{8,9},{9,10},{10,1... | collective-permute-start | bytes 589832 | tf_op jit(solution)/shard_map/ppermute | solution.py:16
  77.8 24.8 %collective-permute-start.4 = (f32[384,128]{1,0:T(8,128)S(1)}, f32[384,128]{1,0:T(8,128)S(1)}, u32[]{:S(2)}, u32[]{:S(2)}) collective-permute-start(f32[384,128]{1,0:T(8,128)S(1)} %get-tuple-element.20), channel_id=1, source_target_pairs={{1,0},{2,1},{3,2},{4,3},{5,4},{6,5},{7,6},{8,7},{9,8},{10,9},{11,1... | collective-permute-start | bytes 589832 | tf_op jit(solution)/shard_map/ppermute | solution.py:16
  105.3 3.6 %copy-start.1 = (f32[2048,256]{1,0:T(8,128)}, f32[2048,256]{1,0:T(8,128)S(1)}, u32[]{:S(2)}) copy-start(f32[2048,256]{1,0:T(8,128)S(1)} %get-tuple-element.9) | copy-start | bytes 6291460
  105.3 3.6 %copy-start.3 = (f32[2048,256]{1,0:T(8,128)}, f32[2048,256]{1,0:T(8,128)S(1)}, u32[]{:S(2)}) copy-start(f32[2048,256]{1,0:T(8,128)S(1)} %get-tuple-element.10) | copy-start | bytes 6291460
  109.3 80.9 %copy-start.2 = (f32[2048,256]{1,0:T(8,128)S(1)}, f32[2048,256]{1,0:T(8,128)}, u32[]{:S(2)}) copy-start(f32[2048,256]{1,0:T(8,128)} %copy-done.1) | copy-start | bytes 6291460

commit v11 on v10

--- a/solution.py
+++ b/solution.py
@@ -126,7 +126,7 @@
             work[pl.ds(k, 1), low:high] = pivot_row
             return carry
 
-        lax.fori_loop(0, tile, step, 0)
+        lax.fori_loop(0, tile, step, 0, unroll=True)
 
 
 def inverse_kernel(a_ref, o_ref, work):

time: 197 us -> 196 us (level)
  Pallas kernels: 122 us -> 119 us
    pallas_call x2, Pallas kernels: 57 us -> 54.1 us  [lower_inverse(): pl.pallas_call(inverse_kernel, out_shape=jax.ShapeDtypeStruct((size, size...]
  transfers between devices with their start and end apart: 5 -> 5, of which waited for: 1 -> 1; matrix products, arithmetic and copies ran while one was open for 3% -> 3% of each run, Pallas kernels for 15% -> 14%
where the time goes in v11:
time: 196 us; the launch traced here: 195 us
  Pallas kernels  119 us (61%)
  starting transfers between devices  24.6 us (13%)
  matrix products  23.1 us (12%)
  waiting for transfers between devices  19.6 us (10%)
  other arithmetic  5.93 us (3%)
  local copies, waits for them, and re-layouts  2.7 us (1%)
    pallas_call x2, Pallas kernels, allreduce_rows(): pl.pallas_call(functools.partial(allreduce_kernel, n, chunk), out_shape=j...  65 us
    pallas_call x2, Pallas kernels, lower_inverse(): pl.pallas_call(inverse_kernel, out_shape=jax.ShapeDtypeStruct((size, size...  54.1 us
    ppermute x4, starting transfers between devices, from_behind(): lax.ppermute(value, axis, [(source, source + steps) for source in range(l...  23 us
    ppermute x4, waiting for transfers between devices, from_behind(): lax.ppermute(value, axis, [(source, source + steps) for source in range(l...  19.6 us
    dot_general x4, matrix products, gram_of(): lax.dot_general(left, right, (((0,), (0,)), ((), ())), precision=lax.Prec...  12.5 us
    dot_general x5, matrix products, mm(): return jnp.dot(left, right, precision=lax.Precision.HIGHEST)  10.7 us
  transfers between devices with their start and end apart: 5, of which 1 were waited for; matrix products, arithmetic and copies ran while one was open for 3% of the time, Pallas kernels for 14%

profile of v11, /device:TPU:57, one launch (start us, length us, event | category | flops | bytes accessed | tf_op | source)
XLA Modules:
  0.0 195.3 jit_solution(4329834904466753088)
XLA Ops:
  0.0 6.5 %fusion.25.g_ref = f32[256,256]{1,0:T(8,128)} fusion(f32[2048,256]{1,0:T(8,128)} %param.1), kind=kOutput, calls=%fused_computation.32 | convolution fusion | flops 1610612736 | bytes 2359296 | tf_op jit(solution)/shard_map/dot_general | solution.py:20
  6.5 17.9 %shard_map.17 = f32[256,256]{1,0:T(8,128)} custom-call(f32[256,256]{1,0:T(8,128)} %fusion.25.g_ref), custom_call_target="tpu_custom_call" | custom-call | tf_op jit(solution)/shard_map/pallas_call | solution.py:89
  24.4 1.7 broadcast_multiply_fusion.a_ref
  26.1 12.4 %collective-permute-start.2 = (f32[2048,256]{1,0:T(8,128)S(1)}, f32[2048,256]{1,0:T(8,128)}, u32[]{:S(2)}, u32[]{:S(2)}) collective-permute-start(f32[2048,256]{1,0:T(8,128)S(1)} %copy-done), channel_id=1, source_target_pairs={{1,0},{2,1},{3,2},{4,3},{5,4},{6,5},{7,6},{8,7},{9,8},{10,9},{11,1... | collective-permute-start | bytes 6291464 | tf_op jit(solution)/shard_map/ppermute | solution.py:16
  38.5 1.5 fusion.22
  40.0 1.6 collective-permute-start.1
  41.6 2.1 %collective-permute-start = (f32[2048,128]{1,0:T(8,128)}, f32[2048,128]{1,0:T(8,128)}, u32[]{:S(2)}, u32[]{:S(2)}) collective-permute-start(f32[2048,128]{1,0:T(8,128)} %get-tuple-element.11), channel_id=1, source_target_pairs={{0,1},{1,2},{2,3},{3,4},{4,5},{5,6},{6,7},{7,8},{8,9},{9,10},{10,1... | collective-permute-start | bytes 3145736 | tf_op jit(solution)/shard_map/ppermute | solution.py:16
  43.7 27.0 %shard_map.18 = f32[256,256]{1,0:T(8,128)} custom-call(f32[256,256]{1,0:T(8,128)} %broadcast_multiply_fusion.a_ref), custom_call_target="tpu_custom_call" | custom-call | tf_op jit(solution)/shard_map/pallas_call | solution.py:165
  70.6 1.4 fusion.26
  72.0 1.3 fusion.27
  73.3 1.1 copy.2
  74.5 1.9 collective-permute-start.3
  76.5 6.6 %collective-permute-start.4 = (f32[384,128]{1,0:T(8,128)S(1)}, f32[384,128]{1,0:T(8,128)S(1)}, u32[]{:S(2)}, u32[]{:S(2)}) collective-permute-start(f32[384,128]{1,0:T(8,128)S(1)} %get-tuple-element.20), channel_id=1, source_target_pairs={{1,0},{2,1},{3,2},{4,3},{5,4},{6,5},{7,6},{8,7},{9,8},{10,9},{11,1... | collective-permute-start | bytes 589832 | tf_op jit(solution)/shard_map/ppermute | solution.py:16
  83.1 19.6 %collective-permute-done.3 = f32[384,128]{1,0:T(8,128)S(1)} collective-permute-done((f32[384,128]{1,0:T(8,128)S(1)}, f32[384,128]{1,0:T(8,128)S(1)}, u32[]{:S(2)}, u32[]{:S(2)}) %collective-permute-start.3) | collective-permute-done | bytes 196640 | tf_op jit(solution)/shard_map/ppermute | solution.py:16
  102.7 2.6 %maximum_select_fusion = (f32[2048,256]{1,0:T(8,128)S(1)}, f32[2048,256]{1,0:T(8,128)S(1)}) fusion(f32[2048,256]{1,0:T(8,128)S(1)} %copy-done, f32[2048,128]{1,0:T(8,128)} %collective-permute-done.1, f32[2048,128]{1,0:T(8,128)} %collective-permute-done, pred[]{:T(512)S(6)} %eq.6, f32[2048,256]{1,0:T(8,128)} %collective-permute-done.2, pred[]{:T(512)S(6)} %eq.7), kind=kLoop, calls=%fused_computation.4 | loop fusion | flops 1572864 | bytes 10485762 | tf_op jit(solution)/shard_map/jit(_where)/select_n | solution.py:200
  105.3 3.6 %fusion.28 = f32[256,256]{1,0:T(8,128)S(1)} fusion(f32[2048,256]{1,0:T(8,128)S(1)} %get-tuple-element.9, f32[2048,256]{1,0:T(8,128)S(1)} %get-tuple-element.10), kind=kOutput, calls=%fused_computation.35 | convolution fusion | flops 1610612736 | bytes 4456448 | tf_op jit(solution)/shard_map/dot_general | solution.py:20
  109.3 1.0 fusion.18.g_ref
  110.3 47.1 %shard_map.19 = f32[128,128]{1,0:T(8,128)} custom-call(f32[128,128]{1,0:T(8,128)} %fusion.18.g_ref), custom_call_target="tpu_custom_call" | custom-call | tf_op jit(solution)/shard_map/pallas_call | solution.py:89
  157.5 0.9 broadcast_multiply_fusion.1
  158.4 0.7 maximum_maximum_fusion.a_ref
  159.2 27.2 %shard_map.20 = f32[256,256]{1,0:T(8,128)} custom-call(f32[256,256]{1,0:T(8,128)} %maximum_maximum_fusion.a_ref), custom_call_target="tpu_custom_call" | custom-call | tf_op jit(solution)/shard_map/pallas_call | solution.py:165
  186.3 1.3 fusion.7
  187.6 1.3 fusion.9
  188.9 6.4 %fusion = f32[2048,256]{1,0:T(8,128)} fusion(f32[2048,256]{1,0:T(8,128)} %copy-done.3, f32[2048,256]{1,0:T(8,128)S(1)} %copy-done.2, f32[256,256]{1,0:T(8,128)S(1)} %fusion.7, f32[256,256]{1,0:T(8,128)S(1)} %fusion.9), kind=kOutput, calls=%fused_computation | convolution fusion | flops 3222405120 | bytes 6815744 | tf_op jit(solution)/shard_map/dot_general | solution.py:179
  (22 shorter events, 0.6 us)
Async XLA Ops:
  0.0 26.1 %copy-start = (f32[2048,256]{1,0:T(8,128)S(1)}, f32[2048,256]{1,0:T(8,128)}, u32[]{:S(2)}) copy-start(f32[2048,256]{1,0:T(8,128)} %param.1) | copy-start | bytes 6291460
  26.1 44.5 %copy-start.4 = (f32[256,256]{1,0:T(8,128)S(1)}, f32[256,256]{1,0:T(8,128)}, u32[]{:S(2)}) copy-start(f32[256,256]{1,0:T(8,128)} %broadcast_multiply_fusion.a_ref) | copy-start | bytes 786436
  26.1 76.6 %collective-permute-start.2 = (f32[2048,256]{1,0:T(8,128)S(1)}, f32[2048,256]{1,0:T(8,128)}, u32[]{:S(2)}, u32[]{:S(2)}) collective-permute-start(f32[2048,256]{1,0:T(8,128)S(1)} %copy-done), channel_id=1, source_target_pairs={{1,0},{2,1},{3,2},{4,3},{5,4},{6,5},{7,6},{8,7},{9,8},{10,9},{11,1... | collective-permute-start | bytes 6291464 | tf_op jit(solution)/shard_map/ppermute | solution.py:16
  40.0 62.7 %collective-permute-start.1 = (f32[2048,128]{1,0:T(8,128)}, f32[2048,128]{1,0:T(8,128)}, u32[]{:S(2)}, u32[]{:S(2)}) collective-permute-start(f32[2048,128]{1,0:T(8,128)} %get-tuple-element.12), channel_id=1, source_target_pairs={{0,1},{32,33},{64,65},{96,97},{128,129},{160,161},{192,193},{224,2... | collective-permute-start | bytes 3145736 | tf_op jit(solution)/shard_map/ppermute | solution.py:199
  41.6 61.1 %collective-permute-start = (f32[2048,128]{1,0:T(8,128)}, f32[2048,128]{1,0:T(8,128)}, u32[]{:S(2)}, u32[]{:S(2)}) collective-permute-start(f32[2048,128]{1,0:T(8,128)} %get-tuple-element.11), channel_id=1, source_target_pairs={{0,1},{1,2},{2,3},{3,4},{4,5},{5,6},{6,7},{7,8},{8,9},{9,10},{10,1... | collective-permute-start | bytes 3145736 | tf_op jit(solution)/shard_map/ppermute | solution.py:16
  74.5 28.1 %collective-permute-start.3 = (f32[384,128]{1,0:T(8,128)S(1)}, f32[384,128]{1,0:T(8,128)S(1)}, u32[]{:S(2)}, u32[]{:S(2)}) collective-permute-start(f32[384,128]{1,0:T(8,128)S(1)} %get-tuple-element.19), channel_id=1, source_target_pairs={{0,1},{1,2},{2,3},{3,4},{4,5},{5,6},{6,7},{7,8},{8,9},{9,10},{10,1... | collective-permute-start | bytes 589832 | tf_op jit(solution)/shard_map/ppermute | solution.py:16
  76.5 26.2 %collective-permute-start.4 = (f32[384,128]{1,0:T(8,128)S(1)}, f32[384,128]{1,0:T(8,128)S(1)}, u32[]{:S(2)}, u32[]{:S(2)}) collective-permute-start(f32[384,128]{1,0:T(8,128)S(1)} %get-tuple-element.20), channel_id=1, source_target_pairs={{1,0},{2,1},{3,2},{4,3},{5,4},{6,5},{7,6},{8,7},{9,8},{10,9},{11,1... | collective-permute-start | bytes 589832 | tf_op jit(solution)/shard_map/ppermute | solution.py:16
  105.3 3.6 %copy-start.1 = (f32[2048,256]{1,0:T(8,128)}, f32[2048,256]{1,0:T(8,128)S(1)}, u32[]{:S(2)}) copy-start(f32[2048,256]{1,0:T(8,128)S(1)} %get-tuple-element.9) | copy-start | bytes 6291460
  105.3 3.6 %copy-start.3 = (f32[2048,256]{1,0:T(8,128)}, f32[2048,256]{1,0:T(8,128)S(1)}, u32[]{:S(2)}) copy-start(f32[2048,256]{1,0:T(8,128)S(1)} %get-tuple-element.10) | copy-start | bytes 6291460
  109.3 79.6 %copy-start.2 = (f32[2048,256]{1,0:T(8,128)S(1)}, f32[2048,256]{1,0:T(8,128)}, u32[]{:S(2)}) copy-start(f32[2048,256]{1,0:T(8,128)} %copy-done.1) | copy-start | bytes 6291460

commit v12 on v11

--- a/solution.py
+++ b/solution.py
@@ -51,8 +51,6 @@
         scatter[d - 1].wait_recv()
         total = total + recv[d]
     o_ref[pl.ds(mine, chunk), :] = total
-    for copy in scatter:
-        copy.wait_send()
 
     gather = []
     for d in range(1, n):
@@ -78,7 +76,7 @@
             device_id=(source, col),
             device_id_type=MESH,
         ).wait_recv()
-    for copy in gather:
+    for copy in scatter + gather:
         copy.wait_send()
 
 

time: 196 us -> 196 us (level)
  no operation moved by 1% of the time
where the time goes in v12:
time: 196 us; the launch traced here: 195 us
  Pallas kernels  119 us (61%)
  starting transfers between devices  24.6 us (13%)
  matrix products  23.1 us (12%)
  waiting for transfers between devices  19.6 us (10%)
  other arithmetic  5.93 us (3%)
  local copies, waits for them, and re-layouts  2.7 us (1%)
    pallas_call x2, Pallas kernels, allreduce_rows(): pl.pallas_call(functools.partial(allreduce_kernel, n, chunk), out_shape=j...  65 us
    pallas_call x2, Pallas kernels, lower_inverse(): pl.pallas_call(inverse_kernel, out_shape=jax.ShapeDtypeStruct((size, size...  54.1 us
    ppermute x4, starting transfers between devices, from_behind(): lax.ppermute(value, axis, [(source, source + steps) for source in range(l...  23 us
    ppermute x4, waiting for transfers between devices, from_behind(): lax.ppermute(value, axis, [(source, source + steps) for source in range(l...  19.6 us
    dot_general x4, matrix products, gram_of(): lax.dot_general(left, right, (((0,), (0,)), ((), ())), precision=lax.Prec...  12.5 us
    dot_general x5, matrix products, mm(): return jnp.dot(left, right, precision=lax.Precision.HIGHEST)  10.7 us
  transfers between devices with their start and end apart: 5, of which 1 were waited for; matrix products, arithmetic and copies ran while one was open for 3% of the time, Pallas kernels for 14%

profile of v12, /device:TPU:57, one launch (start us, length us, event | category | flops | bytes accessed | tf_op | source)
XLA Modules:
  0.0 195.3 jit_solution(13468689922088611369)
XLA Ops:
  0.0 6.5 %fusion.25.g_ref = f32[256,256]{1,0:T(8,128)} fusion(f32[2048,256]{1,0:T(8,128)} %param.1), kind=kOutput, calls=%fused_computation.32 | convolution fusion | flops 1610612736 | bytes 2359296 | tf_op jit(solution)/shard_map/dot_general | solution.py:20
  6.5 17.9 %shard_map.17 = f32[256,256]{1,0:T(8,128)} custom-call(f32[256,256]{1,0:T(8,128)} %fusion.25.g_ref), custom_call_target="tpu_custom_call" | custom-call | tf_op jit(solution)/shard_map/pallas_call | solution.py:87
  24.4 1.7 broadcast_multiply_fusion.a_ref
  26.1 12.4 %collective-permute-start.2 = (f32[2048,256]{1,0:T(8,128)S(1)}, f32[2048,256]{1,0:T(8,128)}, u32[]{:S(2)}, u32[]{:S(2)}) collective-permute-start(f32[2048,256]{1,0:T(8,128)S(1)} %copy-done), channel_id=1, source_target_pairs={{1,0},{2,1},{3,2},{4,3},{5,4},{6,5},{7,6},{8,7},{9,8},{10,9},{11,1... | collective-permute-start | bytes 6291464 | tf_op jit(solution)/shard_map/ppermute | solution.py:16
  38.5 1.5 fusion.22
  40.0 1.6 collective-permute-start.1
  41.6 2.1 %collective-permute-start = (f32[2048,128]{1,0:T(8,128)}, f32[2048,128]{1,0:T(8,128)}, u32[]{:S(2)}, u32[]{:S(2)}) collective-permute-start(f32[2048,128]{1,0:T(8,128)} %get-tuple-element.11), channel_id=1, source_target_pairs={{0,1},{1,2},{2,3},{3,4},{4,5},{5,6},{6,7},{7,8},{8,9},{9,10},{10,1... | collective-permute-start | bytes 3145736 | tf_op jit(solution)/shard_map/ppermute | solution.py:16
  43.7 27.0 %shard_map.18 = f32[256,256]{1,0:T(8,128)} custom-call(f32[256,256]{1,0:T(8,128)} %broadcast_multiply_fusion.a_ref), custom_call_target="tpu_custom_call" | custom-call | tf_op jit(solution)/shard_map/pallas_call | solution.py:163
  70.6 1.4 fusion.26
  72.0 1.3 fusion.27
  73.3 1.1 copy.2
  74.5 1.9 collective-permute-start.3
  76.5 6.6 %collective-permute-start.4 = (f32[384,128]{1,0:T(8,128)S(1)}, f32[384,128]{1,0:T(8,128)S(1)}, u32[]{:S(2)}, u32[]{:S(2)}) collective-permute-start(f32[384,128]{1,0:T(8,128)S(1)} %get-tuple-element.20), channel_id=1, source_target_pairs={{1,0},{2,1},{3,2},{4,3},{5,4},{6,5},{7,6},{8,7},{9,8},{10,9},{11,1... | collective-permute-start | bytes 589832 | tf_op jit(solution)/shard_map/ppermute | solution.py:16
  83.1 19.6 %collective-permute-done.3 = f32[384,128]{1,0:T(8,128)S(1)} collective-permute-done((f32[384,128]{1,0:T(8,128)S(1)}, f32[384,128]{1,0:T(8,128)S(1)}, u32[]{:S(2)}, u32[]{:S(2)}) %collective-permute-start.3) | collective-permute-done | bytes 196640 | tf_op jit(solution)/shard_map/ppermute | solution.py:16
  102.7 2.6 %maximum_select_fusion = (f32[2048,256]{1,0:T(8,128)S(1)}, f32[2048,256]{1,0:T(8,128)S(1)}) fusion(f32[2048,256]{1,0:T(8,128)S(1)} %copy-done, f32[2048,128]{1,0:T(8,128)} %collective-permute-done.1, f32[2048,128]{1,0:T(8,128)} %collective-permute-done, pred[]{:T(512)S(6)} %eq.6, f32[2048,256]{1,0:T(8,128)} %collective-permute-done.2, pred[]{:T(512)S(6)} %eq.7), kind=kLoop, calls=%fused_computation.4 | loop fusion | flops 1572864 | bytes 10485762 | tf_op jit(solution)/shard_map/jit(_where)/select_n | solution.py:198
  105.3 3.6 %fusion.28 = f32[256,256]{1,0:T(8,128)S(1)} fusion(f32[2048,256]{1,0:T(8,128)S(1)} %get-tuple-element.9, f32[2048,256]{1,0:T(8,128)S(1)} %get-tuple-element.10), kind=kOutput, calls=%fused_computation.35 | convolution fusion | flops 1610612736 | bytes 4456448 | tf_op jit(solution)/shard_map/dot_general | solution.py:20
  109.3 1.0 fusion.18.g_ref
  110.3 47.1 %shard_map.19 = f32[128,128]{1,0:T(8,128)} custom-call(f32[128,128]{1,0:T(8,128)} %fusion.18.g_ref), custom_call_target="tpu_custom_call" | custom-call | tf_op jit(solution)/shard_map/pallas_call | solution.py:87
  157.5 0.9 broadcast_multiply_fusion.1
  158.4 0.7 maximum_maximum_fusion.a_ref
  159.2 27.2 %shard_map.20 = f32[256,256]{1,0:T(8,128)} custom-call(f32[256,256]{1,0:T(8,128)} %maximum_maximum_fusion.a_ref), custom_call_target="tpu_custom_call" | custom-call | tf_op jit(solution)/shard_map/pallas_call | solution.py:163
  186.3 1.3 fusion.7
  187.6 1.3 fusion.9
  188.9 6.4 %fusion = f32[2048,256]{1,0:T(8,128)} fusion(f32[2048,256]{1,0:T(8,128)} %copy-done.3, f32[2048,256]{1,0:T(8,128)S(1)} %copy-done.2, f32[256,256]{1,0:T(8,128)S(1)} %fusion.7, f32[256,256]{1,0:T(8,128)S(1)} %fusion.9), kind=kOutput, calls=%fused_computation | convolution fusion | flops 3222405120 | bytes 6815744 | tf_op jit(solution)/shard_map/dot_general | solution.py:177
  (22 shorter events, 0.6 us)
Async XLA Ops:
  0.0 26.1 %copy-start = (f32[2048,256]{1,0:T(8,128)S(1)}, f32[2048,256]{1,0:T(8,128)}, u32[]{:S(2)}) copy-start(f32[2048,256]{1,0:T(8,128)} %param.1) | copy-start | bytes 6291460
  26.1 44.5 %copy-start.4 = (f32[256,256]{1,0:T(8,128)S(1)}, f32[256,256]{1,0:T(8,128)}, u32[]{:S(2)}) copy-start(f32[256,256]{1,0:T(8,128)} %broadcast_multiply_fusion.a_ref) | copy-start | bytes 786436
  26.1 76.6 %collective-permute-start.2 = (f32[2048,256]{1,0:T(8,128)S(1)}, f32[2048,256]{1,0:T(8,128)}, u32[]{:S(2)}, u32[]{:S(2)}) collective-permute-start(f32[2048,256]{1,0:T(8,128)S(1)} %copy-done), channel_id=1, source_target_pairs={{1,0},{2,1},{3,2},{4,3},{5,4},{6,5},{7,6},{8,7},{9,8},{10,9},{11,1... | collective-permute-start | bytes 6291464 | tf_op jit(solution)/shard_map/ppermute | solution.py:16
  40.0 62.7 %collective-permute-start.1 = (f32[2048,128]{1,0:T(8,128)}, f32[2048,128]{1,0:T(8,128)}, u32[]{:S(2)}, u32[]{:S(2)}) collective-permute-start(f32[2048,128]{1,0:T(8,128)} %get-tuple-element.12), channel_id=1, source_target_pairs={{0,1},{32,33},{64,65},{96,97},{128,129},{160,161},{192,193},{224,2... | collective-permute-start | bytes 3145736 | tf_op jit(solution)/shard_map/ppermute | solution.py:197
  41.6 61.1 %collective-permute-start = (f32[2048,128]{1,0:T(8,128)}, f32[2048,128]{1,0:T(8,128)}, u32[]{:S(2)}, u32[]{:S(2)}) collective-permute-start(f32[2048,128]{1,0:T(8,128)} %get-tuple-element.11), channel_id=1, source_target_pairs={{0,1},{1,2},{2,3},{3,4},{4,5},{5,6},{6,7},{7,8},{8,9},{9,10},{10,1... | collective-permute-start | bytes 3145736 | tf_op jit(solution)/shard_map/ppermute | solution.py:16
  74.5 28.1 %collective-permute-start.3 = (f32[384,128]{1,0:T(8,128)S(1)}, f32[384,128]{1,0:T(8,128)S(1)}, u32[]{:S(2)}, u32[]{:S(2)}) collective-permute-start(f32[384,128]{1,0:T(8,128)S(1)} %get-tuple-element.19), channel_id=1, source_target_pairs={{0,1},{1,2},{2,3},{3,4},{4,5},{5,6},{6,7},{7,8},{8,9},{9,10},{10,1... | collective-permute-start | bytes 589832 | tf_op jit(solution)/shard_map/ppermute | solution.py:16
  76.5 26.2 %collective-permute-start.4 = (f32[384,128]{1,0:T(8,128)S(1)}, f32[384,128]{1,0:T(8,128)S(1)}, u32[]{:S(2)}, u32[]{:S(2)}) collective-permute-start(f32[384,128]{1,0:T(8,128)S(1)} %get-tuple-element.20), channel_id=1, source_target_pairs={{1,0},{2,1},{3,2},{4,3},{5,4},{6,5},{7,6},{8,7},{9,8},{10,9},{11,1... | collective-permute-start | bytes 589832 | tf_op jit(solution)/shard_map/ppermute | solution.py:16
  105.3 3.6 %copy-start.1 = (f32[2048,256]{1,0:T(8,128)}, f32[2048,256]{1,0:T(8,128)S(1)}, u32[]{:S(2)}) copy-start(f32[2048,256]{1,0:T(8,128)S(1)} %get-tuple-element.9) | copy-start | bytes 6291460
  105.3 3.6 %copy-start.3 = (f32[2048,256]{1,0:T(8,128)}, f32[2048,256]{1,0:T(8,128)S(1)}, u32[]{:S(2)}) copy-start(f32[2048,256]{1,0:T(8,128)S(1)} %get-tuple-element.10) | copy-start | bytes 6291460
  109.3 79.6 %copy-start.2 = (f32[2048,256]{1,0:T(8,128)S(1)}, f32[2048,256]{1,0:T(8,128)}, u32[]{:S(2)}) copy-start(f32[2048,256]{1,0:T(8,128)} %copy-done.1) | copy-start | bytes 6291460

commit v13 on v12

--- a/solution.py
+++ b/solution.py
@@ -118,9 +118,10 @@
             pivot = jnp.sum(jnp.where(lane == k, row[:, here - low:here - low + lanes], 0.0), axis=1, keepdims=True)
             scale = lax.rsqrt(pivot)
             pivot_row = row * scale
-            column = jnp.sum(jnp.where(lane == k, work[top:, here:here + lanes], 0.0), axis=1, keepdims=True)
+            part = work[top:, low:high]
+            column = jnp.sum(jnp.where(lane == k, part[:, here - low:here - low + lanes], 0.0), axis=1, keepdims=True)
             column = jnp.where(row_id > k, column * scale, 0.0)
-            work[top:, low:high] = work[top:, low:high] - column * pivot_row
+            work[top:, low:high] = part - column * pivot_row
             work[pl.ds(k, 1), low:high] = pivot_row
             return carry
 

time: 196 us -> 196 us (level)
  no operation moved by 1% of the time
where the time goes in v13:
time: 196 us; the launch traced here: 195 us
  Pallas kernels  119 us (61%)
  starting transfers between devices  24.6 us (13%)
  matrix products  23.1 us (12%)
  waiting for transfers between devices  19.6 us (10%)
  other arithmetic  5.93 us (3%)
  local copies, waits for them, and re-layouts  2.7 us (1%)
    pallas_call x2, Pallas kernels, allreduce_rows(): pl.pallas_call(functools.partial(allreduce_kernel, n, chunk), out_shape=j...  65 us
    pallas_call x2, Pallas kernels, lower_inverse(): pl.pallas_call(inverse_kernel, out_shape=jax.ShapeDtypeStruct((size, size...  54.1 us
    ppermute x4, starting transfers between devices, from_behind(): lax.ppermute(value, axis, [(source, source + steps) for source in range(l...  23 us
    ppermute x4, waiting for transfers between devices, from_behind(): lax.ppermute(value, axis, [(source, source + steps) for source in range(l...  19.6 us
    dot_general x4, matrix products, gram_of(): lax.dot_general(left, right, (((0,), (0,)), ((), ())), precision=lax.Prec...  12.5 us
    dot_general x5, matrix products, mm(): return jnp.dot(left, right, precision=lax.Precision.HIGHEST)  10.7 us
  transfers between devices with their start and end apart: 5, of which 1 were waited for; matrix products, arithmetic and copies ran while one was open for 3% of the time, Pallas kernels for 14%

profile of v13, /device:TPU:57, one launch (start us, length us, event | category | flops | bytes accessed | tf_op | source)
XLA Modules:
  0.0 195.3 jit_solution(15472421923554056647)
XLA Ops:
  0.0 6.5 %fusion.25.g_ref = f32[256,256]{1,0:T(8,128)} fusion(f32[2048,256]{1,0:T(8,128)} %param.1), kind=kOutput, calls=%fused_computation.32 | convolution fusion | flops 1610612736 | bytes 2359296 | tf_op jit(solution)/shard_map/dot_general | solution.py:20
  6.5 17.9 %shard_map.17 = f32[256,256]{1,0:T(8,128)} custom-call(f32[256,256]{1,0:T(8,128)} %fusion.25.g_ref), custom_call_target="tpu_custom_call" | custom-call | tf_op jit(solution)/shard_map/pallas_call | solution.py:87
  24.4 1.7 broadcast_multiply_fusion.a_ref
  26.1 12.4 %collective-permute-start.2 = (f32[2048,256]{1,0:T(8,128)S(1)}, f32[2048,256]{1,0:T(8,128)}, u32[]{:S(2)}, u32[]{:S(2)}) collective-permute-start(f32[2048,256]{1,0:T(8,128)S(1)} %copy-done), channel_id=1, source_target_pairs={{1,0},{2,1},{3,2},{4,3},{5,4},{6,5},{7,6},{8,7},{9,8},{10,9},{11,1... | collective-permute-start | bytes 6291464 | tf_op jit(solution)/shard_map/ppermute | solution.py:16
  38.5 1.5 fusion.22
  40.0 1.6 collective-permute-start.1
  41.6 2.1 %collective-permute-start = (f32[2048,128]{1,0:T(8,128)}, f32[2048,128]{1,0:T(8,128)}, u32[]{:S(2)}, u32[]{:S(2)}) collective-permute-start(f32[2048,128]{1,0:T(8,128)} %get-tuple-element.11), channel_id=1, source_target_pairs={{0,1},{1,2},{2,3},{3,4},{4,5},{5,6},{6,7},{7,8},{8,9},{9,10},{10,1... | collective-permute-start | bytes 3145736 | tf_op jit(solution)/shard_map/ppermute | solution.py:16
  43.7 27.0 %shard_map.18 = f32[256,256]{1,0:T(8,128)} custom-call(f32[256,256]{1,0:T(8,128)} %broadcast_multiply_fusion.a_ref), custom_call_target="tpu_custom_call" | custom-call | tf_op jit(solution)/shard_map/pallas_call | solution.py:164
  70.6 1.4 fusion.26
  72.0 1.3 fusion.27
  73.3 1.1 copy.2
  74.5 1.9 collective-permute-start.3
  76.5 6.6 %collective-permute-start.4 = (f32[384,128]{1,0:T(8,128)S(1)}, f32[384,128]{1,0:T(8,128)S(1)}, u32[]{:S(2)}, u32[]{:S(2)}) collective-permute-start(f32[384,128]{1,0:T(8,128)S(1)} %get-tuple-element.20), channel_id=1, source_target_pairs={{1,0},{2,1},{3,2},{4,3},{5,4},{6,5},{7,6},{8,7},{9,8},{10,9},{11,1... | collective-permute-start | bytes 589832 | tf_op jit(solution)/shard_map/ppermute | solution.py:16
  83.1 19.6 %collective-permute-done.3 = f32[384,128]{1,0:T(8,128)S(1)} collective-permute-done((f32[384,128]{1,0:T(8,128)S(1)}, f32[384,128]{1,0:T(8,128)S(1)}, u32[]{:S(2)}, u32[]{:S(2)}) %collective-permute-start.3) | collective-permute-done | bytes 196640 | tf_op jit(solution)/shard_map/ppermute | solution.py:16
  102.7 2.6 %maximum_select_fusion = (f32[2048,256]{1,0:T(8,128)S(1)}, f32[2048,256]{1,0:T(8,128)S(1)}) fusion(f32[2048,256]{1,0:T(8,128)S(1)} %copy-done, f32[2048,128]{1,0:T(8,128)} %collective-permute-done.1, f32[2048,128]{1,0:T(8,128)} %collective-permute-done, pred[]{:T(512)S(6)} %eq.6, f32[2048,256]{1,0:T(8,128)} %collective-permute-done.2, pred[]{:T(512)S(6)} %eq.7), kind=kLoop, calls=%fused_computation.4 | loop fusion | flops 1572864 | bytes 10485762 | tf_op jit(solution)/shard_map/jit(_where)/select_n | solution.py:199
  105.3 3.6 %fusion.28 = f32[256,256]{1,0:T(8,128)S(1)} fusion(f32[2048,256]{1,0:T(8,128)S(1)} %get-tuple-element.9, f32[2048,256]{1,0:T(8,128)S(1)} %get-tuple-element.10), kind=kOutput, calls=%fused_computation.35 | convolution fusion | flops 1610612736 | bytes 4456448 | tf_op jit(solution)/shard_map/dot_general | solution.py:20
  109.3 1.0 fusion.18.g_ref
  110.3 47.1 %shard_map.19 = f32[128,128]{1,0:T(8,128)} custom-call(f32[128,128]{1,0:T(8,128)} %fusion.18.g_ref), custom_call_target="tpu_custom_call" | custom-call | tf_op jit(solution)/shard_map/pallas_call | solution.py:87
  157.5 0.9 broadcast_multiply_fusion.1
  158.4 0.7 maximum_maximum_fusion.a_ref
  159.2 27.2 %shard_map.20 = f32[256,256]{1,0:T(8,128)} custom-call(f32[256,256]{1,0:T(8,128)} %maximum_maximum_fusion.a_ref), custom_call_target="tpu_custom_call" | custom-call | tf_op jit(solution)/shard_map/pallas_call | solution.py:164
  186.4 1.3 fusion.7
  187.6 1.3 fusion.9
  188.9 6.4 %fusion = f32[2048,256]{1,0:T(8,128)} fusion(f32[2048,256]{1,0:T(8,128)} %copy-done.3, f32[2048,256]{1,0:T(8,128)S(1)} %copy-done.2, f32[256,256]{1,0:T(8,128)S(1)} %fusion.7, f32[256,256]{1,0:T(8,128)S(1)} %fusion.9), kind=kOutput, calls=%fused_computation | convolution fusion | flops 3222405120 | bytes 6815744 | tf_op jit(solution)/shard_map/dot_general | solution.py:178
  (22 shorter events, 0.6 us)
Async XLA Ops:
  0.0 26.1 %copy-start = (f32[2048,256]{1,0:T(8,128)S(1)}, f32[2048,256]{1,0:T(8,128)}, u32[]{:S(2)}) copy-start(f32[2048,256]{1,0:T(8,128)} %param.1) | copy-start | bytes 6291460
  26.1 44.5 %copy-start.4 = (f32[256,256]{1,0:T(8,128)S(1)}, f32[256,256]{1,0:T(8,128)}, u32[]{:S(2)}) copy-start(f32[256,256]{1,0:T(8,128)} %broadcast_multiply_fusion.a_ref) | copy-start | bytes 786436
  26.1 76.6 %collective-permute-start.2 = (f32[2048,256]{1,0:T(8,128)S(1)}, f32[2048,256]{1,0:T(8,128)}, u32[]{:S(2)}, u32[]{:S(2)}) collective-permute-start(f32[2048,256]{1,0:T(8,128)S(1)} %copy-done), channel_id=1, source_target_pairs={{1,0},{2,1},{3,2},{4,3},{5,4},{6,5},{7,6},{8,7},{9,8},{10,9},{11,1... | collective-permute-start | bytes 6291464 | tf_op jit(solution)/shard_map/ppermute | solution.py:16
  40.0 62.7 %collective-permute-start.1 = (f32[2048,128]{1,0:T(8,128)}, f32[2048,128]{1,0:T(8,128)}, u32[]{:S(2)}, u32[]{:S(2)}) collective-permute-start(f32[2048,128]{1,0:T(8,128)} %get-tuple-element.12), channel_id=1, source_target_pairs={{0,1},{32,33},{64,65},{96,97},{128,129},{160,161},{192,193},{224,2... | collective-permute-start | bytes 3145736 | tf_op jit(solution)/shard_map/ppermute | solution.py:198
  41.6 61.1 %collective-permute-start = (f32[2048,128]{1,0:T(8,128)}, f32[2048,128]{1,0:T(8,128)}, u32[]{:S(2)}, u32[]{:S(2)}) collective-permute-start(f32[2048,128]{1,0:T(8,128)} %get-tuple-element.11), channel_id=1, source_target_pairs={{0,1},{1,2},{2,3},{3,4},{4,5},{5,6},{6,7},{7,8},{8,9},{9,10},{10,1... | collective-permute-start | bytes 3145736 | tf_op jit(solution)/shard_map/ppermute | solution.py:16
  74.5 28.1 %collective-permute-start.3 = (f32[384,128]{1,0:T(8,128)S(1)}, f32[384,128]{1,0:T(8,128)S(1)}, u32[]{:S(2)}, u32[]{:S(2)}) collective-permute-start(f32[384,128]{1,0:T(8,128)S(1)} %get-tuple-element.19), channel_id=1, source_target_pairs={{0,1},{1,2},{2,3},{3,4},{4,5},{5,6},{6,7},{7,8},{8,9},{9,10},{10,1... | collective-permute-start | bytes 589832 | tf_op jit(solution)/shard_map/ppermute | solution.py:16
  76.5 26.2 %collective-permute-start.4 = (f32[384,128]{1,0:T(8,128)S(1)}, f32[384,128]{1,0:T(8,128)S(1)}, u32[]{:S(2)}, u32[]{:S(2)}) collective-permute-start(f32[384,128]{1,0:T(8,128)S(1)} %get-tuple-element.20), channel_id=1, source_target_pairs={{1,0},{2,1},{3,2},{4,3},{5,4},{6,5},{7,6},{8,7},{9,8},{10,9},{11,1... | collective-permute-start | bytes 589832 | tf_op jit(solution)/shard_map/ppermute | solution.py:16
  105.3 3.6 %copy-start.1 = (f32[2048,256]{1,0:T(8,128)}, f32[2048,256]{1,0:T(8,128)S(1)}, u32[]{:S(2)}) copy-start(f32[2048,256]{1,0:T(8,128)S(1)} %get-tuple-element.9) | copy-start | bytes 6291460
  105.3 3.6 %copy-start.3 = (f32[2048,256]{1,0:T(8,128)}, f32[2048,256]{1,0:T(8,128)S(1)}, u32[]{:S(2)}) copy-start(f32[2048,256]{1,0:T(8,128)S(1)} %get-tuple-element.10) | copy-start | bytes 6291460
  109.3 79.6 %copy-start.2 = (f32[2048,256]{1,0:T(8,128)S(1)}, f32[2048,256]{1,0:T(8,128)}, u32[]{:S(2)}) copy-start(f32[2048,256]{1,0:T(8,128)} %copy-done.1) | copy-start | bytes 6291460

commit v14 on v12

--- a/solution.py
+++ b/solution.py
@@ -191,7 +191,13 @@
     last = index == count - 1
     pair = snapshots
 
-    gram = allreduce_rows(gram_of(pair, pair)) / total
+    lead, rest = pair[:, :width], pair[:, width:]
+    below = gram_of(rest, lead)
+    local = jnp.concatenate(
+        [jnp.concatenate([gram_of(lead, lead), below.T], axis=1), jnp.concatenate([below, gram_of(rest, rest)], axis=1)],
+        axis=0,
+    )
+    gram = allreduce_rows(local) / total
     sent, gram = lax.optimization_barrier((pair, gram))
     left = from_behind(sent[:, :width], "pairs", 1)
     right = lax.ppermute(sent[:, width:], "pairs", [(0, 1)])

time: 196 us -> 199 us (1.015)
  matrix products: 23.1 us -> 25.3 us
    dot_general x4 -> x6, matrix products: 12.5 us -> 14.6 us  [gram_of(): lax.dot_general(left, right, (((0,), (0,)), ((), ())), precision=lax.Prec...]
where the time goes in v14:
time: 199 us; the launch traced here: 198 us
  Pallas kernels  119 us (60%)
  matrix products  25.3 us (13%)
  starting transfers between devices  24.6 us (12%)
  waiting for transfers between devices  19.6 us (10%)
  other arithmetic  6.66 us (3%)
  local copies, waits for them, and re-layouts  2.79 us (1%)
    pallas_call x2, Pallas kernels, allreduce_rows(): pl.pallas_call(functools.partial(allreduce_kernel, n, chunk), out_shape=j...  65 us
    pallas_call x2, Pallas kernels, lower_inverse(): pl.pallas_call(inverse_kernel, out_shape=jax.ShapeDtypeStruct((size, size...  54.1 us
    ppermute x4, starting transfers between devices, from_behind(): lax.ppermute(value, axis, [(source, source + steps) for source in range(l...  23 us
    ppermute x4, waiting for transfers between devices, from_behind(): lax.ppermute(value, axis, [(source, source + steps) for source in range(l...  19.6 us
    dot_general x6, matrix products, gram_of(): lax.dot_general(left, right, (((0,), (0,)), ((), ())), precision=lax.Prec...  14.6 us
    dot_general x5, matrix products, mm(): return jnp.dot(left, right, precision=lax.Precision.HIGHEST)  10.7 us
  transfers between devices with their start and end apart: 5, of which 1 were waited for; matrix products, arithmetic and copies ran while one was open for 3% of the time, Pallas kernels for 14%

profile of v14, /device:TPU:57, one launch (start us, length us, event | category | flops | bytes accessed | tf_op | source)
XLA Modules:
  0.0 198.3 jit_solution(15145161426641396357)
XLA Ops:
  0.0 3.5 %fusion.4 = f32[128,128]{1,0:T(8,128)S(1)} fusion(f32[2048,256]{1,0:T(8,128)} %param.1), kind=kOutput, calls=%fused_computation.6 | convolution fusion | flops 402653184 | bytes 1114112 | tf_op jit(solution)/shard_map/dot_general | solution.py:20
  3.5 3.4 %fusion.6 = f32[128,128]{1,0:T(8,128)S(1)} fusion(f32[2048,256]{1,0:T(8,128)} %param.1), kind=kOutput, calls=%fused_computation.8 | convolution fusion | flops 402653184 | bytes 2162688 | tf_op jit(solution)/shard_map/dot_general | solution.py:20
  6.9 1.8 fusion.9
  9.5 17.9 %shard_map.17 = f32[256,256]{1,0:T(8,128)} custom-call(f32[256,256]{1,0:T(8,128)} %maximum_maximum_fusion.g_ref), custom_call_target="tpu_custom_call" | custom-call | tf_op jit(solution)/shard_map/pallas_call | solution.py:87
  27.4 1.7 broadcast_multiply_fusion.a_ref
  29.1 12.4 %collective-permute-start.2 = (f32[2048,256]{1,0:T(8,128)S(1)}, f32[2048,256]{1,0:T(8,128)}, u32[]{:S(2)}, u32[]{:S(2)}) collective-permute-start(f32[2048,256]{1,0:T(8,128)S(1)} %copy-done), channel_id=1, source_target_pairs={{1,0},{2,1},{3,2},{4,3},{5,4},{6,5},{7,6},{8,7},{9,8},{10,9},{11,1... | collective-permute-start | bytes 6291464 | tf_op jit(solution)/shard_map/ppermute | solution.py:16
  41.5 1.5 fusion.29
  42.9 1.6 collective-permute-start.1
  44.6 2.1 %collective-permute-start = (f32[2048,128]{1,0:T(8,128)}, f32[2048,128]{1,0:T(8,128)}, u32[]{:S(2)}, u32[]{:S(2)}) collective-permute-start(f32[2048,128]{1,0:T(8,128)} %get-tuple-element.11), channel_id=1, source_target_pairs={{0,1},{1,2},{2,3},{3,4},{4,5},{5,6},{6,7},{7,8},{8,9},{9,10},{10,1... | collective-permute-start | bytes 3145736 | tf_op jit(solution)/shard_map/ppermute | solution.py:16
  46.7 27.0 %shard_map.18 = f32[256,256]{1,0:T(8,128)} custom-call(f32[256,256]{1,0:T(8,128)} %broadcast_multiply_fusion.a_ref), custom_call_target="tpu_custom_call" | custom-call | tf_op jit(solution)/shard_map/pallas_call | solution.py:163
  73.6 1.4 fusion.32
  75.0 1.3 fusion.33
  76.3 1.1 copy.5
  77.5 1.9 collective-permute-start.3
  79.4 6.6 %collective-permute-start.4 = (f32[384,128]{1,0:T(8,128)S(1)}, f32[384,128]{1,0:T(8,128)S(1)}, u32[]{:S(2)}, u32[]{:S(2)}) collective-permute-start(f32[384,128]{1,0:T(8,128)S(1)} %get-tuple-element.20), channel_id=1, source_target_pairs={{1,0},{2,1},{3,2},{4,3},{5,4},{6,5},{7,6},{8,7},{9,8},{10,9},{11,1... | collective-permute-start | bytes 589832 | tf_op jit(solution)/shard_map/ppermute | solution.py:16
  86.0 19.6 %collective-permute-done.3 = f32[384,128]{1,0:T(8,128)S(1)} collective-permute-done((f32[384,128]{1,0:T(8,128)S(1)}, f32[384,128]{1,0:T(8,128)S(1)}, u32[]{:S(2)}, u32[]{:S(2)}) %collective-permute-start.3) | collective-permute-done | bytes 196640 | tf_op jit(solution)/shard_map/ppermute | solution.py:16
  105.7 2.6 %maximum_select_fusion = (f32[2048,256]{1,0:T(8,128)S(1)}, f32[2048,256]{1,0:T(8,128)S(1)}) fusion(f32[2048,256]{1,0:T(8,128)S(1)} %copy-done, f32[2048,128]{1,0:T(8,128)} %collective-permute-done.1, f32[2048,128]{1,0:T(8,128)} %collective-permute-done, pred[]{:T(512)S(6)} %eq.6, f32[2048,256]{1,0:T(8,128)} %collective-permute-done.2, pred[]{:T(512)S(6)} %eq.7), kind=kLoop, calls=%fused_computation.4 | loop fusion | flops 1572864 | bytes 10485762 | tf_op jit(solution)/shard_map/jit(_where)/select_n | solution.py:204
  108.3 3.6 %fusion.34 = f32[256,256]{1,0:T(8,128)S(1)} fusion(f32[2048,256]{1,0:T(8,128)S(1)} %get-tuple-element.9, f32[2048,256]{1,0:T(8,128)S(1)} %get-tuple-element.10), kind=kOutput, calls=%fused_computation.42 | convolution fusion | flops 1610612736 | bytes 4456448 | tf_op jit(solution)/shard_map/dot_general | solution.py:20
  112.3 1.0 fusion.25.g_ref
  113.3 47.1 %shard_map.19 = f32[128,128]{1,0:T(8,128)} custom-call(f32[128,128]{1,0:T(8,128)} %fusion.25.g_ref), custom_call_target="tpu_custom_call" | custom-call | tf_op jit(solution)/shard_map/pallas_call | solution.py:87
  162.2 27.2 %shard_map.20 = f32[256,256]{1,0:T(8,128)} custom-call(f32[256,256]{1,0:T(8,128)} %maximum_maximum_fusion.1.a_ref), custom_call_target="tpu_custom_call" | custom-call | tf_op jit(solution)/shard_map/pallas_call | solution.py:163
  189.3 1.3 fusion.14
  190.6 1.3 fusion.16
  191.9 6.4 %fusion = f32[2048,256]{1,0:T(8,128)} fusion(f32[2048,256]{1,0:T(8,128)} %copy-done.3, f32[2048,256]{1,0:T(8,128)S(1)} %copy-done.2, f32[256,256]{1,0:T(8,128)S(1)} %fusion.14, f32[256,256]{1,0:T(8,128)S(1)} %fusion.16), kind=kOutput, calls=%fused_computation | convolution fusion | flops 3222405120 | bytes 6815744 | tf_op jit(solution)/shard_map/dot_general | solution.py:177
  (26 shorter events, 3.0 us)
Async XLA Ops:
  0.0 6.9 %copy-start = (f32[2048,256]{1,0:T(8,128)S(1)}, f32[2048,256]{1,0:T(8,128)}, u32[]{:S(2)}) copy-start(f32[2048,256]{1,0:T(8,128)} %param.1) | copy-start | bytes 6291460
  29.1 44.5 %copy-start.4 = (f32[256,256]{1,0:T(8,128)S(1)}, f32[256,256]{1,0:T(8,128)}, u32[]{:S(2)}) copy-start(f32[256,256]{1,0:T(8,128)} %broadcast_multiply_fusion.a_ref) | copy-start | bytes 786436
  29.1 76.6 %collective-permute-start.2 = (f32[2048,256]{1,0:T(8,128)S(1)}, f32[2048,256]{1,0:T(8,128)}, u32[]{:S(2)}, u32[]{:S(2)}) collective-permute-start(f32[2048,256]{1,0:T(8,128)S(1)} %copy-done), channel_id=1, source_target_pairs={{1,0},{2,1},{3,2},{4,3},{5,4},{6,5},{7,6},{8,7},{9,8},{10,9},{11,1... | collective-permute-start | bytes 6291464 | tf_op jit(solution)/shard_map/ppermute | solution.py:16
  42.9 62.7 %collective-permute-start.1 = (f32[2048,128]{1,0:T(8,128)}, f32[2048,128]{1,0:T(8,128)}, u32[]{:S(2)}, u32[]{:S(2)}) collective-permute-start(f32[2048,128]{1,0:T(8,128)} %get-tuple-element.12), channel_id=1, source_target_pairs={{0,1},{32,33},{64,65},{96,97},{128,129},{160,161},{192,193},{224,2... | collective-permute-start | bytes 3145736 | tf_op jit(solution)/shard_map/ppermute | solution.py:203
  44.6 61.1 %collective-permute-start = (f32[2048,128]{1,0:T(8,128)}, f32[2048,128]{1,0:T(8,128)}, u32[]{:S(2)}, u32[]{:S(2)}) collective-permute-start(f32[2048,128]{1,0:T(8,128)} %get-tuple-element.11), channel_id=1, source_target_pairs={{0,1},{1,2},{2,3},{3,4},{4,5},{5,6},{6,7},{7,8},{8,9},{9,10},{10,1... | collective-permute-start | bytes 3145736 | tf_op jit(solution)/shard_map/ppermute | solution.py:16
  77.5 28.1 %collective-permute-start.3 = (f32[384,128]{1,0:T(8,128)S(1)}, f32[384,128]{1,0:T(8,128)S(1)}, u32[]{:S(2)}, u32[]{:S(2)}) collective-permute-start(f32[384,128]{1,0:T(8,128)S(1)} %get-tuple-element.19), channel_id=1, source_target_pairs={{0,1},{1,2},{2,3},{3,4},{4,5},{5,6},{6,7},{7,8},{8,9},{9,10},{10,1... | collective-permute-start | bytes 589832 | tf_op jit(solution)/shard_map/ppermute | solution.py:16
  79.4 26.2 %collective-permute-start.4 = (f32[384,128]{1,0:T(8,128)S(1)}, f32[384,128]{1,0:T(8,128)S(1)}, u32[]{:S(2)}, u32[]{:S(2)}) collective-permute-start(f32[384,128]{1,0:T(8,128)S(1)} %get-tuple-element.20), channel_id=1, source_target_pairs={{1,0},{2,1},{3,2},{4,3},{5,4},{6,5},{7,6},{8,7},{9,8},{10,9},{11,1... | collective-permute-start | bytes 589832 | tf_op jit(solution)/shard_map/ppermute | solution.py:16
  108.3 3.6 %copy-start.1 = (f32[2048,256]{1,0:T(8,128)}, f32[2048,256]{1,0:T(8,128)S(1)}, u32[]{:S(2)}) copy-start(f32[2048,256]{1,0:T(8,128)S(1)} %get-tuple-element.9) | copy-start | bytes 6291460
  108.3 3.6 %copy-start.3 = (f32[2048,256]{1,0:T(8,128)}, f32[2048,256]{1,0:T(8,128)S(1)}, u32[]{:S(2)}) copy-start(f32[2048,256]{1,0:T(8,128)S(1)} %get-tuple-element.10) | copy-start | bytes 6291460
  112.3 79.6 %copy-start.2 = (f32[2048,256]{1,0:T(8,128)S(1)}, f32[2048,256]{1,0:T(8,128)}, u32[]{:S(2)}) copy-start(f32[2048,256]{1,0:T(8,128)} %copy-done.1) | copy-start | bytes 6291460

commit v15 on v12

--- a/solution.py
+++ b/solution.py
@@ -200,9 +200,11 @@
 
 
     whiten = whitener(gram)
-    moment = tmm(whiten, mm(gram, whiten))
-    top = jnp.concatenate([whiten[:, :width], moment[:width, :width]], axis=0)
-    bottom = jnp.concatenate([whiten[:, width:], moment[width:, width:]], axis=0)
+    head_w, tail_w = whiten[:width, :width], whiten[:, width:]
+    moment_top = tmm(head_w, mm(gram[:width, :width], head_w))
+    moment_bottom = tmm(tail_w, mm(gram, tail_w))
+    top = jnp.concatenate([whiten[:, :width], moment_top], axis=0)
+    bottom = jnp.concatenate([whiten[:, width:], moment_bottom], axis=0)
     outgoing = jnp.where(first, bottom, top)
     arrived_a = from_behind(outgoing, "pairs", 1)
     arrived_b = from_behind(bottom, "pairs", -1)

time: 196 us -> 196 us (level)
    dot_general x5 -> x6, matrix products: 10.7 us -> 9.9 us  [mm(): return jnp.dot(left, right, precision=lax.Precision.HIGHEST)]
    dot_general x4 -> x5, matrix products: 12.5 us -> 11.8 us  [gram_of(): lax.dot_general(left, right, (((0,), (0,)), ((), ())), precision=lax.Prec...]
  transfers between devices with their start and end apart: 5 -> 5, of which waited for: 1 -> 1; matrix products, arithmetic and copies ran while one was open for 3% -> 2% of each run, Pallas kernels for 14% -> 14%
where the time goes in v15:
time: 196 us; the launch traced here: 195 us
  Pallas kernels  119 us (61%)
  starting transfers between devices  24.6 us (13%)
  matrix products  21.7 us (11%)
  waiting for transfers between devices  21 us (11%)
  other arithmetic  5.91 us (3%)
  local copies, waits for them, and re-layouts  2.67 us (1%)
    pallas_call x2, Pallas kernels, allreduce_rows(): pl.pallas_call(functools.partial(allreduce_kernel, n, chunk), out_shape=j...  65 us
    pallas_call x2, Pallas kernels, lower_inverse(): pl.pallas_call(inverse_kernel, out_shape=jax.ShapeDtypeStruct((size, size...  54.1 us
    ppermute x4, starting transfers between devices, from_behind(): lax.ppermute(value, axis, [(source, source + steps) for source in range(l...  23 us
    ppermute x4, waiting for transfers between devices, from_behind(): lax.ppermute(value, axis, [(source, source + steps) for source in range(l...  21 us
    dot_general x5, matrix products, gram_of(): lax.dot_general(left, right, (((0,), (0,)), ((), ())), precision=lax.Prec...  11.8 us
    dot_general x6, matrix products, mm(): return jnp.dot(left, right, precision=lax.Precision.HIGHEST)  9.9 us
  transfers between devices with their start and end apart: 5, of which 1 were waited for; matrix products, arithmetic and copies ran while one was open for 2% of the time, Pallas kernels for 14%

profile of v15, /device:TPU:57, one launch (start us, length us, event | category | flops | bytes accessed | tf_op | source)
XLA Modules:
  0.0 195.3 jit_solution(394412920888057309)
XLA Ops:
  0.0 6.5 %fusion.33.g_ref = f32[256,256]{1,0:T(8,128)} fusion(f32[2048,256]{1,0:T(8,128)} %param.1), kind=kOutput, calls=%fused_computation.40 | convolution fusion | flops 1610612736 | bytes 2359296 | tf_op jit(solution)/shard_map/dot_general | solution.py:20
  6.5 17.9 %shard_map.17 = f32[256,256]{1,0:T(8,128)} custom-call(f32[256,256]{1,0:T(8,128)} %fusion.33.g_ref), custom_call_target="tpu_custom_call" | custom-call | tf_op jit(solution)/shard_map/pallas_call | solution.py:87
  24.4 1.7 broadcast_multiply_fusion.a_ref
  26.1 12.4 %collective-permute-start.2 = (f32[2048,256]{1,0:T(8,128)S(1)}, f32[2048,256]{1,0:T(8,128)}, u32[]{:S(2)}, u32[]{:S(2)}) collective-permute-start(f32[2048,256]{1,0:T(8,128)S(1)} %copy-done), channel_id=1, source_target_pairs={{1,0},{2,1},{3,2},{4,3},{5,4},{6,5},{7,6},{8,7},{9,8},{10,9},{11,1... | collective-permute-start | bytes 6291464 | tf_op jit(solution)/shard_map/ppermute | solution.py:16
  38.5 1.5 fusion.31
  39.9 1.6 collective-permute-start.1
  41.6 2.1 %collective-permute-start = (f32[2048,128]{1,0:T(8,128)}, f32[2048,128]{1,0:T(8,128)}, u32[]{:S(2)}, u32[]{:S(2)}) collective-permute-start(f32[2048,128]{1,0:T(8,128)} %get-tuple-element.11), channel_id=1, source_target_pairs={{0,1},{1,2},{2,3},{3,4},{4,5},{5,6},{6,7},{7,8},{8,9},{9,10},{10,1... | collective-permute-start | bytes 3145736 | tf_op jit(solution)/shard_map/ppermute | solution.py:16
  43.7 26.9 %shard_map.18 = f32[256,256]{1,0:T(8,128)} custom-call(f32[256,256]{1,0:T(8,128)} %broadcast_multiply_fusion.a_ref), custom_call_target="tpu_custom_call" | custom-call | tf_op jit(solution)/shard_map/pallas_call | solution.py:163
  70.6 1.1 copy.2
  71.9 0.4 fusion.29
  72.6 0.4 fusion.27
  73.1 1.9 collective-permute-start.3
  75.0 6.6 %collective-permute-start.4 = (f32[384,128]{1,0:T(8,128)S(1)}, f32[384,128]{1,0:T(8,128)S(1)}, u32[]{:S(2)}, u32[]{:S(2)}) collective-permute-start(f32[384,128]{1,0:T(8,128)S(1)} %get-tuple-element.18), channel_id=1, source_target_pairs={{1,0},{2,1},{3,2},{4,3},{5,4},{6,5},{7,6},{8,7},{9,8},{10,9},{11,1... | collective-permute-start | bytes 589832 | tf_op jit(solution)/shard_map/ppermute | solution.py:16
  81.6 21.0 %collective-permute-done.3 = f32[384,128]{1,0:T(8,128)S(1)} collective-permute-done((f32[384,128]{1,0:T(8,128)S(1)}, f32[384,128]{1,0:T(8,128)S(1)}, u32[]{:S(2)}, u32[]{:S(2)}) %collective-permute-start.3) | collective-permute-done | bytes 196640 | tf_op jit(solution)/shard_map/ppermute | solution.py:16
  102.7 2.6 %maximum_select_fusion = (f32[2048,256]{1,0:T(8,128)S(1)}, f32[2048,256]{1,0:T(8,128)S(1)}) fusion(f32[2048,256]{1,0:T(8,128)S(1)} %copy-done, f32[2048,128]{1,0:T(8,128)} %collective-permute-done.1, f32[2048,128]{1,0:T(8,128)} %collective-permute-done, pred[]{:T(512)S(6)} %eq.6, f32[2048,256]{1,0:T(8,128)} %collective-permute-done.2, pred[]{:T(512)S(6)} %eq.7), kind=kLoop, calls=%fused_computation.4 | loop fusion | flops 1572864 | bytes 10485762 | tf_op jit(solution)/shard_map/jit(_where)/select_n | solution.py:198
  105.3 3.6 %fusion.34 = f32[256,256]{1,0:T(8,128)S(1)} fusion(f32[2048,256]{1,0:T(8,128)S(1)} %get-tuple-element.9, f32[2048,256]{1,0:T(8,128)S(1)} %get-tuple-element.10), kind=kOutput, calls=%fused_computation.41 | convolution fusion | flops 1610612736 | bytes 4456448 | tf_op jit(solution)/shard_map/dot_general | solution.py:20
  109.3 1.0 fusion.18.g_ref
  110.3 47.1 %shard_map.19 = f32[128,128]{1,0:T(8,128)} custom-call(f32[128,128]{1,0:T(8,128)} %fusion.18.g_ref), custom_call_target="tpu_custom_call" | custom-call | tf_op jit(solution)/shard_map/pallas_call | solution.py:87
  157.5 0.9 broadcast_multiply_fusion.1
  158.4 0.7 maximum_maximum_fusion.a_ref
  159.1 27.2 %shard_map.20 = f32[256,256]{1,0:T(8,128)} custom-call(f32[256,256]{1,0:T(8,128)} %maximum_maximum_fusion.a_ref), custom_call_target="tpu_custom_call" | custom-call | tf_op jit(solution)/shard_map/pallas_call | solution.py:163
  186.3 1.3 fusion.7
  187.6 1.3 fusion.9
  188.9 6.4 %fusion = f32[2048,256]{1,0:T(8,128)} fusion(f32[2048,256]{1,0:T(8,128)} %copy-done.3, f32[2048,256]{1,0:T(8,128)S(1)} %copy-done.2, f32[256,256]{1,0:T(8,128)S(1)} %fusion.7, f32[256,256]{1,0:T(8,128)S(1)} %fusion.9), kind=kOutput, calls=%fused_computation | convolution fusion | flops 3222405120 | bytes 6815744 | tf_op jit(solution)/shard_map/dot_general | solution.py:177
  (23 shorter events, 1.1 us)
Async XLA Ops:
  0.0 26.1 %copy-start = (f32[2048,256]{1,0:T(8,128)S(1)}, f32[2048,256]{1,0:T(8,128)}, u32[]{:S(2)}) copy-start(f32[2048,256]{1,0:T(8,128)} %param.1) | copy-start | bytes 6291460
  26.1 45.6 %copy-start.4 = (f32[256,256]{1,0:T(8,128)S(1)}, f32[256,256]{1,0:T(8,128)}, u32[]{:S(2)}) copy-start(f32[256,256]{1,0:T(8,128)} %broadcast_multiply_fusion.a_ref) | copy-start | bytes 786436
  26.1 76.6 %collective-permute-start.2 = (f32[2048,256]{1,0:T(8,128)S(1)}, f32[2048,256]{1,0:T(8,128)}, u32[]{:S(2)}, u32[]{:S(2)}) collective-permute-start(f32[2048,256]{1,0:T(8,128)S(1)} %copy-done), channel_id=1, source_target_pairs={{1,0},{2,1},{3,2},{4,3},{5,4},{6,5},{7,6},{8,7},{9,8},{10,9},{11,1... | collective-permute-start | bytes 6291464 | tf_op jit(solution)/shard_map/ppermute | solution.py:16
  39.9 62.7 %collective-permute-start.1 = (f32[2048,128]{1,0:T(8,128)}, f32[2048,128]{1,0:T(8,128)}, u32[]{:S(2)}, u32[]{:S(2)}) collective-permute-start(f32[2048,128]{1,0:T(8,128)} %get-tuple-element.12), channel_id=1, source_target_pairs={{0,1},{32,33},{64,65},{96,97},{128,129},{160,161},{192,193},{224,2... | collective-permute-start | bytes 3145736 | tf_op jit(solution)/shard_map/ppermute | solution.py:197
  41.6 61.1 %collective-permute-start = (f32[2048,128]{1,0:T(8,128)}, f32[2048,128]{1,0:T(8,128)}, u32[]{:S(2)}, u32[]{:S(2)}) collective-permute-start(f32[2048,128]{1,0:T(8,128)} %get-tuple-element.11), channel_id=1, source_target_pairs={{0,1},{1,2},{2,3},{3,4},{4,5},{5,6},{6,7},{7,8},{8,9},{9,10},{10,1... | collective-permute-start | bytes 3145736 | tf_op jit(solution)/shard_map/ppermute | solution.py:16
  73.1 29.5 %collective-permute-start.3 = (f32[384,128]{1,0:T(8,128)S(1)}, f32[384,128]{1,0:T(8,128)S(1)}, u32[]{:S(2)}, u32[]{:S(2)}) collective-permute-start(f32[384,128]{1,0:T(8,128)S(1)} %get-tuple-element.17), channel_id=1, source_target_pairs={{0,1},{1,2},{2,3},{3,4},{4,5},{5,6},{6,7},{7,8},{8,9},{9,10},{10,1... | collective-permute-start | bytes 589832 | tf_op jit(solution)/shard_map/ppermute | solution.py:16
  75.0 27.6 %collective-permute-start.4 = (f32[384,128]{1,0:T(8,128)S(1)}, f32[384,128]{1,0:T(8,128)S(1)}, u32[]{:S(2)}, u32[]{:S(2)}) collective-permute-start(f32[384,128]{1,0:T(8,128)S(1)} %get-tuple-element.18), channel_id=1, source_target_pairs={{1,0},{2,1},{3,2},{4,3},{5,4},{6,5},{7,6},{8,7},{9,8},{10,9},{11,1... | collective-permute-start | bytes 589832 | tf_op jit(solution)/shard_map/ppermute | solution.py:16
  105.3 3.6 %copy-start.1 = (f32[2048,256]{1,0:T(8,128)}, f32[2048,256]{1,0:T(8,128)S(1)}, u32[]{:S(2)}) copy-start(f32[2048,256]{1,0:T(8,128)S(1)} %get-tuple-element.9) | copy-start | bytes 6291460
  105.3 3.6 %copy-start.3 = (f32[2048,256]{1,0:T(8,128)}, f32[2048,256]{1,0:T(8,128)S(1)}, u32[]{:S(2)}) copy-start(f32[2048,256]{1,0:T(8,128)S(1)} %get-tuple-element.10) | copy-start | bytes 6291460
  109.3 79.6 %copy-start.2 = (f32[2048,256]{1,0:T(8,128)S(1)}, f32[2048,256]{1,0:T(8,128)}, u32[]{:S(2)}) copy-start(f32[2048,256]{1,0:T(8,128)} %copy-done.1) | copy-start | bytes 6291460
